TPU v7x, 32 devices: a whole 2x2x4 slice. The times are simulated.
32 devices in a mesh: row: 16 (over z, y, core), col: 2 (over x).
Axes of the slice: x: 2, y: 2, z: 4, core: 2. Of those that a mesh axis runs over, the one named last changes fastest.
Arguments:
- layer_input: bfloat16 [16384, 1152], P(('row', 'col')), may hold values from -6 to 6
- attn_gain: bfloat16 [1152], replicated, may hold values from 0.099609375 to 1.8984375
- mlp_gain: bfloat16 [1152], replicated, may hold values from 0.099609375 to 1.8984375
- query_weight: bfloat16 [1152, 1152], P('row', 'col'), may hold values from -0.1875 to 0.1875
- key_weight: bfloat16 [1152, 384], P('row', 'col'), may hold values from -0.1875 to 0.1875
- value_weight: bfloat16 [1152, 384], P('row', 'col'), may hold values from -0.1875 to 0.1875
- out_weight: bfloat16 [1152, 1152], P('col', 'row'), may hold values from -4 to 4
- gate_weight: bfloat16 [1152, 3072], P('row', 'col'), may hold values from -0.1875 to 0.1875
- up_weight: bfloat16 [1152, 3072], P('row', 'col'), may hold values from -0.1875 to 0.1875
- down_weight: bfloat16 [3072, 1152], P('col', 'row'), may hold values from -0.109375 to 0.109375
- seq_ids: int32 [16384], P('row'), may hold values from 0 to 31, as said below
- block_ends: int32 [16384], P('row'), may hold values from 255 to 16383, as said below
- grad_output: bfloat16 [16384, 1152], P(('row', 'col')), may hold values from -6 to 6
Outputs:
- layer_output: bfloat16 [16384, 1152], P(('row', 'col'))
- grad_input: bfloat16 [16384, 1152], P(('row', 'col'))
- grad_attn_gain: float32 [1152], replicated
- grad_mlp_gain: float32 [1152], replicated
- grad_query: float32 [1152, 1152], P('row', 'col')
- grad_key: float32 [1152, 384], P('row', 'col')
- grad_value: float32 [1152, 384], P('row', 'col')
- grad_out_weight: float32 [1152, 1152], P('col', 'row')
- grad_gate: float32 [1152, 3072], P('row', 'col')
- grad_up: float32 [1152, 3072], P('row', 'col')
- grad_down: float32 [3072, 1152], P('col', 'row')
Inputs may be any that keep to these rules, and one draw needn't show every extreme that they name: `seq_ids`: ids never fall; span number s of the aligned spans of 1024 tokens holds exactly two sequences, with ids 2 * s and 2 * s + 1, each of 256 tokens or more. `block_ends`: values never fall; an attention block is a run of 1 to 256 tokens inside one sequence, and the first block of every sequence has exactly 256 tokens.
All inputs are finite; a program needn't handle non-finite values.
Results may differ from a plain program's by a relative error of at most 0.014.
The roundings to bfloat16 on the way count: a program that leaves them out, or rounds other values in their place, can miss the bound.
Values may be sent and summed in bfloat16 or wider, within the bound.
A program may use at most 192 MiB of HBM per device.

v0:
```python
import math

import jax
import jax.numpy as jnp
from jax import lax
from jax.sharding import PartitionSpec as P

QUERY_HEADS = 18
KEY_VALUE_HEADS = 6
HEAD_SIZE_DIM = 64


eps = 1e-05
rope_base = 10000.0
neg_fill = -1e30


def rotate_half(values, head_size):
    lane_index = jnp.arange(values.shape[-1], dtype=jnp.int32) % head_size
    forward_roll = jnp.roll(values, -(head_size // 2), axis=-1)
    backward_roll = jnp.roll(values, head_size // 2, axis=-1)
    return jnp.where(lane_index < head_size // 2, -forward_roll, backward_roll)


def rope_tables(position, table_width, head_size):
    lane_index = (jnp.arange(table_width, dtype=jnp.int32) % (head_size // 2)).astype(jnp.float32)
    frequency = jnp.exp(lane_index * (-2.0 * math.log(rope_base) / head_size))
    angles = position[:, None] * frequency[None, :]
    return (jnp.cos(angles), jnp.sin(angles))


def rotary(values, cosine, sine_part, head_size):
    return values * cosine + rotate_half(values, head_size) * sine_part


def rotary_back(upstream, cosine, sine_part, head_size):
    return upstream * cosine - rotate_half(upstream * sine_part, head_size)


def positions(seq_ids):
    token_index = jnp.arange(seq_ids.shape[0], dtype=jnp.int32)
    earlier = jnp.concatenate([seq_ids[:1] - 1, seq_ids[:-1]])
    seq_start = lax.cummax(jnp.where(seq_ids != earlier, token_index, 0), axis=0)
    return (token_index - seq_start).astype(jnp.float32)


def visible(query_seq, query_end, seq_ids, block_ends):
    return (query_seq[:, None] == seq_ids[None, :]) & (block_ends[None, :] <= query_end[:, None])


def to_rows(values):
    return lax.all_to_all(values, "col", split_axis=0, concat_axis=1, tiled=True)


def to_tokens(values):
    return lax.all_to_all(values, "col", split_axis=1, concat_axis=0, tiled=True)


def col_sums(values):
    return lax.psum_scatter(values, "col", scatter_dimension=0, tiled=True)


def widen(values):
    return lax.all_gather(values, "col", axis=0, tiled=True)


def shards(
    layer_input,
    attn_gain,
    mlp_gain,
    query_weight,
    key_weight,
    value_weight,
    out_weight,
    gate_weight,
    up_weight,
    down_weight,
    seq_ids,
    block_ends,
    grad_output,
):
    col_index = lax.axis_index("col")
    query_rows = layer_input.shape[0]
    block_rows = min(512, query_rows)
    block_count = query_rows // block_rows
    heads_per_group = QUERY_HEADS // KEY_VALUE_HEADS
    group_head_width = heads_per_group * HEAD_SIZE_DIM
    query_width = QUERY_HEADS * HEAD_SIZE_DIM
    score_scale = HEAD_SIZE_DIM ** (-0.5)
    attn_gain_float = attn_gain.astype(jnp.float32)
    mlp_gain_float = mlp_gain.astype(jnp.float32)
    full_input = lax.all_gather(layer_input, "col", axis=0, tiled=True)
    token_rows = full_input.shape[0]
    query_cols, key_cols, value_cols, out_rows, gate_cols, up_cols, down_rows = (
        lax.all_gather(query_weight, "row", axis=0, tiled=True),
        lax.all_gather(key_weight, "row", axis=0, tiled=True),
        lax.all_gather(value_weight, "row", axis=0, tiled=True),
        lax.all_gather(out_weight, "row", axis=1, tiled=True),
        lax.all_gather(gate_weight, "row", axis=0, tiled=True),
        lax.all_gather(up_weight, "row", axis=0, tiled=True),
        lax.all_gather(down_weight, "row", axis=1, tiled=True),
    )
    input_float = full_input.astype(jnp.float32)
    inv_all = lax.rsqrt(jnp.mean(input_float * input_float, axis=1, keepdims=True) + eps)
    attn_in = (input_float * inv_all * attn_gain_float).astype(jnp.bfloat16)
    query_unrotated = jnp.dot(attn_in, query_cols, preferred_element_type=jnp.float32).astype(
        jnp.bfloat16
    )
    key_raw = jnp.dot(attn_in, key_cols, preferred_element_type=jnp.float32).astype(jnp.bfloat16)
    value_projected = jnp.dot(attn_in, value_cols, preferred_element_type=jnp.float32).astype(
        jnp.bfloat16
    )
    query_all = to_rows(query_unrotated)
    key_all, value_all = (
        lax.all_gather(key_raw, "col", axis=1, tiled=True),
        lax.all_gather(value_projected, "col", axis=1, tiled=True),
    )
    position = positions(seq_ids)
    row_start = col_index * query_rows
    query_pos = lax.dynamic_slice_in_dim(position, row_start, query_rows)
    query_seq = lax.dynamic_slice_in_dim(seq_ids, row_start, query_rows)
    query_end = lax.dynamic_slice_in_dim(block_ends, row_start, query_rows)
    query_cos, query_sin = rope_tables(query_pos, query_width, HEAD_SIZE_DIM)
    key_cos, key_sin = rope_tables(position, key_all.shape[1], HEAD_SIZE_DIM)
    query_rotated = (
        rotary(query_all.astype(jnp.float32), query_cos, query_sin, HEAD_SIZE_DIM) * score_scale
    ).astype(jnp.bfloat16)
    key_rotated = rotary(key_all.astype(jnp.float32), key_cos, key_sin, HEAD_SIZE_DIM).astype(
        jnp.bfloat16
    )

    def block_inputs(block_index):
        first_row = block_index * block_rows
        allowed = visible(query_seq, query_end, seq_ids, block_ends)
        return (first_row, allowed)

    def group_scores(query_block, group_index, allowed):
        query_head_rows = lax.dynamic_slice_in_dim(
            query_block, group_index * group_head_width, group_head_width, 1
        ).reshape(block_rows, heads_per_group, HEAD_SIZE_DIM)
        key_group = lax.dynamic_slice_in_dim(
            key_rotated, group_index * HEAD_SIZE_DIM, HEAD_SIZE_DIM, 1
        )
        value_group = lax.dynamic_slice_in_dim(
            value_all, group_index * HEAD_SIZE_DIM, HEAD_SIZE_DIM, 1
        )
        scores = jnp.einsum(
            "qhd,kd->hqk", query_head_rows, key_group, preferred_element_type=jnp.float32
        )
        return (query_head_rows, key_group, value_group, jnp.where(allowed[None], scores, neg_fill))

    def attend_block(block_index):
        first_row, allowed = block_inputs(block_index)

        def attend_head_group(group_index):
            query_head_rows, key_group, value_group, scores = group_scores(
                query_rotated, group_index, allowed
            )
            row_top = jnp.max(scores, axis=2, keepdims=True)
            powers = jnp.exp(scores - row_top)
            exp_total = jnp.sum(powers, axis=2, keepdims=True)
            attn_probs = (powers / exp_total).astype(jnp.bfloat16)
            weighted_values = jnp.einsum(
                "hqk,kd->qhd", attn_probs, value_group, preferred_element_type=jnp.float32
            )
            return (
                weighted_values.reshape(block_rows, group_head_width),
                (row_top + jnp.log(exp_total))[:, :, 0],
            )

        weighted_value_rows, logsumexp_rows = lax.map(
            attend_head_group, jnp.arange(KEY_VALUE_HEADS, dtype=jnp.int32)
        )
        return (
            jnp.transpose(weighted_value_rows, (1, 0, 2)).reshape(block_rows, query_width),
            logsumexp_rows,
        )

    mixed_blocks, log_blocks = lax.map(attend_block, jnp.arange(block_count, dtype=jnp.int32))
    attn_rows = mixed_blocks.reshape(query_rows, query_width).astype(jnp.bfloat16)
    attn_tokens = to_tokens(attn_rows)
    attn_share = col_sums(jnp.dot(attn_tokens, out_rows, preferred_element_type=jnp.float32))
    residual = layer_input.astype(jnp.float32) + attn_share
    inv_two = lax.rsqrt(jnp.mean(residual * residual, axis=1, keepdims=True) + eps)
    normed_two = residual * inv_two
    mlp_in = widen((normed_two * mlp_gain_float).astype(jnp.bfloat16))
    gate_act = jnp.dot(mlp_in, gate_cols, preferred_element_type=jnp.float32)
    up_act = jnp.dot(mlp_in, up_cols, preferred_element_type=jnp.float32)
    hidden = (jax.nn.silu(gate_act) * up_act).astype(jnp.bfloat16)
    mlp_share = col_sums(jnp.dot(hidden, down_rows, preferred_element_type=jnp.float32))
    layer_output = (residual + mlp_share).astype(jnp.bfloat16)
    grad_float = grad_output.astype(jnp.float32)
    grad_full = widen(grad_output)
    grad_down = jnp.einsum("tf,td->fd", hidden, grad_full, preferred_element_type=jnp.float32)
    grad_hidden = jnp.einsum("td,fd->tf", grad_full, down_rows, preferred_element_type=jnp.float32)
    gate_sigmoid = jax.nn.sigmoid(gate_act)
    grad_gate_act = (
        grad_hidden * up_act * gate_sigmoid * (1.0 + gate_act * (1.0 - gate_sigmoid))
    ).astype(jnp.bfloat16)
    grad_up_act = (grad_hidden * gate_act * gate_sigmoid).astype(jnp.bfloat16)
    grad_gate = jnp.einsum("td,tf->df", mlp_in, grad_gate_act, preferred_element_type=jnp.float32)
    grad_up = jnp.einsum("td,tf->df", mlp_in, grad_up_act, preferred_element_type=jnp.float32)
    grad_mlp_share = col_sums(
        jnp.einsum("tf,df->td", grad_gate_act, gate_cols, preferred_element_type=jnp.float32)
        + jnp.einsum("tf,df->td", grad_up_act, up_cols, preferred_element_type=jnp.float32)
    )
    scaled_two = grad_mlp_share * mlp_gain_float
    inner_two = jnp.mean(scaled_two * normed_two, axis=1, keepdims=True)
    grad_residual = grad_float + inv_two * (scaled_two - normed_two * inner_two)
    grad_mlp_gain = jnp.sum(grad_mlp_share * normed_two, axis=0)
    grad_branch = grad_residual.astype(jnp.bfloat16)
    grad_attn_full = widen(grad_branch)
    grad_out_weight = jnp.einsum(
        "tq,td->qd", attn_tokens, grad_attn_full, preferred_element_type=jnp.float32
    )
    grad_mixture = to_rows(
        jnp.einsum(
            "td,qd->tq", grad_attn_full, out_rows, preferred_element_type=jnp.float32
        ).astype(jnp.bfloat16)
    )

    def back_block(carried_state, scan_items):
        block_index, block_log_total = scan_items
        first_row, allowed = block_inputs(block_index)

        def backward_head_group(inner_acc, group_items):
            group_index, log_group = group_items
            keys_acc, values_acc = inner_acc
            query_head_rows, key_group, value_group, scores = group_scores(
                query_rotated, group_index, allowed
            )
            attn_probs = jnp.exp(scores - log_group[:, :, None])
            grad_heads = lax.dynamic_slice_in_dim(
                grad_mixture, group_index * group_head_width, group_head_width, 1
            ).reshape(block_rows, heads_per_group, HEAD_SIZE_DIM)
            grad_probs = jnp.einsum(
                "qhd,kd->hqk", grad_heads, value_group, preferred_element_type=jnp.float32
            )
            value_piece = jnp.einsum(
                "hqk,qhd->kd",
                attn_probs.astype(jnp.bfloat16),
                grad_heads,
                preferred_element_type=jnp.float32,
            )
            inner_dot = jnp.sum(attn_probs * grad_probs, axis=2, keepdims=True)
            grad_scores = (attn_probs * (grad_probs - inner_dot)).astype(jnp.bfloat16)
            query_piece = jnp.einsum(
                "hqk,kd->qhd", grad_scores, key_group, preferred_element_type=jnp.float32
            ).reshape(block_rows, group_head_width)
            key_piece = jnp.einsum(
                "hqk,qhd->kd", grad_scores, query_head_rows, preferred_element_type=jnp.float32
            )
            column = group_index * HEAD_SIZE_DIM
            keys_acc = lax.dynamic_update_slice_in_dim(
                keys_acc,
                lax.dynamic_slice_in_dim(keys_acc, column, HEAD_SIZE_DIM, 1) + key_piece,
                column,
                1,
            )
            values_acc = lax.dynamic_update_slice_in_dim(
                values_acc,
                lax.dynamic_slice_in_dim(values_acc, column, HEAD_SIZE_DIM, 1) + value_piece,
                column,
                1,
            )
            return ((keys_acc, values_acc), query_piece)

        carried_state, query_pieces = lax.scan(
            backward_head_group,
            carried_state,
            (jnp.arange(KEY_VALUE_HEADS, dtype=jnp.int32), block_log_total),
        )
        return (
            carried_state,
            jnp.transpose(query_pieces, (1, 0, 2)).reshape(block_rows, query_width),
        )

    zeros_kv = jnp.zeros((token_rows, key_all.shape[1]), jnp.float32)
    (grad_keys, grad_values), query_blocks = lax.scan(
        back_block, (zeros_kv, zeros_kv), (jnp.arange(block_count, dtype=jnp.int32), log_blocks)
    )
    grad_query_rot = query_blocks.reshape(query_rows, query_width)
    grad_query_raw = to_tokens(
        rotary_back(grad_query_rot * score_scale, query_cos, query_sin, HEAD_SIZE_DIM).astype(
            jnp.bfloat16
        )
    )
    grad_key_part = rotary_back(grad_keys, key_cos, key_sin, HEAD_SIZE_DIM)
    grad_key_sum, grad_value_sum = (
        lax.psum_scatter(grad_key_part, "col", scatter_dimension=1, tiled=True),
        lax.psum_scatter(grad_values, "col", scatter_dimension=1, tiled=True),
    )
    grad_key_raw = grad_key_sum.astype(jnp.bfloat16)
    grad_value_raw = grad_value_sum.astype(jnp.bfloat16)
    grad_query = jnp.einsum(
        "td,tq->dq", attn_in, grad_query_raw, preferred_element_type=jnp.float32
    )
    grad_key = jnp.einsum("td,tq->dq", attn_in, grad_key_raw, preferred_element_type=jnp.float32)
    grad_value = jnp.einsum(
        "td,tq->dq", attn_in, grad_value_raw, preferred_element_type=jnp.float32
    )
    grad_attn_share = col_sums(
        jnp.einsum("tq,dq->td", grad_query_raw, query_cols, preferred_element_type=jnp.float32)
        + jnp.einsum("tq,dq->td", grad_key_raw, key_cols, preferred_element_type=jnp.float32)
        + jnp.einsum("tq,dq->td", grad_value_raw, value_cols, preferred_element_type=jnp.float32)
    )
    own_float = layer_input.astype(jnp.float32)
    inv_one = lax.rsqrt(jnp.mean(own_float * own_float, axis=1, keepdims=True) + eps)
    normed_one = own_float * inv_one
    scaled_one = grad_attn_share * attn_gain_float
    inner_one = jnp.mean(scaled_one * normed_one, axis=1, keepdims=True)
    grad_input = (grad_residual + inv_one * (scaled_one - normed_one * inner_one)).astype(
        jnp.bfloat16
    )
    grad_attn_gain = jnp.sum(grad_attn_share * normed_one, axis=0)
    weight_sums = (
        lax.psum_scatter(grad_query, "row", scatter_dimension=0, tiled=True),
        lax.psum_scatter(grad_key, "row", scatter_dimension=0, tiled=True),
        lax.psum_scatter(grad_value, "row", scatter_dimension=0, tiled=True),
        lax.psum_scatter(grad_out_weight, "row", scatter_dimension=1, tiled=True),
        lax.psum_scatter(grad_gate, "row", scatter_dimension=0, tiled=True),
        lax.psum_scatter(grad_up, "row", scatter_dimension=0, tiled=True),
        lax.psum_scatter(grad_down, "row", scatter_dimension=1, tiled=True),
    )
    gain_sums = lax.psum((grad_attn_gain, grad_mlp_gain), ("row", "col"))
    return (
        layer_output,
        grad_input,
        gain_sums[0],
        gain_sums[1],
        weight_sums[0],
        weight_sums[1],
        weight_sums[2],
        weight_sums[3],
        weight_sums[4],
        weight_sums[5],
        weight_sums[6],
    )


def solution(mesh):
    in_specs = (
        P(("row", "col"), None),
        P(),
        P(),
        P("row", "col"),
        P("row", "col"),
        P("row", "col"),
        P("col", "row"),
        P("row", "col"),
        P("row", "col"),
        P("col", "row"),
        P("row"),
        P("row"),
        P(("row", "col"), None),
    )
    out_specs = (
        P(("row", "col"), None),
        P(("row", "col"), None),
        P(),
        P(),
        P("row", "col"),
        P("row", "col"),
        P("row", "col"),
        P("col", "row"),
        P("row", "col"),
        P("row", "col"),
        P("col", "row"),
    )
    return jax.shard_map(shards, mesh=mesh, in_specs=in_specs, out_specs=out_specs, check_vma=False)
```

profile of v0, /device:TPU:0, one launch (start us, length us, event | category | flops | bytes accessed | tf_op | source)
XLA Modules:
  0.0 1523.2 jit_solution(14034235379282888117)
XLA Ops:
  14.5 24.8 %all_gather.42 = bf16[1152,192]{1,0:T(8,128)(2,1)S(1)} all-gather(bf16[72,192]{1,0:T(8,128)(2,1)S(1)} %copy-done.33), channel_id=1, replica_groups=mesh['row'=16,'col'=2] {'row'}, dimensions={0}, use_global_device_ids=true | all-gather | bytes 470016 | tf_op jit(solution)/shard_map/all_gather | solution.py:96
  39.4 19.0 %all_gather.40 = bf16[1152,192]{1,0:T(8,128)(2,1)S(1)} all-gather(bf16[72,192]{1,0:T(8,128)(2,1)S(1)} %copy-done.34), channel_id=1, replica_groups=mesh['row'=16,'col'=2] {'row'}, dimensions={0}, use_global_device_ids=true | all-gather | bytes 470016 | tf_op jit(solution)/shard_map/all_gather | solution.py:97
  62.2 12.0 all_gather.43
  76.2 11.4 all_gather.41
  115.5 11.3 fusion.64
  126.8 62.2 %while.50 = (s32[]{:T(128)}, bf16[6,512,192]{1,2,0:T(8,128)(2,1)S(1)}, f32[6,3,512]{2,1,0:T(4,128)}, s32[6]{0:T(128)S(1)}, bf16[1024,384]{0,1:T(8,128)(2,1)}, /*...) while((s32[]{:T(128)}, ...), condition=%wide.region_6.7_spmd.clone.clone, body=%wide.region_3.6_spmd.clone.sunk.clone | while | flops 418380288 | bytes 22477056 | solution.py:171
  189.0 17.3 %all_to_all.64 = bf16[512,2,576]{0,2,1:T(8,128)(2,1)S(1)} all-to-all(bf16[512,2,576]{0,2,1:T(8,128)(2,1)S(1)} %bitcast.276), channel_id=1, replica_groups=mesh['row'=16,'col'=2] {'col'}, dimensions={1} | all-to-all | bytes 2359296 | tf_op jit(solution)/shard_map/all_to_all | solution.py:56
  214.1 56.8 %reduce-scatter.18.cloned.1.call-done = f32[512,1152]{1,0:T(8,128)} async-done(((f32[1024,1152]{1,0:T(8,128)}), f32[512,1152]{1,0:T(8,128)}) %reduce-scatter.18.cloned.1.call-update) | async-done | bytes 2359312 | tf_op jit(solution)/shard_map/reduce_scatter | solution.py:60
  277.9 42.6 %all-gather.20.cloned.1.call-done = bf16[1152,1536]{1,0:T(8,128)(2,1)} async-done(((bf16[72,1536]{1,0:T(8,128)(2,1)}), bf16[1152,1536]{1,0:T(8,128)(2,1)}) %all-gather.20.cloned.1.call-update) | async-done | bytes 3538960 | tf_op jit(solution)/shard_map/all_gather | solution.py:100
  320.5 37.1 %all-gather.16.cloned.1.call-done = bf16[1024,1152]{1,0:T(8,128)(2,1)} async-done(((bf16[512,1152]{1,0:T(8,128)(2,1)}), bf16[1024,1152]{1,0:T(8,128)(2,1)}) %all-gather.16.cloned.1.call-update) | async-done | bytes 2359312 | tf_op jit(solution)/shard_map/all_gather | solution.py:64
  357.6 9.6 fusion.126
  367.3 40.2 %all-gather.18.cloned.1.call-done = bf16[1152,1536]{1,0:T(8,128)(2,1)} async-done(((bf16[72,1536]{1,0:T(8,128)(2,1)}), bf16[1152,1536]{1,0:T(8,128)(2,1)}) %all-gather.18.cloned.1.call-update) | async-done | bytes 3538960 | tf_op jit(solution)/shard_map/all_gather | solution.py:99
  407.4 9.7 fusion.125
  417.1 27.0 %all-gather.24.cloned.1.call-done = bf16[1024,1152]{1,0:T(8,128)(2,1)} async-done(((bf16[512,1152]{1,0:T(8,128)(2,1)}), bf16[1024,1152]{1,0:T(8,128)(2,1)}) %all-gather.24.cloned.1.call-update) | async-done | bytes 2359312 | tf_op jit(solution)/shard_map/all_gather | solution.py:64
  444.1 49.8 %all-gather.22.cloned.1.call-done = bf16[1536,1152]{0,1:T(8,128)(2,1)} async-done(((bf16[1536,72]{0,1:T(8,128)(2,1)}), bf16[1536,1152]{0,1:T(8,128)(2,1)}) %all-gather.22.cloned.1.call-update) | async-done | bytes 3538960 | tf_op jit(solution)/shard_map/all_gather | solution.py:101
  493.9 12.5 multiply_convert_fusion
  516.8 59.1 %reduce-scatter.22.cloned.1.call-done = f32[512,1152]{1,0:T(8,128)} async-done(((f32[1024,1152]{1,0:T(8,128)}), f32[512,1152]{1,0:T(8,128)}) %reduce-scatter.22.cloned.1.call-update) | async-done | bytes 2359312 | tf_op jit(solution)/shard_map/reduce_scatter | solution.py:60
  581.8 36.2 %all-gather.26.cloned.1.call-done = bf16[1024,1152]{1,0:T(8,128)(2,1)} async-done(((bf16[512,1152]{1,0:T(8,128)(2,1)}), bf16[1024,1152]{1,0:T(8,128)(2,1)}) %all-gather.26.cloned.1.call-update) | async-done | bytes 2359312 | tf_op jit(solution)/shard_map/all_gather | solution.py:64
  627.7 15.1 all-to-all-done.2
  645.5 125.0 %while.51 = (s32[]{:T(128)}, f32[1024,384]{0,1:T(8,128)}, f32[1024,384]{0,1:T(8,128)}, f32[6,512,192]{1,2,0:T(8,128)}, s32[6]{0:T(128)S(1)}, /*index=5*/bf16[102...) while((s32[]{:T(128)}, f32[1024,384]{0,1:T(8,128)}, ...), condition=%wide.region_15.16_spmd.clone.clone, body=%wide.region_13.15_spmd.clone.sunk.clone | while | flops 1027209728 | bytes 55630144 | solution.py:268
  796.7 8.7 subtract_convert_fusion
  805.4 18.5 %all_to_all.65 = bf16[512,2,576]{0,2,1:T(8,128)(2,1)S(1)} all-to-all(bf16[512,2,576]{0,2,1:T(8,128)(2,1)S(1)} %subtract_convert_fusion), channel_id=1, replica_groups=mesh['row'=16,'col'=2] {'col'}, dimensions={1} | all-to-all | bytes 2359296 | tf_op jit(solution)/shard_map/all_to_all | solution.py:56
  846.7 9.4 fusion.127
  909.8 40.1 %all-reduce.2 = (f32[1152]{0:T(1024)}, f32[1152]{0:T(1024)}) all-reduce(f32[1152]{0:T(1024)} %get-tuple-element.251, f32[1152]{0:T(1024)} %get-tuple-element.249), channel_id=1, replica_groups=mesh['row'=16,'col'=2] {'row','col'}, use_global_device_ids=true, to_apply=%region_21.22 | all-reduce | flops 2304 | bytes 18432 | tf_op jit(solution)/shard_map/psum | solution.py:325
  951.1 19.2 %reduce-scatter.20.cloned.1.call-done = f32[512,1152]{1,0:T(8,128)} async-done(((f32[1024,1152]{1,0:T(8,128)}), f32[512,1152]{1,0:T(8,128)}) %reduce-scatter.20.cloned.1.call-update) | async-done | bytes 2359312 | tf_op jit(solution)/shard_map/reduce_scatter | solution.py:60
  975.4 89.2 %reduce-scatter.38.cloned.1.call-done = f32[1536,72]{0,1:T(8,128)} async-done(((f32[1536,1152]{0,1:T(8,128)}), f32[1536,72]{0,1:T(8,128)}) %reduce-scatter.38.cloned.1.call-update) | async-done | bytes 442384 | tf_op jit(solution)/shard_map/reduce_scatter | solution.py:323
  1064.7 94.5 %reduce-scatter.36.cloned.1.call-done = f32[72,1536]{1,0:T(8,128)} async-done(((f32[1152,1536]{1,0:T(8,128)}), f32[72,1536]{1,0:T(8,128)}) %reduce-scatter.36.cloned.1.call-update) | async-done | bytes 442384 | tf_op jit(solution)/shard_map/reduce_scatter | solution.py:322
  1159.2 94.0 %reduce-scatter.34.cloned.1.call-done = f32[72,1536]{1,0:T(8,128)} async-done(((f32[1152,1536]{1,0:T(8,128)}), f32[72,1536]{1,0:T(8,128)}) %reduce-scatter.34.cloned.1.call-update) | async-done | bytes 442384 | tf_op jit(solution)/shard_map/reduce_scatter | solution.py:321
  1253.3 69.9 %reduce-scatter.42.cloned.1.call-done = f32[576,72]{0,1:T(8,128)} async-done(((f32[576,1152]{0,1:T(8,128)}), f32[576,72]{0,1:T(8,128)}) %reduce-scatter.42.cloned.1.call-update) | async-done | bytes 165904
  1323.1 61.6 %reduce-scatter.32.cloned.1.call-done = f32[72,192]{1,0:T(8,128)} async-done(((f32[1152,192]{1,0:T(8,128)}), f32[72,192]{1,0:T(8,128)}) %reduce-scatter.32.cloned.1.call-update) | async-done | bytes 55312 | tf_op jit(solution)/shard_map/reduce_scatter | solution.py:319
  1384.8 61.8 %reduce-scatter.30.cloned.1.call-done = f32[72,192]{1,0:T(8,128)} async-done(((f32[1152,192]{1,0:T(8,128)}), f32[72,192]{1,0:T(8,128)}) %reduce-scatter.30.cloned.1.call-update) | async-done | bytes 55312 | tf_op jit(solution)/shard_map/reduce_scatter | solution.py:318
  1446.6 69.3 %reduce-scatter.40.cloned.1.call-done = f32[72,576]{1,0:T(8,128)} async-done(((f32[1152,576]{1,0:T(8,128)}), f32[72,576]{1,0:T(8,128)}) %reduce-scatter.40.cloned.1.call-update) | async-done | bytes 165904
  (358 shorter events, 363.0 us)
Async XLA Ops:
  7.2 51.2 %all-gather.10.cloned.1.call-start = ((), (), s32[]{:S(2)}) async-start(), calls=%async_computation.17 | async-start | bytes 3538944 | tf_op jit(solution)/shard_map/all_gather | solution.py:92
  8.0 82.0 %all-gather.12.cloned.1.call-start = ((), (), s32[]{:S(2)}) async-start(), calls=%async_computation.18 | async-start | bytes 1566720 | tf_op jit(solution)/shard_map/all_gather | solution.py:95
  8.7 197.8 %all-gather.14.cloned.1.call-start = ((), (), s32[]{:S(2)}) async-start(), calls=%async_computation.19 | async-start | bytes 1566720 | tf_op jit(solution)/shard_map/all_gather | solution.py:98
  13.9 47.0 %copy-start.24 = (f32[1024]{0:T(1024)}, f32[1024]{0:T(1024)S(1)}, u32[]{:S(2)}) copy-start(f32[1024]{0:T(1024)S(1)} %fusion.97) | copy-start | bytes 12292
  95.1 19.3 %all-to-all-start = ((bf16[2,512,576]{1,2,0:T(8,128)(2,1)}), bf16[2,512,576]{1,2,0:T(8,128)(2,1)S(1)}, u32[]{:S(2)}, u32[]{:S(2)}) async-start(bf16[2,512,576]{1,2,0:T(8,128)(2,1)} %bitcast.277), calls=%async_computation | async-start | bytes 2359296 | tf_op jit(solution)/shard_map/all_to_all | solution.py:52
  98.7 172.2 %reduce-scatter.18.cloned.1.call-start = ((), (), s32[]{:S(2)}) async-start(), calls=%async_computation.20 | async-start | bytes 7077888 | tf_op jit(solution)/shard_map/reduce_scatter | solution.py:60
  212.8 58.1 %copy-start.7 = (bf16[512,1152]{1,0:T(8,128)(2,1)S(1)}, bf16[512,1152]{1,0:T(8,128)(2,1)}, u32[]{:S(2)}) copy-start(bf16[512,1152]{1,0:T(8,128)(2,1)} %param.17) | copy-start | bytes 3538948
  212.8 107.7 %all-gather.20.cloned.1.call-start = ((), (), s32[]{:S(2)}) async-start(), calls=%async_computation.23 | async-start | bytes 3760128 | tf_op jit(solution)/shard_map/all_gather | solution.py:100
  213.4 144.2 %all-gather.16.cloned.1.call-start = ((), (), s32[]{:S(2)}) async-start(), calls=%async_computation.21 | async-start | bytes 3538944 | tf_op jit(solution)/shard_map/all_gather | solution.py:64
  273.7 305.2 %copy-start.1 = (f32[512,1152]{1,0:T(8,128)}, f32[512,1152]{1,0:T(8,128)S(1)}, u32[]{:S(2)}) copy-start(f32[512,1152]{1,0:T(8,128)S(1)} %get-tuple-element.306) | copy-start | bytes 7077892
  275.3 132.2 %all-gather.18.cloned.1.call-start = ((), (), s32[]{:S(2)}) async-start(), calls=%async_computation.22 | async-start | bytes 3760128 | tf_op jit(solution)/shard_map/all_gather | solution.py:99
  276.0 168.1 %all-gather.24.cloned.1.call-start = ((), (), s32[]{:S(2)}) async-start(), calls=%async_computation.26 | async-start | bytes 3538944 | tf_op jit(solution)/shard_map/all_gather | solution.py:64
  276.8 217.1 %all-gather.22.cloned.1.call-start = ((), (), s32[]{:S(2)}) async-start(), calls=%async_computation.24 | async-start | bytes 3760128 | tf_op jit(solution)/shard_map/all_gather | solution.py:101
  277.5 298.4 %reduce-scatter.22.cloned.1.call-start = ((), (), s32[]{:S(2)}) async-start(), calls=%async_computation.27 | async-start | bytes 7077888 | tf_op jit(solution)/shard_map/reduce_scatter | solution.py:60
  516.7 62.8 %copy-start.9 = (bf16[512,1152]{1,0:T(8,128)(2,1)S(1)}, bf16[512,1152]{1,0:T(8,128)(2,1)}, u32[]{:S(2)}) copy-start(bf16[512,1152]{1,0:T(8,128)(2,1)} %param.29) | copy-start | bytes 3538948
  516.7 101.3 %all-gather.26.cloned.1.call-start = ((), (), s32[]{:S(2)}) async-start(), calls=%async_computation.28 | async-start | bytes 3538944 | tf_op jit(solution)/shard_map/all_gather | solution.py:64
  623.0 19.8 %all-to-all-start.2 = ((bf16[2,512,576]{1,2,0:T(8,128)(2,1)}), bf16[2,512,576]{1,2,0:T(8,128)(2,1)}, u32[]{:S(2)}, u32[]{:S(2)}) async-start(bf16[2,512,576]{1,2,0:T(8,128)(2,1)} %bitcast.162), calls=%async_computation.5 | async-start | bytes 2359296 | tf_op jit(solution)/shard_map/all_to_all | solution.py:52
  627.4 201.0 %reduce-scatter.24.cloned.1.call-start = ((), (), s32[]{:S(2)}) async-start(), calls=%async_computation.29 | async-start | bytes 2359296 | tf_op jit(solution)/shard_map/reduce_scatter | solution.py:290
  645.5 125.0 %copy-start.26 = (f32[1024]{0:T(1024)S(1)}, f32[1024]{0:T(1024)}, u32[]{:S(2)}) copy-start(f32[1024]{0:T(1024)} %copy-done.24) | copy-start | bytes 12292
  645.5 125.0 %copy-start.36 = (f32[384]{0:T(512)S(1)}, f32[384]{0:T(512)}, u32[]{:S(2)}) copy-start(f32[384]{0:T(512)} %fusion.100) | copy-start | bytes 4612
  785.3 55.7 %reduce-scatter.26.cloned.1.call-start = ((), (), s32[]{:S(2)}) async-start(), calls=%async_computation.30 | async-start | bytes 2359296 | tf_op jit(solution)/shard_map/reduce_scatter | solution.py:291
  794.4 112.4 %reduce-scatter.28.cloned.1.call-start = ((), (), s32[]{:S(2)}) async-start(), calls=%async_computation.31 | async-start | bytes 7077888 | tf_op jit(solution)/shard_map/reduce_scatter | solution.py:60
  846.7 123.7 %reduce-scatter.20.cloned.1.call-start = ((), (), s32[]{:S(2)}) async-start(), calls=%async_computation.25 | async-start | bytes 7077888 | tf_op jit(solution)/shard_map/reduce_scatter | solution.py:60
  856.1 208.6 %reduce-scatter.38.cloned.1.call-start = ((), (), s32[]{:S(2)}) async-start(), calls=%async_computation.36 | async-start | bytes 7520256 | tf_op jit(solution)/shard_map/reduce_scatter | solution.py:323
  865.4 293.8 %reduce-scatter.36.cloned.1.call-start = ((), (), s32[]{:S(2)}) async-start(), calls=%async_computation.35 | async-start | bytes 7520256 | tf_op jit(solution)/shard_map/reduce_scatter | solution.py:322
  874.7 378.6 %reduce-scatter.34.cloned.1.call-start = ((), (), s32[]{:S(2)}) async-start(), calls=%async_computation.34 | async-start | bytes 7520256 | tf_op jit(solution)/shard_map/reduce_scatter | solution.py:321
  882.6 440.5 %reduce-scatter.42.cloned.1.call-start = ((), (), s32[]{:S(2)}) async-start(), calls=%async_computation.38 | async-start | bytes 3133440
  889.3 495.4 %reduce-scatter.32.cloned.1.call-start = ((), (), s32[]{:S(2)}) async-start(), calls=%async_computation.33 | async-start | bytes 1253376 | tf_op jit(solution)/shard_map/reduce_scatter | solution.py:319
  894.2 552.4 %reduce-scatter.30.cloned.1.call-start = ((), (), s32[]{:S(2)}) async-start(), calls=%async_computation.32 | async-start | bytes 1253376 | tf_op jit(solution)/shard_map/reduce_scatter | solution.py:318
  897.5 618.4 %reduce-scatter.40.cloned.1.call-start = ((), (), s32[]{:S(2)}) async-start(), calls=%async_computation.37 | async-start | bytes 3133440
  901.6 68.7 %copy-start.2 = (f32[512,1152]{1,0:T(8,128)S(1)}, f32[512,1152]{1,0:T(8,128)}, u32[]{:S(2)}) copy-start(f32[512,1152]{1,0:T(8,128)} %copy-done.1) | copy-start | bytes 7077892
  901.6 68.7 %copy-start.23 = (f32[1152]{0:T(1024)S(1)}, f32[1152]{0:T(1024)}, u32[]{:S(2)}) copy-start(f32[1152]{0:T(1024)} %convert_element_type.142) | copy-start | bytes 13828
  (51 other events, 326.2 us)
Sparse Core Ops, SparseCore 0:
  9.6 38.7 all-gather.9
  50.6 39.3 all-gather.11
  92.1 38.1 all-gather.13
  212.9 57.8 reduce-scatter.17
  273.3 47.1 all-gather.19
  322.5 35.0 all-gather.15
  360.2 47.1 all-gather.17
  409.0 35.0 all-gather.23
  446.7 47.1 all-gather.21
  516.8 58.9 reduce-scatter.21
  582.0 36.0 all-gather.25
  785.4 26.4 reduce-scatter.23
  814.2 26.7 reduce-scatter.25
  846.8 59.9 reduce-scatter.27
  909.1 61.2 reduce-scatter.19
  974.8 89.8 reduce-scatter.37
  1069.6 89.5 reduce-scatter.35
  1163.7 89.5 reduce-scatter.33
  1258.3 64.8 reduce-scatter.41
  1327.6 57.0 reduce-scatter.31
  1389.4 57.1 reduce-scatter.29
  1451.6 64.2 reduce-scatter.39
where the time goes:
time: 1530 us; the launch traced here: 1520 us
  waiting for transfers between devices  949 us (62%)
  matrix products  228 us (15%)
  blocking collectives  143 us (9%)
  other arithmetic  115 us (8%)
  local copies, waits for them, and re-layouts  45.7 us (3%)
  loops' own time  16.1 us (1%)
  between operations  16.1 us (1%)
    unnamed x24, waiting for transfers between devices  144 us
    reduce_scatter x4, waiting for transfers between devices, col_sums(): return lax.psum_scatter(values, 'col', scatter_dimension=0, tiled=True)  139 us
    all_gather x3, waiting for transfers between devices, widen(): return lax.all_gather(values, 'col', axis=0, tiled=True)  100 us
    reduce_scatter x1, waiting for transfers between devices, shards(): lax.psum_scatter(grad_up, 'row', scatter_dimension=0, tiled=True)  94.5 us
    reduce_scatter x1, waiting for transfers between devices, shards(): lax.psum_scatter(grad_gate, 'row', scatter_dimension=0, tiled=True)  94 us
    reduce_scatter x1, waiting for transfers between devices, shards(): lax.psum_scatter(grad_down, 'row', scatter_dimension=1, tiled=True)  89.2 us
    reduce_scatter x1, waiting for transfers between devices, shards(): lax.psum_scatter(grad_key, 'row', scatter_dimension=0, tiled=True)  61.8 us
    reduce_scatter x1, waiting for transfers between devices, shards(): lax.psum_scatter(grad_value, 'row', scatter_dimension=0, tiled=True)  61.6 us
  transfers between devices with their start and end apart: 24, of which 21 were waited for; matrix products, arithmetic and copies ran while one was open for 13% of the time, Pallas kernels for 0%

commit v1 on v0

v1 whole, which is shorter than its diff:
```python
import math

import jax
import jax.numpy as jnp
from jax import lax
from jax.experimental import pallas as pl
from jax.experimental.pallas import tpu as pltpu
from jax.sharding import PartitionSpec as P

HEAD = 64
LANES = 128
eps = 1e-05
rope_base = 10000.0
neg_fill = -1e30
f32 = jnp.float32
bf16 = jnp.bfloat16
VMEM_BYTES = 60 * 1024 * 1024


def dot_nn(a, b):
    return lax.dot_general(a, b, (((1,), (0,)), ((), ())), preferred_element_type=f32)


def dot_nt(a, b):
    return lax.dot_general(a, b, (((1,), (1,)), ((), ())), preferred_element_type=f32)


def halves(values):
    rows, cols = values.shape
    return jnp.transpose(values.reshape(rows, 2, cols // 2), (1, 0, 2))


def whole(values):
    two, rows, cols = values.shape
    return jnp.transpose(values, (1, 0, 2)).reshape(rows, two * cols)


def gather_any(weights):
    query, key, value, out, gate, up, down = weights

    def both(weight, row_axis):
        part = lax.all_gather(weight, "row", axis=row_axis, tiled=True)
        return lax.all_gather(part, "col", axis=1 - row_axis, tiled=True)

    mix = [halves(both(key, 0)), halves(both(value, 0)), halves(both(query, 0)), halves(both(out, 1).T)]
    return [
        jnp.concatenate(mix, axis=2),
        halves(both(gate, 0)),
        halves(both(up, 0)),
        halves(both(down, 1).T),
    ]


def scatter_any(grads, gains):
    first, gate, up, down = [grad.astype(f32) for grad in grads]
    kv = first.shape[2] // 8
    key, value, query, out = (
        whole(first[:, :, :kv]),
        whole(first[:, :, kv : 2 * kv]),
        whole(first[:, :, 2 * kv : 5 * kv]),
        whole(first[:, :, 5 * kv :]).T,
    )

    def both(grad, row_axis):
        part = lax.psum_scatter(grad, "row", scatter_dimension=row_axis, tiled=True)
        return lax.psum_scatter(part, "col", scatter_dimension=1 - row_axis, tiled=True)

    return (
        lax.psum(gains, ("row", "col")),
        (
            both(query, 0),
            both(key, 0),
            both(value, 0),
            both(out, 1),
            both(whole(gate), 0),
            both(whole(up), 0),
            both(whole(down).T, 1),
        ),
    )


PACKS = 4
MESH = pl.DeviceIdType.MESH


class Place:
    def __init__(self):
        row, x = lax.axis_index("row"), lax.axis_index("col")
        z, y, c = row // 4, (row // 2) % 2, row % 2
        self.x, self.z, self.y, self.c = x, z, y, c
        self.xa, self.ya = jnp.where(c == 0, 1 - x, x), jnp.where(c == 0, y, 1 - y)
        self.xb, self.yb = jnp.where(c == 0, x, 1 - x), jnp.where(c == 0, 1 - y, y)
        self.others = [(z + k) % 4 for k in (1, 2, 3)]
        self.line = [self.device(x, other, y, c) for other in self.others]
        self.near = self.device(self.xa, z, self.ya, c)
        self.far = self.device(self.xb, z, self.yb, c)
        self.twin = self.device(x, z, y, 1 - c)

    @staticmethod
    def device(x, z, y, c):
        return ((z * 2 + y) * 2 + c, x)

    def greet(self):
        barrier = pltpu.get_barrier_semaphore()
        for peer in self.line + [self.near, self.far, self.twin]:
            pl.semaphore_signal(barrier, inc=1, device_id=peer, device_id_type=MESH)
        pl.semaphore_wait(barrier, 6)


def remote(src, dst, send, recv, device):
    return pltpu.make_async_remote_copy(
        src_ref=src, dst_ref=dst, send_sem=send, recv_sem=recv, device_id=device, device_id_type=MESH
    )


GATHER_PLAN = [(p, h * 768, 768, (0, 0, 0, 1, 0, 0, 0, 1)[2 * p + h]) for p in range(PACKS) for h in range(2)]
SCATTER_PLAN = [(p, h * 768, 768) for p in range(PACKS) for h in range(2)]


def gather_kernel(plan, ahead, own_ref, out_ref, copied, sent, came):
    at = Place()
    at.greet()
    x, y, z, c = at.x, at.y, at.z, at.c
    steps = []
    for i, (pack, lane, lanes, kind) in enumerate(plan):
        cols = pl.ds(lane, lanes)
        own = own_ref.at[pack, :, cols]

        def one(xx, yy):
            return out_ref.at[pack, xx, z, yy, c, :, cols]

        def line(xx, yy, slot, device):
            ref = out_ref.at[pack, xx, :, yy, c, :, cols]
            return remote(ref, ref, sent.at[i, slot], came.at[i, slot], device)

        step = {"kind": kind, "keep": pltpu.make_async_copy(own, one(x, y), copied.at[i])}
        step["line"] = [remote(own, one(x, y), sent.at[i, k], came.at[i, k], at.line[k]) for k in range(3)]
        if kind == 0:
            step["near"] = line(x, y, 3, at.near)
        else:
            step["near"] = remote(own, one(x, y), sent.at[i, 3], came.at[i, 3], at.near)
            step["more"] = [
                remote(one(at.xa, at.ya), one(at.xa, at.ya), sent.at[i, 4 + k], came.at[i, 4 + k], at.line[k])
                for k in range(3)
            ]
        step["far"] = [line(x, y, 7, at.far), line(at.xa, at.ya, 8, at.far)]
        step["twin"] = [
            line(xx, yy, 9 + j, at.twin)
            for j, (xx, yy) in enumerate([(x, y), (at.xa, at.ya), (at.xb, at.yb), (1 - x, 1 - y)])
        ]
        steps.append(step)
    count = len(steps)

    def begin(i):
        if 0 <= i < count:
            steps[i]["keep"].start()
            for copy in steps[i]["line"]:
                copy.start()
            if steps[i]["kind"] == 1:
                steps[i]["near"].start()

    def first(i):
        if 0 <= i < count:
            step = steps[i]
            if step["kind"] == 1:
                step["near"].wait_recv()
                for copy in step["more"]:
                    copy.start()
            for copy in step["line"]:
                copy.wait_recv()
            step["keep"].wait()
            if step["kind"] == 0:
                step["near"].start()
            step["far"][0].start()
            step["twin"][0].start()

    def second(i):
        if 0 <= i < count:
            step = steps[i]
            for copy in [step["near"]] if step["kind"] == 0 else step["more"]:
                copy.wait_recv()
            step["far"][1].start()
            step["twin"][1].start()

    def third(i):
        if 0 <= i < count:
            step = steps[i]
            for j in range(2):
                step["far"][j].wait_recv()
                step["twin"][2 + j].start()

    for i in range(ahead):
        begin(i)
    for t in range(count + 2):
        first(t)
        begin(t + ahead)
        second(t - 1)
        third(t - 2)
    for step in steps:
        for copy in step["line"] + step.get("more", []) + [step["near"]] + step["far"]:
            copy.wait_send()
        for copy in step["twin"]:
            copy.wait()


def gather_special(packs):
    plan = GATHER_PLAN
    _, rows, lanes = packs.shape
    dma = pltpu.SemaphoreType.DMA
    anywhere = pl.BlockSpec(memory_space=pl.ANY)
    out = pl.pallas_call(
        lambda *refs: gather_kernel(plan, 2, *refs),
        out_shape=jax.ShapeDtypeStruct((PACKS, 2, 4, 2, 2, rows, lanes), packs.dtype),
        in_specs=[anywhere],
        out_specs=anywhere,
        scratch_shapes=[dma((len(plan),)), dma((len(plan), 13)), dma((len(plan), 13))],
        compiler_params=pltpu.CompilerParams(collective_id=1, has_side_effects=True),
        name="gather_weights",
    )(packs)
    return out.reshape(PACKS, 2, 16 * rows, lanes)


def scatter_kernel(plan, ahead, *refs):
    grad_ref, gain_ref, out_ref, gain_out_ref = refs[:4]
    own, from_twin, from_far, from_near, from_line, result, gains = refs[4:11]
    copied, stored, sent, came, gain_sent, gain_came = refs[11:]
    at = Place()
    at.greet()
    x, y, z, c = at.x, at.y, at.z, at.c
    mine = [(at.xb, at.yb), (1 - x, 1 - y), (at.xa, at.ya), (x, y)]
    theirs = [(at.xa, at.ya), (1 - x, 1 - y), (at.xb, at.yb), (x, y)]
    steps = []
    for i, (pack, lane, lanes) in enumerate(plan):
        cols = pl.ds(lane, lanes)

        def line(place, core):
            return grad_ref.at[pack, place[0], :, place[1], core, :, cols]

        def send(src, dst, slot, device):
            return remote(src, dst, sent.at[i, slot], came.at[i, slot], device)

        steps.append(
            {
                "twin": [send(line(theirs[j], 1 - c), from_twin.at[i, j], j, at.twin) for j in range(4)],
                "load": [
                    pltpu.make_async_copy(line(mine[j], c), own.at[i, j], copied.at[i, j]) for j in range(4)
                ],
                "far": [send(own.at[i, j], from_far.at[i, j], 4 + j, at.far) for j in range(2)],
                "near": send(own.at[i, 2], from_near.at[i], 6, at.near),
                "line": [
                    send(own.at[i, 3, at.others[k]], from_line.at[i, k], 7 + k, at.line[k]) for k in range(3)
                ],
                "store": pltpu.make_async_copy(result.at[i % 2], out_ref.at[pack, :, cols], stored.at[i]),
            }
        )
    count = len(steps)

    def add(total, terms):
        def body(q, carry):
            value = total[q].astype(f32)
            for term in terms:
                value = value + term[q].astype(f32)
            total[q] = value.astype(bf16)
            return carry

        lax.fori_loop(0, 4, body, 0)

    def begin(i):
        if 0 <= i < count:
            for j in (1, 0, 2, 3):
                steps[i]["twin"][j].start()
                steps[i]["load"][j].start()

    def first(i):
        if 0 <= i < count:
            step = steps[i]
            for j in (1, 0):
                step["twin"][j].wait_recv()
                step["load"][j].wait()
                add(own.at[i, j], [from_twin.at[i, j]])
                step["far"][j].start()

    def second(i):
        if 0 <= i < count:
            step = steps[i]
            step["twin"][2].wait_recv()
            step["load"][2].wait()
            step["far"][1].wait_recv()
            add(own.at[i, 2], [from_twin.at[i, 2], from_far.at[i, 1]])
            step["near"].start()

    def third(i):
        if 0 <= i < count:
            step = steps[i]
            step["twin"][3].wait_recv()
            step["load"][3].wait()
            step["far"][0].wait_recv()
            step["near"].wait_recv()

            def total(q):
                value = own[i, 3, q].astype(f32) + from_twin[i, 3, q].astype(f32)
                return value + from_far[i, 0, q].astype(f32) + from_near[i, q].astype(f32)

            for k in range(3):
                own[i, 3, at.others[k]] = total(at.others[k]).astype(bf16)
                step["line"][k].start()
            if i >= 2:
                steps[i - 2]["store"].wait()
            result[i % 2] = total(z)

    def fourth(i):
        if 0 <= i < count:
            step = steps[i]
            value = result[i % 2]
            for k in range(3):
                step["line"][k].wait_recv()
                value = value + from_line[i, k].astype(f32)
            result[i % 2] = value
            step["store"].start()

    for i in range(ahead):
        begin(i)
    gains[0] = gain_ref[...]
    exchanges = [
        remote(gains.at[2 * k], gains.at[2 * k + 1], gain_sent.at[k], gain_came.at[k], peer)
        for k, peer in enumerate([at.twin, at.near, at.far])
    ]
    everyone = [
        remote(gains.at[6 + z], gains.at[6 + z], gain_sent.at[3 + k], gain_came.at[3 + k], at.line[k])
        for k in range(3)
    ]
    for t in range(count + 3):
        first(t)
        begin(t + ahead)
        second(t - 1)
        third(t - 2)
        fourth(t - 3)
        if 2 <= t < 5:
            exchanges[t - 2].wait()
            spot = 6 + z if t == 4 else 2 * (t - 1)
            gains[spot] = gains[2 * (t - 2)] + gains[2 * (t - 2) + 1]
        if 1 <= t < 4:
            exchanges[t - 1].start()
        if t == 4:
            for copy in everyone:
                copy.start()
        if t == 5:
            for copy in everyone:
                copy.wait()
            gain_out_ref[...] = gains[6] + gains[7] + gains[8] + gains[9]
    for i, step in enumerate(steps):
        for copy in step["twin"] + step["far"] + [step["near"]] + step["line"]:
            copy.wait_send()
        if i >= count - 2:
            step["store"].wait()


def scatter_special(grads, gains):
    plan = SCATTER_PLAN
    count, lanes = len(plan), plan[0][2]
    rows, width = grads.shape[5:]
    dma, vmem = pltpu.SemaphoreType.DMA, pltpu.VMEM
    anywhere = pl.BlockSpec(memory_space=pl.ANY)
    near = pl.BlockSpec(memory_space=pltpu.VMEM)
    return pl.pallas_call(
        lambda *refs: scatter_kernel(plan, 2, *refs),
        out_shape=(
            jax.ShapeDtypeStruct((PACKS, rows, width), f32),
            jax.ShapeDtypeStruct(gains.shape, f32),
        ),
        in_specs=[anywhere, near],
        out_specs=(anywhere, near),
        scratch_shapes=[
            vmem((count, 4, 4, rows, lanes), bf16),
            vmem((count, 4, 4, rows, lanes), bf16),
            vmem((count, 2, 4, rows, lanes), bf16),
            vmem((count, 4, rows, lanes), bf16),
            vmem((count, 3, rows, lanes), bf16),
            vmem((2, rows, lanes), f32),
            vmem((10,) + gains.shape, f32),
            dma((count, 4)),
            dma((count,)),
            dma((count, 10)),
            dma((count, 10)),
            dma((6,)),
            dma((6,)),
        ],
        compiler_params=pltpu.CompilerParams(
            collective_id=2, has_side_effects=True, vmem_limit_bytes=VMEM_BYTES
        ),
        name="scatter_gradients",
    )(grads, gains)


def gather_packs(weights):
    if (lax.axis_size("row"), lax.axis_size("col")) != (16, 2):
        return gather_any(weights)
    query, key, value, out, gate, up, down = weights
    mix = jnp.concatenate([key, value, query, out.T], axis=1)
    full = gather_special(jnp.stack([mix, gate, up, down.T]))
    return [full[p] for p in range(PACKS)]


def scatter_packs(grads, gains):
    if (lax.axis_size("row"), lax.axis_size("col")) != (16, 2):
        return scatter_any(grads, gains)
    _, depth, lanes = grads[0].shape
    stacked = jnp.stack(grads).reshape(PACKS, 2, 4, 2, 2, depth // 16, lanes)
    sums, gain_sums = scatter_special(stacked, gains.reshape(-1, LANES))
    kv = lanes // 8
    first = sums[0]
    return (
        gain_sums.reshape(gains.shape),
        (
            first[:, 2 * kv : 5 * kv],
            first[:, :kv],
            first[:, kv : 2 * kv],
            first[:, 5 * kv :].T,
            sums[1],
            sums[2],
            sums[3].T,
        ),
    )


def lane_of(shape):
    return lax.broadcasted_iota(jnp.int32, shape, len(shape) - 1)


def turn(values, cosine, sine, lower):
    ahead = pltpu.roll(values, LANES - HEAD // 2, 1)
    behind = pltpu.roll(values, HEAD // 2, 1)
    return values * cosine + jnp.where(lower, -ahead, behind) * sine


def turn_back(values, cosine, sine, lower):
    scaled = values * sine
    ahead = pltpu.roll(scaled, LANES - HEAD // 2, 1)
    behind = pltpu.roll(scaled, HEAD // 2, 1)
    return values * cosine - jnp.where(lower, -ahead, behind)


def project_kernel(x_ref, gain_ref, weight_ref, cos_ref, sin_ref, attn_in_ref, y_ref):
    values = x_ref[...].astype(f32)
    inverse = lax.rsqrt(jnp.mean(values * values, axis=1, keepdims=True) + eps)
    attn_in = (values * inverse * gain_ref[...]).astype(bf16)
    attn_in_ref[...] = attn_in
    cosine, sine = cos_ref[...], sin_ref[...]
    lane = lane_of(cosine.shape)
    lower = lane % HEAD < HEAD // 2
    for half in range(2):
        for tile in range(8):
            cols = pl.ds(tile * LANES, LANES)
            raw = dot_nn(attn_in, weight_ref[half, :, cols]).astype(bf16).astype(f32)
            if tile == 0:
                out = turn(raw, cosine, sine, lower)
            elif tile == 1:
                out = jnp.where(lane < HEAD, turn(raw, cosine, sine, lower), raw)
            elif tile == 2:
                out = raw
            else:
                out = turn(raw, cosine, sine, lower) * HEAD ** (-0.5)
            y_ref[half, :, cols] = out.astype(bf16)


def head_rows(values, side, lane):
    return jnp.where((lane < HEAD) if side == 0 else (lane >= HEAD), values, jnp.zeros_like(values))


def twice(tile, side, lane):
    values = tile.astype(f32)
    other = pltpu.roll(values, HEAD, 1)
    keep = (lane < HEAD) if side == 0 else (lane >= HEAD)
    return jnp.where(keep, values, other)


def load_groups(kv_ref, half, dup_ref, flip_ref):
    for slot in range(6):
        tile = kv_ref[half, :, pl.ds((slot // 2) * LANES, LANES)]
        both = twice(tile, slot % 2, lane_of(tile.shape))
        dup_ref[slot] = both.astype(bf16)
        flip_ref[slot] = both.T.astype(bf16)


def seen(first_ref, last_ref, rows, keys):
    index = lax.broadcasted_iota(jnp.int32, (keys, rows.size), 0)
    return (index >= first_ref[:, rows]) & (index <= last_ref[:, rows])


def attend_kernel(block, y_ref, kv_ref, first_ref, last_ref, mix_ref, log_ref, dup_ref, flip_ref):
    keys = kv_ref.shape[1]
    half = pl.program_id(0)
    load_groups(kv_ref, 0, dup_ref, flip_ref)
    lane = lane_of((block, LANES))

    def rows_of(step, carry):
        rows = pl.ds(pl.multiple_of(step * block, block), block)
        allowed = seen(first_ref, last_ref, rows, keys)
        previous = jnp.zeros((block, LANES), f32)
        for head in range(9):
            group = head // 3
            query = head_rows(y_ref[0, rows, pl.ds((3 + head // 2) * LANES, LANES)], head % 2, lane)
            scores = jnp.where(allowed, dot_nt(dup_ref[group], query), neg_fill)
            top = jnp.max(scores, axis=0, keepdims=True)
            powers = jnp.exp(scores - top)
            total = jnp.sum(powers, axis=0, keepdims=True)
            probs = (powers * (1.0 / total)).astype(bf16)
            mixed = dot_nn(flip_ref[3 + group], probs).T
            log_ref[0, pl.ds(head, 1), rows] = top + jnp.log(total)
            if head % 2 == 0:
                tile = jnp.where(lane < HEAD, previous, mixed)
                mix_ref[0, rows, pl.ds((head // 2) * LANES, LANES)] = tile.astype(bf16)
            previous = mixed
        return carry

    lax.fori_loop(0, y_ref.shape[1] // block, rows_of, 0)


def attend_back_kernel(
    block, y_ref, kv_ref, first_ref, last_ref, log_ref, grad_ref, cos_ref, sin_ref, dq_ref, dkv_ref, dup_ref, flip_ref, acc_ref
):
    keys = kv_ref.shape[1]
    load_groups(kv_ref, 0, dup_ref, flip_ref)
    acc_ref[...] = jnp.zeros_like(acc_ref)
    lane = lane_of((block, LANES))
    lower = lane % HEAD < HEAD // 2

    def rows_of(step, carry):
        rows = pl.ds(pl.multiple_of(step * block, block), block)
        allowed = seen(first_ref, last_ref, rows, keys)
        previous = None
        for head in range(9):
            group = head // 3
            query = head_rows(y_ref[0, rows, pl.ds((3 + head // 2) * LANES, LANES)], head % 2, lane)
            upstream = head_rows(grad_ref[0, rows, pl.ds(((head + 1) // 2) * LANES, LANES)], (head + 1) % 2, lane)
            scores = jnp.where(allowed, dot_nt(dup_ref[group], query), neg_fill)
            probs = jnp.exp(scores - log_ref[0, pl.ds(head, 1), rows])
            grad_probs = dot_nt(dup_ref[3 + group], upstream)
            inner = jnp.sum(probs * grad_probs, axis=0, keepdims=True)
            grad_scores = (probs * (grad_probs - inner)).astype(bf16)
            acc_ref[3 + group] += dot_nn(probs.astype(bf16), upstream)
            acc_ref[group] += dot_nn(grad_scores, query)
            grad_query = dot_nn(flip_ref[group], grad_scores).T
            if head % 2 == 1 or head == 8:
                if head == 8:
                    tile = jnp.where(lane < HEAD, grad_query, 0.0)
                else:
                    tile = jnp.where(lane < HEAD, previous, grad_query)
                tile = turn_back(tile * HEAD ** (-0.5), cos_ref[rows, :], sin_ref[rows, :], lower)
                dq_ref[0, rows, pl.ds((head // 2) * LANES, LANES)] = tile.astype(bf16)
            previous = grad_query
        return carry

    lax.fori_loop(0, y_ref.shape[1] // block, rows_of, 0)
    lane_k = lane_of((keys, LANES))
    for tile in range(3):
        low, high = acc_ref[2 * tile], acc_ref[2 * tile + 1]
        low = low + pltpu.roll(low, HEAD, 1)
        high = high + pltpu.roll(high, HEAD, 1)
        dkv_ref[0, :, pl.ds(tile * LANES, LANES)] = jnp.where(lane_k < HEAD, low, high).astype(dkv_ref.dtype)


def full_spec(shape):
    return pl.BlockSpec(shape, lambda i: (0,) * len(shape))


def half_spec(shape):
    return pl.BlockSpec((1,) + shape[1:], lambda i: (i,) + (0,) * (len(shape) - 1))


def params():
    return pltpu.CompilerParams(vmem_limit_bytes=VMEM_BYTES)


def project(layer_input, gain, first_pack, cosine, sine):
    tokens, width = layer_input.shape
    vm = pl.BlockSpec(memory_space=pltpu.VMEM)
    return pl.pallas_call(
        project_kernel,
        grid=(1,),
        out_shape=(
            jax.ShapeDtypeStruct((tokens, width), bf16),
            jax.ShapeDtypeStruct((2, tokens, 8 * LANES), bf16),
        ),
        in_specs=[
            full_spec((tokens, width)),
            full_spec((1, width)),
            full_spec((2, width, 8 * LANES)),
            full_spec((tokens, LANES)),
            full_spec((tokens, LANES)),
        ],
        out_specs=(full_spec((tokens, width)), full_spec((2, tokens, 8 * LANES))),
        compiler_params=params(),
        name="project",
    )(layer_input, gain, first_pack, cosine, sine)


def attend(y, kv, first, last):
    tokens, keys = y.shape[1], kv.shape[1]
    block = min(256, tokens)
    return pl.pallas_call(
        lambda *refs: attend_kernel(block, *refs),
        grid=(2,),
        out_shape=(
            jax.ShapeDtypeStruct((2, tokens, 5 * LANES), bf16),
            jax.ShapeDtypeStruct((2, 16, tokens), f32),
        ),
        in_specs=[half_spec(y.shape), half_spec(kv.shape), full_spec((1, tokens)), full_spec((1, tokens))],
        out_specs=(half_spec((2, tokens, 5 * LANES)), half_spec((2, 16, tokens))),
        scratch_shapes=[pltpu.VMEM((6, keys, LANES), bf16), pltpu.VMEM((6, LANES, keys), bf16)],
        compiler_params=params(),
        name="attend",
    )(y, kv, first, last)


def attend_back(y, kv, first, last, logs, grad, cosine, sine):
    tokens, keys = y.shape[1], kv.shape[1]
    block = min(256, tokens)
    return pl.pallas_call(
        lambda *refs: attend_back_kernel(block, *refs),
        grid=(2,),
        out_shape=(
            jax.ShapeDtypeStruct((2, tokens, 5 * LANES), bf16),
            jax.ShapeDtypeStruct((2, keys, 3 * LANES), f32),
        ),
        in_specs=[
            half_spec(y.shape),
            half_spec(kv.shape),
            full_spec((1, tokens)),
            full_spec((1, tokens)),
            half_spec(logs.shape),
            half_spec(grad.shape),
            full_spec((tokens, LANES)),
            full_spec((tokens, LANES)),
        ],
        out_specs=(half_spec((2, tokens, 5 * LANES)), half_spec((2, keys, 3 * LANES))),
        scratch_shapes=[
            pltpu.VMEM((6, keys, LANES), bf16),
            pltpu.VMEM((6, LANES, keys), bf16),
            pltpu.VMEM((6, keys, LANES), f32),
        ],
        compiler_params=params(),
        name="attend_back",
    )(y, kv, first, last, logs, grad, cosine, sine)


def rope_tables(position):
    lane_index = (jnp.arange(LANES, dtype=jnp.int32) % (HEAD // 2)).astype(f32)
    frequency = jnp.exp(lane_index * (-2.0 * math.log(rope_base) / HEAD))
    angles = position[:, None] * frequency[None, :]
    return jnp.cos(angles), jnp.sin(angles)


def shards(
    layer_input,
    attn_gain,
    mlp_gain,
    query_weight,
    key_weight,
    value_weight,
    out_weight,
    gate_weight,
    up_weight,
    down_weight,
    seq_ids,
    block_ends,
    grad_output,
):
    tokens, width = layer_input.shape
    span = seq_ids.shape[0]
    start = lax.axis_index("col") * tokens
    index = jnp.arange(span, dtype=jnp.int32)
    in_first = seq_ids == seq_ids[0]
    seq_first = jnp.where(in_first, 0, jnp.sum(in_first.astype(jnp.int32)))
    block_last = block_ends - lax.axis_index("row") * span
    own_first = lax.dynamic_slice_in_dim(seq_first, start, tokens)
    own_last = lax.dynamic_slice_in_dim(block_last, start, tokens)
    position = lax.dynamic_slice_in_dim(index - seq_first, start, tokens).astype(f32)
    cosine, sine = rope_tables(position)
    own_first, own_last = own_first[None, :], own_last[None, :]
    gain_one = attn_gain.astype(f32)[None, :]
    gain_two = mlp_gain.astype(f32)[None, :]

    pack_first, pack_gate, pack_up, pack_down = gather_packs(
        (query_weight, key_weight, value_weight, out_weight, gate_weight, up_weight, down_weight)
    )
    attn_in, y = project(layer_input, gain_one, pack_first, cosine, sine)
    kv = lax.all_gather(y[:, :, : 3 * LANES], "col", axis=1, tiled=True)
    mix, logs = attend(y, kv, own_first, own_last)
    pack_out = pack_first[:, :, 7 * LANES :]
    branch = jnp.einsum("htq,hdq->td", mix, pack_out, preferred_element_type=f32)
    own = layer_input.astype(f32)
    residual = own + branch
    inv_two = lax.rsqrt(jnp.mean(residual * residual, axis=1, keepdims=True) + eps)
    normed_two = residual * inv_two
    mlp_in = (normed_two * gain_two).astype(bf16)
    gate_act = jnp.einsum("td,hdf->htf", mlp_in, pack_gate, preferred_element_type=f32)
    up_act = jnp.einsum("td,hdf->htf", mlp_in, pack_up, preferred_element_type=f32)
    hidden = (jax.nn.silu(gate_act) * up_act).astype(bf16)
    layer_output = (
        residual + jnp.einsum("htf,hdf->td", hidden, pack_down, preferred_element_type=f32)
    ).astype(bf16)
    grad_down = jnp.einsum("td,htf->hdf", grad_output, hidden, preferred_element_type=f32).astype(bf16)
    grad_hidden = jnp.einsum("td,hdf->htf", grad_output, pack_down, preferred_element_type=f32)
    sigmoid = jax.nn.sigmoid(gate_act)
    grad_gate_act = (grad_hidden * up_act * sigmoid * (1.0 + gate_act * (1.0 - sigmoid))).astype(bf16)
    grad_up_act = (grad_hidden * gate_act * sigmoid).astype(bf16)
    grad_gate = jnp.einsum("td,htf->hdf", mlp_in, grad_gate_act, preferred_element_type=f32).astype(bf16)
    grad_up = jnp.einsum("td,htf->hdf", mlp_in, grad_up_act, preferred_element_type=f32).astype(bf16)
    grad_mlp_in = jnp.einsum(
        "htf,hdf->td", grad_gate_act, pack_gate, preferred_element_type=f32
    ) + jnp.einsum("htf,hdf->td", grad_up_act, pack_up, preferred_element_type=f32)
    scaled_two = grad_mlp_in * gain_two
    inner_two = jnp.mean(scaled_two * normed_two, axis=1, keepdims=True)
    grad_residual = grad_output.astype(f32) + inv_two * (scaled_two - normed_two * inner_two)
    grad_mlp_gain = jnp.sum(grad_mlp_in * normed_two, axis=0)
    grad_branch = grad_residual.astype(bf16)
    grad_mixture = jnp.einsum("td,hdq->htq", grad_branch, pack_out, preferred_element_type=f32).astype(bf16)
    grad_q, grad_kv = attend_back(y, kv, own_first, own_last, logs, grad_mixture, cosine, sine)
    grad_kv = lax.psum_scatter(grad_kv, "col", scatter_dimension=1, tiled=True)
    key_cos, key_sin = jnp.tile(cosine, (1, 3)), jnp.tile(sine, (1, 3))
    lane = jnp.arange(3 * LANES, dtype=jnp.int32)
    is_key = lane < 3 * HEAD
    scaled = grad_kv * key_sin
    turned = jnp.where(
        lane % HEAD < HEAD // 2, -jnp.roll(scaled, -(HEAD // 2), axis=2), jnp.roll(scaled, HEAD // 2, axis=2)
    )
    grad_kv = jnp.where(is_key, grad_kv * key_cos - turned, grad_kv).astype(bf16)
    grad_y = jnp.concatenate([grad_kv, grad_q], axis=2)
    grad_proj = jnp.einsum("td,htf->hdf", attn_in, grad_y, preferred_element_type=f32)
    grad_out = jnp.einsum("td,htq->hdq", grad_branch, mix, preferred_element_type=f32)
    grad_first = jnp.concatenate(
        [
            grad_proj[:, :, : 7 * LANES],
            grad_proj[:, :, 7 * LANES :] + grad_out[:, :, :LANES],
            grad_out[:, :, LANES:],
        ],
        axis=2,
    ).astype(bf16)
    grad_attn_in = jnp.einsum(
        "htf,hdf->td", grad_y, pack_first[:, :, : 8 * LANES], preferred_element_type=f32
    )
    inv_one = lax.rsqrt(jnp.mean(own * own, axis=1, keepdims=True) + eps)
    normed_one = own * inv_one
    scaled_one = grad_attn_in * gain_one
    inner_one = jnp.mean(scaled_one * normed_one, axis=1, keepdims=True)
    grad_input = (grad_residual + inv_one * (scaled_one - normed_one * inner_one)).astype(bf16)
    grad_attn_gain = jnp.sum(grad_attn_in * normed_one, axis=0)
    gain_sums, weight_sums = scatter_packs(
        (grad_first, grad_gate, grad_up, grad_down), jnp.stack([grad_attn_gain, grad_mlp_gain])
    )
    return (layer_output, grad_input, gain_sums[0], gain_sums[1]) + tuple(weight_sums)


def solution(mesh):
    tokens_spec = P(("row", "col"), None)
    in_specs = (
        tokens_spec,
        P(),
        P(),
        P("row", "col"),
        P("row", "col"),
        P("row", "col"),
        P("col", "row"),
        P("row", "col"),
        P("row", "col"),
        P("col", "row"),
        P("row"),
        P("row"),
        tokens_spec,
    )
    out_specs = (
        tokens_spec,
        tokens_spec,
        P(),
        P(),
        P("row", "col"),
        P("row", "col"),
        P("row", "col"),
        P("col", "row"),
        P("row", "col"),
        P("row", "col"),
        P("col", "row"),
    )
    return jax.shard_map(shards, mesh=mesh, in_specs=in_specs, out_specs=out_specs, check_vma=False)
```

time: 1530 us -> 601 us (0.39)
  waiting for transfers between devices: 949 us -> 31.2 us
  Pallas kernels: 0 us -> 346 us
  blocking collectives: 143 us -> 0 us
  matrix products: 228 us -> 99.9 us
  other arithmetic: 115 us -> 34.2 us
  local copies, waits for them, and re-layouts: 45.7 us -> 66.9 us
  loops' own time: 16.1 us -> 0 us
    reduce_scatter x11 -> x1, waiting for transfers between devices: 547 us -> 0.01 us  [shards(): grad_kv = lax.psum_scatter(grad_kv, 'col', scatter_dimension=1, tiled=True)]
    pallas_call x0 -> x5, Pallas kernels: none -> 346 us  [the longest x1 134 us: scatter_special(): pl.pallas_call(lambda *refs: scatter_kernel(plan, 2, *refs), out_shape=(j...]
    all_gather x9 -> x1, waiting for transfers between devices: 235 us -> 31.1 us  [shards(): kv = lax.all_gather(y[:, :, :3 * LANES], 'col', axis=1, tiled=True)]
    unnamed x24 -> x2, waiting for transfers between devices: 144 us -> 0.03 us
    dot_general x63 -> x14, matrix products: 228 us -> 99.9 us  [the longest x1 18 us: shards(): jnp.einsum('td,hdf->htf', mlp_in, pack_up, preferred_element_type=f32)]
    all_gather x4 -> x0, blocking collectives: 67.3 us -> none  [the longest x1 24.8 us: shards(): lax.all_gather(key_weight, 'row', axis=0, tiled=True)]
    convert_element_type x15 -> x5, other arithmetic: 50.2 us -> 1.04 us  [the longest x1 0.68 us: shards(): jnp.where(is_key, grad_kv * key_cos - turned, grad_kv).astype(bf16)]
    psum x1 -> x0, blocking collectives: 40.1 us -> none  [shards(): gain_sums = lax.psum((grad_attn_gain, grad_mlp_gain), ('row', 'col'))]
  transfers between devices with their start and end apart: 24 -> 2, of which waited for: 21 -> 1; matrix products, arithmetic and copies ran while one was open for 13% -> 9% of each run, Pallas kernels for 0% -> 0%
where the time goes in v1:
time: 601 us; the launch traced here: 593 us
  Pallas kernels  346 us (58%)
  matrix products  99.9 us (17%)
  local copies, waits for them, and re-layouts  66.9 us (11%)
  other arithmetic  34.2 us (6%)
  waiting for transfers between devices  31.2 us (5%)
  between operations  15 us (2%)
    pallas_call x1, Pallas kernels, scatter_special(): pl.pallas_call(lambda *refs: scatter_kernel(plan, 2, *refs), out_shape=(j...  134 us
    pallas_call x1, Pallas kernels, gather_special(): pl.pallas_call(lambda *refs: gather_kernel(plan, 2, *refs), out_shape=jax...  128 us
    pallas_call x1, Pallas kernels, attend_back(): pl.pallas_call(lambda *refs: attend_back_kernel(block, *refs), grid=(2,),...  39.2 us
    pallas_call x1, Pallas kernels, attend(): pl.pallas_call(lambda *refs: attend_kernel(block, *refs), grid=(2,), out_...  35 us
    all_gather x1, waiting for transfers between devices, shards(): kv = lax.all_gather(y[:, :, :3 * LANES], 'col', axis=1, tiled=True)  31.1 us
    another operation x1, other arithmetic, scatter_packs(): stacked = jnp.stack(grads).reshape(PACKS, 2, 4, 2, 2, depth // 16, lanes)  19.5 us
    slice x1, local copies, waits for them, and re-layouts, gather_packs(): return [full[p] for p in range(PACKS)]  19.3 us
    dot_general x1, matrix products, shards(): jnp.einsum('td,hdf->htf', mlp_in, pack_up, preferred_element_type=f32)  18 us
  transfers between devices with their start and end apart: 2, of which 1 were waited for; matrix products, arithmetic and copies ran while one was open for 9% of the time, Pallas kernels for 0%

profile of v1, /device:TPU:0, one launch (start us, length us, event | category | flops | bytes accessed | tf_op | source)
XLA Modules:
  0.0 593.5 jit_solution(11633975165902406865)
XLA Ops:
  9.6 2.2 pad_maximum_fusion.4.refs_0_
  11.8 128.0 %gather_weights.1 = bf16[4,2,4,2,2,72,1536]{6,5,4,3,2,1,0:T(8,128)(2,1)} custom-call(bf16[4,72,1536]{2,1,0:T(8,128)(2,1)} %pad_maximum_fusion.4.refs_0_), custom_call_target="tpu_custom_call" | custom-call | tf_op jit(solution)/shard_map/gather_weights/pallas_call | solution.py:211
  139.9 19.3 %fusion.60 = (bf16[1,2,4,2,2,72,1536]{6,5,4,3,2,1,0:T(8,128)(2,1)}, bf16[1,2,4,2,2,72,1536]{6,5,4,3,2,1,0:T(8,128)(2,1)}, bf16[1,2,4,2,2,72,1536]{6,5,4,3,2,1,0:T(8,128)(2,1)}, bf16[1,2,4,2,2,72,1536]{6,5,4,3,2,1,0:T(8,128)(2,1)}) fusion(bf16[4,2,4,2,2,72,1536]{6,5,4,3,2,1,0:T(8,128)(2,1)} %gather_weights.1), kind=kLoop, calls=%fused_computation.109 | loop fusion | bytes 56623104 | tf_op jit(solution)/shard_map/slice | solution.py:401
  163.5 9.7 %project.1 = (bf16[512,1152]{1,0:T(8,128)(2,1)}, bf16[2,512,1024]{2,1,0:T(8,128)(2,1)}) custom-call(bf16[512,1152]{1,0:T(8,128)(2,1)} %x_ref.1, f32[1,1152]{1,0:T(1,128)} %broadcast_in_dim.31.gain_ref, bf16[2,1152,1536]{2,1,0:T(8,128)(2,1)} %bitcast.147, f32[512,128]{1,0:T(8,128)} %get-tuple-element.55.cos_ref.refs_6_, ...), custom_call_target="tpu_custom_call" | custom-call | tf_op jit(solution)/shard_map/project/pallas_call | solution.py:578
  177.0 31.1 %all-gather.2.cloned.1.call-done.refs_1_ = bf16[2,1024,384]{2,1,0:T(8,128)(2,1)} async-done(((bf16[2,512,384]{2,1,0:T(8,128)(2,1)}), bf16[2,1024,384]{2,1,0:T(8,128)(2,1)}) %all-gather.2.cloned.1.call-update) | async-done | bytes 1572880 | tf_op jit(solution)/shard_map/all_gather | solution.py:688
  208.1 35.0 %attend.1 = (bf16[2,512,640]{2,1,0:T(8,128)(2,1)}, f32[2,16,512]{2,1,0:T(8,128)}) custom-call(bf16[2,512,1024]{2,1,0:T(8,128)(2,1)} %get-tuple-element.19.refs_0_, bf16[2,1024,384]{2,1,0:T(8,128)(2,1)} %all-gather.2.cloned.1.call-done.refs_1_, s32[1,512]{1,0:T(1,128)} %bitcast.178, s32[1,512]{1,0:T(1,128)} %bitcast.180), custom_call_target="tpu_custom_call" | custom-call | tf_op jit(solution)/shard_map/attend/pallas_call | solution.py:601
  243.1 4.4 multiply_reduce_fusion.2
  247.9 6.3 %fusion.64 = f32[2,1536,512]{2,1,0:T(8,128)} fusion(bf16[2,1152,1536]{2,1,0:T(8,128)(2,1)S(1)} %bitcast.166, bf16[512,1152,1]{1,0,2:T(8,128)(2,1)S(1)} %fusion.41), kind=kOutput, calls=%fused_computation.113 | convolution fusion | flops 3623878656 | bytes 14548992 | tf_op jit(solution)/shard_map/td,hdf->htf/dot_general | solution.py:697
  254.2 18.0 %fusion.65 = f32[2,1536,512]{2,1,0:T(8,128)} fusion(bf16[2,1152,1536]{2,1,0:T(8,128)(2,1)S(1)} %bitcast.161, bf16[512,1152,1]{1,0,2:T(8,128)(2,1)S(1)} %fusion.41), kind=kOutput, calls=%fused_computation.114 | convolution fusion | flops 3623878656 | bytes 14548992 | tf_op jit(solution)/shard_map/td,hdf->htf/dot_general | solution.py:698
  272.2 11.6 %fusion.4 = (bf16[2,512,1536]{1,2,0:T(8,128)(2,1)}, bf16[2,512,1536]{1,2,0:T(8,128)(2,1)}, bf16[2,512,1536]{1,2,0:T(8,128)(2,1)}) fusion(f32[2,1536,512]{2,1,0:T(8,128)} %fusion.64, f32[2,1536,512]{2,1,0:T(8,128)} %fusion.65, bf16[2,1152,1536]{2,1,0:T(8,128)(2,1)S(1)} %bitcast.155, bf16[512,1152]{1,0:T(8,128)(2,1)S(1)} %copy-done.7), kind=kOutput, calls=%fused_computation.12 | convolution fusion | flops 3649044480 | bytes 30277632 | tf_op jit(solution)/shard_map/td,hdf->htf/dot_general | solution.py:704
  283.8 8.4 %convolution_bitcast_fusion.4 = f32[512,1152]{1,0:T(8,128)S(1)} fusion(bf16[2,512,1536]{1,2,0:T(8,128)(2,1)} %get-tuple-element.38, bf16[2,1152,1536]{2,1,0:T(8,128)(2,1)} %bitcast.163), kind=kOutput, calls=%fused_computation.33 | convolution fusion | flops 3623878656 | bytes 12582912 | tf_op jit(solution)/shard_map/htf,hdf->td/dot_general | solution.py:710
  292.2 5.5 multiply_reduce_fusion
  298.4 4.8 fusion.38.refs_5_
  303.2 39.2 %attend_back.1 = (bf16[2,512,640]{2,1,0:T(8,128)(2,1)}, f32[2,1024,384]{2,1,0:T(8,128)}) custom-call(bf16[2,512,1024]{2,1,0:T(8,128)(2,1)} %get-tuple-element.19.refs_0_, bf16[2,1024,384]{2,1,0:T(8,128)(2,1)} %all-gather.2.cloned.1.call-done.refs_1_, s32[1,512]{1,0:T(1,128)} %bitcast.179, s32[1,512]{1,0:T(1,128)} %bitcast.181, ...), custom_call_target="tpu_custom_call" | custom-call | tf_op jit(solution)/shard_map/attend_back/pallas_call | solution.py:619
  348.6 2.5 copy.54
  353.0 2.3 copy.52
  356.8 3.2 convolution_bitcast_fusion.1
  360.0 2.5 copy-done
  364.2 4.3 copy.59
  369.2 9.1 %convolution_convert_fusion.1 = bf16[2,1536,1152]{1,2,0:T(8,128)(2,1)} fusion(bf16[2,512,1536]{1,2,0:T(8,128)(2,1)} %get-tuple-element.37, bf16[512,1152,1]{1,0,2:T(8,128)(2,1)} %copy-done.10), kind=kOutput, calls=%fused_computation.2 | convolution fusion | flops 3627417600 | bytes 11403264 | tf_op jit(solution)/shard_map/td,htf->hdf/dot_general | solution.py:709
  378.3 6.1 %convolution_convert_fusion.2 = bf16[2,1536,1152]{1,2,0:T(8,128)(2,1)} fusion(bf16[2,512,1536]{1,2,0:T(8,128)(2,1)S(1)} %copy-done.30, bf16[512,1152,1]{1,0,2:T(8,128)(2,1)S(1)} %copy-done.11), kind=kOutput, calls=%fused_computation.3 | convolution fusion | flops 3627417600 | bytes 11403264 | tf_op jit(solution)/shard_map/td,htf->hdf/dot_general | solution.py:708
  384.3 6.3 %convolution_convert_fusion = bf16[2,1536,1152]{1,2,0:T(8,128)(2,1)} fusion(bf16[2,512,1536]{1,2,0:T(8,128)(2,1)S(1)} %copy-done.29, bf16[512,1152]{1,0:T(8,128)(2,1)S(1)} %copy-done.9), kind=kOutput, calls=%fused_computation.1 | convolution fusion | flops 3627417600 | bytes 11403264 | tf_op jit(solution)/shard_map/td,htf->hdf/dot_general | solution.py:703
  390.7 5.3 fusion.20
  401.3 2.9 convolution_bitcast_fusion
  404.2 2.3 fusion.42
  406.5 2.4 slice.155
  408.9 2.1 copy.58
  411.0 6.4 %copy.56 = bf16[2,1152,896]{2,1,0:T(8,128)(2,1)} copy(bf16[2,1152,896]{1,2,0:T(8,128)(2,1)} %slice.155) | data formatting | bytes 8257536 | tf_op jit(solution)/shard_map/slice | solution.py:734
  417.4 8.1 %fusion.29 = (f32[1152]{0:T(1024)S(1)}, f32[512]{0:T(512)}, f32[512,1152]{1,0:T(8,128)}) fusion(bf16[512,1152]{1,0:T(8,128)(2,1)S(1)} %copy-done.1, f32[512]{0:T(512)S(1)} %copy-done.19, f32[1152]{0:T(1024)S(1)} %convert_element_type.82, bf16[2,1152,1536]{2,1,0:T(8,128)(2,1)} %bitcast.150, bf16[2,512,640]{2,1,0:T(8,128)(2,1)} %get-tuple-element.23, ...), kind=kOutput, calls=%fused_computation.48 | convolution fusion | flops 2424240640 | bytes 10368000 | tf_op jit(solution)/shard_map/htf,hdf->td/dot_general | solution.py:740
  426.2 19.5 %pad_maximum_fusion.refs_0_ = bf16[4,2,4,2,2,72,1536]{6,5,4,3,2,1,0:T(8,128)(2,1)} fusion(bf16[1,2,4,2,2,72,1536]{6,5,4,3,2,1,0:T(8,128)(2,1)} %bitcast.169, bf16[1,2,4,2,2,72,1536]{6,5,4,3,2,1,0:T(8,128)(2,1)} %bitcast.167, bf16[1,2,4,2,2,72,1536]{6,5,4,3,2,1,0:T(8,128)(2,1)} %bitcast.168, bf16[1,2,4,2,2,72,512]{6,5,4,3,2,1,0:T(8,128)(2,1)} %bitcast.152, ...), kind=kLoop, calls=%fused_computation | loop fusion | flops 169869312 | bytes 56623104 | tf_op jit(solution)/shard_map/stack | solution.py:408
  445.7 134.0 %scatter_gradients.1 = (f32[4,72,1536]{2,1,0:T(8,128)}, f32[18,128]{1,0:T(8,128)}) custom-call(bf16[4,2,4,2,2,72,1536]{6,5,4,3,2,1,0:T(8,128)(2,1)} %pad_maximum_fusion.refs_0_, f32[18,128]{1,0:T(8,128)} %reshape.196.refs_1_), custom_call_target="tpu_custom_call" | custom-call | tf_op jit(solution)/shard_map/scatter_gradients/pallas_call | solution.py:365
  579.8 2.6 slice_bitcast_fusion
  (125 shorter events, 33.1 us)
Async XLA Ops:
  7.2 200.9 %all-gather.2.cloned.1.call-start = ((), (), s32[]{:S(2)}) async-start(), calls=%async_computation.1 | async-start | bytes 2359296 | tf_op jit(solution)/shard_map/all_gather | solution.py:688
  139.9 19.3 %copy-start.21 = (s32[1024]{0:T(1024)S(1)}, s32[1024]{0:T(1024)}, u32[]{:S(2)}) copy-start(s32[1024]{0:T(1024)} %param.23) | copy-start | bytes 12292
  173.2 3.8 copy-start.20
  175.3 67.8 %copy-start.1 = (bf16[512,1152]{1,0:T(8,128)(2,1)S(1)}, bf16[512,1152]{1,0:T(8,128)(2,1)}, u32[]{:S(2)}) copy-start(bf16[512,1152]{1,0:T(8,128)(2,1)} %x_ref.1) | copy-start | bytes 3538948
  175.3 220.6 %reduce-scatter.2.cloned.1.call-start = ((), (), s32[]{:S(2)}) async-start(), calls=%async_computation.2 | async-start | bytes 4718592 | tf_op jit(solution)/shard_map/reduce_scatter | solution.py:720
  243.1 4.7 slice-start.6
  243.1 4.7 slice-start.7
  247.5 50.2 %copy-start.2 = (f32[512,1152]{1,0:T(8,128)}, f32[512,1152]{1,0:T(8,128)S(1)}, u32[]{:S(2)}) copy-start(f32[512,1152]{1,0:T(8,128)S(1)} %get-tuple-element.59) | copy-start | bytes 7077892
  247.5 6.7 %slice-start.4 = ((s8[7077888]{0:T(1024)(128)(4,1)}), s8[4194304]{0:T(1024)(128)(4,1)S(1)}, s32[]{:S(2)}) async-start(s8[7077888]{0:T(1024)(128)(4,1)} %bitcast.159), calls=%async_computation.7 | async-start | bytes 8388608
  247.8 6.4 %copy-start.10 = (bf16[512,1152,1]{1,0,2:T(8,128)(2,1)}, bf16[512,1152,1]{1,0,2:T(8,128)(2,1)S(1)}, u32[]{:S(2)}) copy-start(bf16[512,1152,1]{1,0,2:T(8,128)(2,1)S(1)} %fusion.41) | copy-start | bytes 3538948
  247.9 6.3 %slice-start.5 = ((s8[7077888]{0:T(1024)(128)(4,1)}), s8[2883584]{0:T(1024)(128)(4,1)S(1)}, s32[]{:S(2)}) async-start(s8[7077888]{0:T(1024)(128)(4,1)} %bitcast.159), calls=%async_computation.8 | async-start | bytes 5767168
  247.9 24.4 %slice-start = ((s8[7077888]{0:T(1024)(128)(4,1)}), s8[4194304]{0:T(1024)(128)(4,1)S(1)}, s32[]{:S(2)}) async-start(s8[7077888]{0:T(1024)(128)(4,1)} %bitcast.153), calls=%async_computation.3 | async-start | bytes 8388608
  254.2 18.0 %slice-start.1 = ((s8[7077888]{0:T(1024)(128)(4,1)}), s8[2883584]{0:T(1024)(128)(4,1)S(1)}, s32[]{:S(2)}) async-start(s8[7077888]{0:T(1024)(128)(4,1)} %bitcast.153), calls=%async_computation.4 | async-start | bytes 5767168
  254.2 18.0 %copy-start.7 = (bf16[512,1152]{1,0:T(8,128)(2,1)S(1)}, bf16[512,1152]{1,0:T(8,128)(2,1)}, u32[]{:S(2)}) copy-start(bf16[512,1152]{1,0:T(8,128)(2,1)} %param.25) | copy-start | bytes 3538948
  283.8 8.4 %copy-start.28 = (bf16[2,512,1536]{1,2,0:T(8,128)(2,1)S(1)}, bf16[2,512,1536]{1,2,0:T(8,128)(2,1)}, u32[]{:S(2)}) copy-start(bf16[2,512,1536]{1,2,0:T(8,128)(2,1)} %get-tuple-element.37) | copy-start | bytes 9437188
  292.2 5.5 copy-start.8
  343.1 74.3 %copy-start.13 = (f32[1152]{0:T(1024)}, f32[1152]{0:T(1024)S(1)}, u32[]{:S(2)}) copy-start(f32[1152]{0:T(1024)S(1)} %convert_element_type.82) | copy-start | bytes 13828
  364.2 4.3 copy-start.18
  369.2 9.1 %copy-start.11 = (bf16[512,1152,1]{1,0,2:T(8,128)(2,1)S(1)}, bf16[512,1152,1]{1,0,2:T(8,128)(2,1)}, u32[]{:S(2)}) copy-start(bf16[512,1152,1]{1,0,2:T(8,128)(2,1)} %copy-done.10) | copy-start | bytes 3538948
  369.2 9.1 %copy-start.30 = (bf16[2,512,1536]{1,2,0:T(8,128)(2,1)S(1)}, bf16[2,512,1536]{1,2,0:T(8,128)(2,1)}, u32[]{:S(2)}) copy-start(bf16[2,512,1536]{1,2,0:T(8,128)(2,1)} %get-tuple-element.38) | copy-start | bytes 9437188
  378.2 6.1 %copy-start.9 = (bf16[512,1152]{1,0:T(8,128)(2,1)S(1)}, bf16[512,1152]{1,0:T(8,128)(2,1)}, u32[]{:S(2)}) copy-start(bf16[512,1152]{1,0:T(8,128)(2,1)} %param.25) | copy-start | bytes 3538948
  378.2 6.1 %copy-start.29 = (bf16[2,512,1536]{1,2,0:T(8,128)(2,1)S(1)}, bf16[2,512,1536]{1,2,0:T(8,128)(2,1)}, u32[]{:S(2)}) copy-start(bf16[2,512,1536]{1,2,0:T(8,128)(2,1)} %get-tuple-element.39) | copy-start | bytes 9437188
  378.3 12.4 %slice-start.2 = ((s8[7077888]{0:T(1024)(128)(4,1)}), s8[4194304]{0:T(1024)(128)(4,1)S(1)}, s32[]{:S(2)}) async-start(s8[7077888]{0:T(1024)(128)(4,1)} %bitcast.156), calls=%async_computation.5 | async-start | bytes 8388608
  384.3 6.3 %slice-start.3 = ((s8[7077888]{0:T(1024)(128)(4,1)}), s8[2883584]{0:T(1024)(128)(4,1)S(1)}, s32[]{:S(2)}) async-start(s8[7077888]{0:T(1024)(128)(4,1)} %bitcast.156), calls=%async_computation.6 | async-start | bytes 5767168
  384.3 6.3 %copy-start.3 = (f32[512,1152]{1,0:T(8,128)S(1)}, f32[512,1152]{1,0:T(8,128)}, u32[]{:S(2)}) copy-start(f32[512,1152]{1,0:T(8,128)} %copy-done.2) | copy-start | bytes 7077892
  400.2 4.0 copy-start.12
  411.0 6.4 %copy-start.19 = (f32[512]{0:T(512)S(1)}, f32[512]{0:T(512)}, u32[]{:S(2)}) copy-start(f32[512]{0:T(512)} %add_rsqrt_fusion) | copy-start | bytes 6148
  417.4 8.1 %copy-start.16 = (f32[1,1152]{1,0:T(1,128)S(1)}, f32[1,1152]{1,0:T(1,128)}, u32[]{:S(2)}) copy-start(f32[1,1152]{1,0:T(1,128)} %stack.47) | copy-start | bytes 13828
  579.7 4.2 copy-start.23
  579.7 4.2 copy-start.15
  579.8 4.8 copy-start.6
  579.8 4.8 copy-start.14
  (9 other events, 15.6 us)
Sparse Core Ops, SparseCore 0:
  175.5 32.6 all-gather.1
  342.6 43.3 reduce-scatter.1

commit v2 on v1

v2 whole, which is shorter than its diff:
```python
import math

import jax
import jax.numpy as jnp
from jax import lax
from jax.experimental import pallas as pl
from jax.experimental.pallas import tpu as pltpu
from jax.sharding import PartitionSpec as P

HEAD = 64
LANES = 128
eps = 1e-05
rope_base = 10000.0
neg_fill = -1e30
f32 = jnp.float32
bf16 = jnp.bfloat16
VMEM_BYTES = 62 * 1024 * 1024


def dot_nn(a, b):
    return lax.dot_general(a, b, (((1,), (0,)), ((), ())), preferred_element_type=f32)


def dot_nt(a, b):
    return lax.dot_general(a, b, (((1,), (1,)), ((), ())), preferred_element_type=f32)


def halves(values):
    rows, cols = values.shape
    return jnp.transpose(values.reshape(rows, 2, cols // 2), (1, 0, 2))


def whole(values):
    two, rows, cols = values.shape
    return jnp.transpose(values, (1, 0, 2)).reshape(rows, two * cols)


def gather_any(weights):
    query, key, value, out, gate, up, down = weights

    def both(weight, row_axis):
        part = lax.all_gather(weight, "row", axis=row_axis, tiled=True)
        return lax.all_gather(part, "col", axis=1 - row_axis, tiled=True)

    mix = [halves(both(key, 0)), halves(both(value, 0)), halves(both(query, 0)), halves(both(out, 1).T)]
    return [
        jnp.concatenate(mix, axis=2),
        halves(both(gate, 0)),
        halves(both(up, 0)),
        halves(both(down, 1).T),
    ]


def scatter_any(grads, gains):
    first, gate, up, down = [grad.astype(f32) for grad in grads]
    kv = first.shape[2] // 8
    key, value, query, out = (
        whole(first[:, :, :kv]),
        whole(first[:, :, kv : 2 * kv]),
        whole(first[:, :, 2 * kv : 5 * kv]),
        whole(first[:, :, 5 * kv :]).T,
    )

    def both(grad, row_axis):
        part = lax.psum_scatter(grad, "row", scatter_dimension=row_axis, tiled=True)
        return lax.psum_scatter(part, "col", scatter_dimension=1 - row_axis, tiled=True)

    return (
        lax.psum(gains, ("row", "col")),
        (
            both(query, 0),
            both(key, 0),
            both(value, 0),
            both(out, 1),
            both(whole(gate), 0),
            both(whole(up), 0),
            both(whole(down).T, 1),
        ),
    )


PACKS = 4
MESH = pl.DeviceIdType.MESH


class Place:
    def __init__(self):
        row, x = lax.axis_index("row"), lax.axis_index("col")
        z, y, c = row // 4, (row // 2) % 2, row % 2
        self.x, self.z, self.y, self.c = x, z, y, c
        self.xa, self.ya = jnp.where(c == 0, 1 - x, x), jnp.where(c == 0, y, 1 - y)
        self.xb, self.yb = jnp.where(c == 0, x, 1 - x), jnp.where(c == 0, 1 - y, y)
        self.others = [(z + k) % 4 for k in (1, 2, 3)]
        self.line = [self.device(x, other, y, c) for other in self.others]
        self.near = self.device(self.xa, z, self.ya, c)
        self.far = self.device(self.xb, z, self.yb, c)
        self.twin = self.device(x, z, y, 1 - c)
        self.cross = self.device(1 - x, z, y, c)

    @staticmethod
    def device(x, z, y, c):
        return ((z * 2 + y) * 2 + c, x)

    def greet(self):
        barrier = pltpu.get_barrier_semaphore()
        for peer in self.line + [self.near, self.far, self.twin]:
            pl.semaphore_signal(barrier, inc=1, device_id=peer, device_id_type=MESH)
        pl.semaphore_wait(barrier, 6)


def remote(src, dst, send, recv, device):
    return pltpu.make_async_remote_copy(
        src_ref=src, dst_ref=dst, send_sem=send, recv_sem=recv, device_id=device, device_id_type=MESH
    )


GATHER_PLAN = [
    (0, 0, 512, 0),
    (0, 512, 512, 0),
    (0, 1024, 512, 0),
    (1, 0, 768, 1),
    (2, 0, 768, 0),
    (1, 768, 768, 0),
    (2, 768, 768, 0),
    (3, 0, 768, 1),
    (3, 768, 768, 0),
]
SCATTER_PLAN = [(3, 0), (1, 0), (2, 0), (3, 1), (1, 1), (2, 1), (0, 0), (0, 1)]
RING = 6


class Gather:
    def __init__(self, at, plan, own_refs, out_refs, copied, sent, came):
        x, y, z = at.x, at.y, at.z
        size = own_refs[0].shape[0]
        rows = pl.ds(pl.multiple_of(at.c * size, 8), size)
        self.steps = []
        for i, (pack, lane, lanes, kind) in enumerate(plan):
            cols = pl.ds(lane, lanes)
            own = own_refs[pack].at[:, cols]

            def one(xx, yy):
                return out_refs[pack].at[xx, z, yy, rows, cols]

            def line(xx, yy, slot, device):
                ref = out_refs[pack].at[xx, :, yy, rows, cols]
                return remote(ref, ref, sent.at[i, slot], came.at[i, slot], device)

            step = {"kind": kind, "keep": pltpu.make_async_copy(own, one(x, y), copied.at[i])}
            step["line"] = [remote(own, one(x, y), sent.at[i, k], came.at[i, k], at.line[k]) for k in range(3)]
            if kind == 0:
                step["near"] = line(x, y, 3, at.near)
            else:
                step["near"] = remote(own, one(x, y), sent.at[i, 3], came.at[i, 3], at.near)
                step["more"] = [
                    remote(one(at.xa, at.ya), one(at.xa, at.ya), sent.at[i, 4 + k], came.at[i, 4 + k], at.line[k])
                    for k in range(3)
                ]
            step["far"] = [line(x, y, 7, at.far), line(at.xa, at.ya, 8, at.far)]
            step["twin"] = [
                line(xx, yy, 9 + j, at.twin)
                for j, (xx, yy) in enumerate([(x, y), (at.xa, at.ya), (at.xb, at.yb), (1 - x, 1 - y)])
            ]
            self.steps.append(step)

    def begin(self, i):
        if 0 <= i < len(self.steps):
            self.steps[i]["keep"].start()
            for copy in self.steps[i]["line"]:
                copy.start()
            if self.steps[i]["kind"] == 1:
                self.steps[i]["near"].start()

    def first(self, i):
        if 0 <= i < len(self.steps):
            step = self.steps[i]
            if step["kind"] == 1:
                step["near"].wait_recv()
                for copy in step["more"]:
                    copy.start()
            for copy in step["line"]:
                copy.wait_recv()
            step["keep"].wait()
            if step["kind"] == 0:
                step["near"].start()
            step["far"][0].start()
            step["twin"][0].start()

    def second(self, i):
        if 0 <= i < len(self.steps):
            step = self.steps[i]
            for copy in [step["near"]] if step["kind"] == 0 else step["more"]:
                copy.wait_recv()
            step["far"][1].start()
            step["twin"][1].start()

    def third(self, i):
        if 0 <= i < len(self.steps):
            step = self.steps[i]
            for j in range(2):
                step["far"][j].wait_recv()
                step["twin"][2 + j].start()

    def arrive(self, i):
        for copy in self.steps[i]["twin"]:
            copy.wait_recv()

    def move(self, t):
        self.first(t)
        self.begin(t + 2)
        self.second(t - 1)
        self.third(t - 2)

    def finish(self):
        for step in self.steps:
            for copy in step["line"] + step.get("more", []) + [step["near"]] + step["far"] + step["twin"]:
                copy.wait_send()


def forward_kernel(plan, *refs):
    x_ref, gain_one_ref, gain_two_ref, cos_ref, sin_ref, first_ref, last_ref = refs[:7]
    own_refs, full_refs = refs[7:11], refs[11:15]
    saved = refs[15:25]
    weights, attn_in, y, kv, dup, flip, mix, logs, residual, mlp_in, acts, hidden, output = refs[25:38]
    copied, sent, came, loaded, stored, kv_sent, kv_came = refs[38:]
    at = Place()
    at.greet()
    gather = Gather(at, plan, own_refs, full_refs, copied, sent, came)
    tokens, width = x_ref.shape
    lanes = weights.shape[2]

    def load(pack, cut, slot, k):
        size = lanes // 2
        return [
            pltpu.make_async_copy(
                full_refs[pack].at[half].reshape(width, lanes).at[:, pl.ds(cut * size, size)],
                weights.at[slot, :, pl.ds(half * size, size)],
                loaded.at[k, half],
            )
            for half in range(2)
        ]

    def load_first(half, lane, size, k):
        part = pl.ds(lane, size)
        return pltpu.make_async_copy(
            full_refs[0].at[half].reshape(width, lanes).at[:, part], weights.at[half, :, part], loaded.at[k, half]
        )

    project_loads = [load_first(half, 0, 8 * LANES, 0) for half in range(2)]
    out_loads = [load_first(half, 8 * LANES, lanes - 8 * LANES, 1) for half in range(2)]
    gate_loads = [load(1, 0, 2, 2) + load(2, 0, 3, 3), load(1, 1, 0, 4) + load(2, 1, 1, 5)]
    down_loads = [load(3, 0, 2, 6), load(3, 1, 3, 7)]

    def save(k, ref):
        copy = pltpu.make_async_copy(ref, saved[k], stored.at[k])
        copy.start()
        return copy

    gather.begin(0)
    gather.begin(1)
    values = x_ref[...].astype(f32)
    inverse = lax.rsqrt(jnp.mean(values * values, axis=1, keepdims=True) + eps)
    attn_in[...] = (values * inverse * gain_one_ref[...]).astype(bf16)
    saves = [save(0, attn_in)]
    for t in range(4):
        gather.move(t)
    gather.arrive(0)
    gather.arrive(1)
    start(project_loads)
    mine = pl.ds(pl.multiple_of(at.x * tokens, tokens), tokens)
    for half in range(2):
        project_loads[half].wait()
        project_half(half, attn_in, weights, cos_ref, sin_ref, y)
        kv[half, mine, :] = y[half, :, : 3 * LANES]
        exchange = remote(kv.at[half, mine, :], kv.at[half, mine, :], kv_sent.at[half], kv_came.at[half], at.cross)
        exchange.start()
    saves.append(save(1, y))
    gather.move(4)
    for half in range(2):
        remote(kv.at[half, mine, :], kv.at[half, mine, :], kv_sent.at[half], kv_came.at[half], at.cross).wait()
    saves.append(save(2, kv))
    block = 256
    steps = tokens // block

    def rows_of(i, carry):
        half = i // steps

        @pl.when(i % steps == 0)
        def _():
            load_groups(kv, half, dup, flip)

        attend_rows(half, i % steps, block, y, dup, flip, first_ref, last_ref, mix, logs)
        for k in range(4):

            @pl.when(i == k * steps // 2)
            def _(k=k):
                gather.move(5 + k)

        return carry

    lax.fori_loop(0, 2 * steps, rows_of, 0)
    saves.append(save(3, mix))
    saves.append(save(4, logs))
    gather.arrive(2)
    start(out_loads)
    wait(out_loads)
    span = pl.ds(7 * LANES, 5 * LANES)

    def branch_of(i, carry):
        rows = pl.ds(pl.multiple_of(i * 256, 256), 256)
        total = x_ref[rows, :].astype(f32)
        for half in range(2):
            total = total + dot_nt(mix[half, rows, :], weights[half, :, span])
        residual[rows, :] = total
        inverse = lax.rsqrt(jnp.mean(total * total, axis=1, keepdims=True) + eps)
        mlp_in[rows, :] = (total * inverse * gain_two_ref[...]).astype(bf16)
        return carry

    lax.fori_loop(0, tokens // 256, branch_of, 0)
    saves.append(save(5, residual))
    saves.append(save(6, mlp_in))
    gather.move(9)
    gather.move(10)
    for cut in range(2):
        for i in (3, 4) if cut == 0 else (5, 6):
            gather.arrive(i)
        start(gate_loads[cut])
    size = lanes // 2
    for cut in range(2):
        wait(gate_loads[cut])
        slot = 2 - 2 * cut

        def hidden_of(i, carry):
            half, tile = i // (size // 256), i % (size // 256)
            cols = pl.ds(pl.multiple_of(i * 256, 256), 256)
            into = pl.ds(pl.multiple_of(cut * size + tile * 256, 256), 256)
            gate = dot_nn(mlp_in[...], weights[slot, :, cols])
            up = dot_nn(mlp_in[...], weights[slot + 1, :, cols])
            acts[half, 0, :, into] = gate
            acts[half, 1, :, into] = up
            hidden[half, :, into] = (gate * jax.nn.sigmoid(gate) * up).astype(bf16)
            return carry

        lax.fori_loop(0, lanes // 256, hidden_of, 0)
        if cut == 0:
            gather.arrive(7)
            start(down_loads[0])
    gather.arrive(8)
    start(down_loads[1])
    saves.append(save(7, acts))
    saves.append(save(8, hidden))
    wait(down_loads[0] + down_loads[1])

    def output_of(i, carry):
        rows = pl.ds(pl.multiple_of(i * 256, 256), 256)
        total = residual[rows, :]
        for half in range(2):
            for cut in range(2):
                total = total + dot_nt(
                    hidden[half, rows, pl.ds(cut * size, size)], weights[2 + cut, :, pl.ds(half * size, size)]
                )
        output[rows, :] = total.astype(bf16)
        return carry

    lax.fori_loop(0, tokens // 256, output_of, 0)
    saves.append(save(9, output))
    gather.finish()
    for copy in saves:
        copy.wait()


def forward_special(layer_input, gains, cosine, sine, first, last, packs):
    plan = GATHER_PLAN
    tokens, width = layer_input.shape
    rows, lanes = packs[0].shape
    keys = 2 * tokens
    dma, vmem = pltpu.SemaphoreType.DMA, pltpu.VMEM
    anywhere = pl.BlockSpec(memory_space=pl.ANY)
    near = pl.BlockSpec(memory_space=pltpu.VMEM)
    saved = [
        ((tokens, width), bf16),
        ((2, tokens, 8 * LANES), bf16),
        ((2, keys, 3 * LANES), bf16),
        ((2, tokens, 5 * LANES), bf16),
        ((2, 16, tokens), f32),
        ((tokens, width), f32),
        ((tokens, width), bf16),
        ((2, 2, tokens, lanes), f32),
        ((2, tokens, lanes), bf16),
        ((tokens, width), bf16),
    ]
    full = [((2, 4, 2, 2 * rows, lanes), bf16)] * PACKS
    count = len(plan)
    outs = pl.pallas_call(
        lambda *refs: forward_kernel(plan, *refs),
        out_shape=[jax.ShapeDtypeStruct(*shape) for shape in full + saved],
        in_specs=[near] * 7 + [anywhere] * PACKS,
        out_specs=[anywhere] * (PACKS + len(saved)),
        scratch_shapes=[
            vmem((4, width, lanes), bf16),
            vmem(*saved[0]),
            vmem(*saved[1]),
            vmem(*saved[2]),
            vmem((6, keys, LANES), bf16),
            vmem((6, LANES, keys), bf16),
            vmem(*saved[3]),
            vmem(*saved[4]),
            vmem(*saved[5]),
            vmem(*saved[6]),
            vmem(*saved[7]),
            vmem(*saved[8]),
            vmem(*saved[9]),
            dma((count,)),
            dma((count, 13)),
            dma((count, 13)),
            dma((8, 2)),
            dma((len(saved),)),
            dma((2,)),
            dma((2,)),
        ],
        compiler_params=pltpu.CompilerParams(
            collective_id=1, has_side_effects=True, vmem_limit_bytes=VMEM_BYTES
        ),
        name="forward",
    )(layer_input, gains[0], gains[1], cosine, sine, first, last, *packs)
    return [part.reshape(2, 16 * rows, lanes) for part in outs[:PACKS]], outs[PACKS:]


def start(copies):
    for copy in copies:
        copy.start()


def wait(copies):
    for copy in copies:
        copy.wait()


class Scatter:
    def __init__(self, at, grad_ref, parts, sums, temps, sems, out_ref):
        self.at, self.grad, self.sums, self.temps = at, grad_ref, sums, temps
        self.from_twin, self.from_far, self.from_near, self.from_line = parts
        self.sent, self.came, self.loaded, self.stored = sems
        self.out_ref = out_ref
        x, y = at.x, at.y
        self.mine = [(at.xb, at.yb), (1 - x, 1 - y), (at.xa, at.ya), (x, y)]
        self.theirs = [(at.xa, at.ya), (1 - x, 1 - y), (at.xb, at.yb), (x, y)]
        to_far, to_near, to_line, result = sums
        self.steps = []
        for i, (pack, cut) in enumerate(SCATTER_PLAN):
            lanes = result.shape[2]

            def send(src, dst, slot, device, i=i):
                return remote(src, dst, self.sent.at[i, slot], self.came.at[i, slot], device)

            self.steps.append(
                {
                    "twin": [
                        send(self.line(i, self.theirs[j], 1 - at.c), self.from_twin.at[i, j], j, at.twin)
                        for j in range(4)
                    ],
                    "far": [
                        send(to_far.at[i % RING, j], self.from_far.at[i, j], 4 + j, at.far) for j in range(2)
                    ],
                    "near": send(to_near.at[i % RING], self.from_near.at[i], 6, at.near),
                    "line": [
                        send(to_line.at[i % RING, k], self.from_line.at[i, k], 7 + k, at.line[k])
                        for k in range(3)
                    ],
                    "store": pltpu.make_async_copy(
                        result.at[i % RING], out_ref.at[pack, :, pl.ds(cut * lanes, lanes)], self.stored.at[i]
                    ),
                }
            )

    def line(self, i, place, core):
        size = self.sums[3].shape[1]
        return self.grad.at[i, place[0], :, place[1], pl.ds(pl.multiple_of(core * size, 8), size)]

    def load(self, src, dst, k):
        copy = pltpu.make_async_copy(src, dst, self.loaded.at[k])
        copy.start()
        return copy

    def begin(self, i):
        for j in (1, 0, 2, 3):
            self.steps[i]["twin"][j].start()

    def first(self, i):
        step, to_far, temp, slot = self.steps[i], self.sums[0], self.temps[0], i % RING
        self.free(i, lambda old: old["far"])
        copies = []
        for j in (1, 0):
            own = self.load(self.line(i, self.mine[j], self.at.c), to_far.at[slot, j], 2 * j)
            step["twin"][j].wait_recv()
            copies.append((j, [own, self.load(self.from_twin.at[i, j], temp.at[j], 2 * j + 1)]))
        for j, pair in copies:
            wait(pair)

            def body(q, carry, j=j):
                to_far[slot, j, q] = (to_far[slot, j, q].astype(f32) + temp[j, q].astype(f32)).astype(bf16)
                return carry

            lax.fori_loop(0, 4, body, 0)
            step["far"][j].start()

    def second(self, i):
        step, to_near, temp, slot = self.steps[i], self.sums[1], self.temps[0], i % RING
        self.free(i, lambda old: [old["near"]])
        copies = [self.load(self.line(i, self.mine[2], self.at.c), to_near.at[slot], 4)]
        step["twin"][2].wait_recv()
        copies.append(self.load(self.from_twin.at[i, 2], temp.at[0], 5))
        step["far"][1].wait_recv()
        copies.append(self.load(self.from_far.at[i, 1], temp.at[1], 6))
        wait(copies)

        def body(q, carry):
            value = to_near[slot, q].astype(f32) + temp[0, q].astype(f32) + temp[1, q].astype(f32)
            to_near[slot, q] = value.astype(bf16)
            return carry

        lax.fori_loop(0, 4, body, 0)
        step["near"].start()

    def third(self, i):
        step, temp, slot = self.steps[i], self.temps[0], i % RING
        to_line, result = self.sums[2:]
        self.free(i, lambda old: old["line"])
        if i >= RING:
            self.steps[slot]["store"].wait()
        copies = [self.load(self.line(i, self.mine[3], self.at.c), temp.at[0], 7)]
        step["twin"][3].wait_recv()
        copies.append(self.load(self.from_twin.at[i, 3], temp.at[1], 8))
        step["far"][0].wait_recv()
        copies.append(self.load(self.from_far.at[i, 0], temp.at[2], 9))
        step["near"].wait_recv()
        copies.append(self.load(self.from_near.at[i], temp.at[3], 10))
        wait(copies)

        def total(q):
            return (temp[0, q].astype(f32) + temp[1, q].astype(f32)) + (
                temp[2, q].astype(f32) + temp[3, q].astype(f32)
            )

        for k in range(3):
            to_line[slot, k] = total(self.at.others[k]).astype(bf16)
            step["line"][k].start()
        result[slot] = total(self.at.z)

    def fourth(self, i):
        step, temp, result, slot = self.steps[i], self.temps[1], self.sums[3], i % RING
        copies = []
        for k in range(3):
            step["line"][k].wait_recv()
            copies.append(self.load(self.from_line.at[i, k], temp.at[k], 11 + k))
        wait(copies)
        result[slot] = result[slot] + temp[0].astype(f32) + temp[1].astype(f32) + temp[2].astype(f32)
        step["store"].start()

    def free(self, i, sends):
        if i >= RING:
            for copy in sends(self.steps[i - RING]):
                copy.wait_send()

    def finish(self):
        for i, step in enumerate(self.steps):
            for copy in step["twin"]:
                copy.wait_send()
            if i + RING >= len(self.steps):
                for copy in step["far"] + [step["near"]] + step["line"]:
                    copy.wait_send()
                step["store"].wait()


def flip_rows(src, dst):
    for tile in range(src.shape[1] // LANES):
        cols = pl.ds(tile * LANES, LANES)
        dst[cols, :] = src[:, cols].astype(f32).T.astype(bf16)


def backward_kernel(*refs):
    grad_out_ref, x_ref, gain_one_ref, gain_two_ref, cos_ref, sin_ref, first_ref, last_ref = refs[:8]
    full_refs, kept = refs[8:12], refs[12:21]
    attn_in_ref, y_ref, kv_ref, mix_ref, logs_ref, residual_ref, mlp_in_ref, acts_ref, hidden_ref = kept
    sum_ref, grad_in_ref, gain_sum_ref, grad_ref = refs[21:25]
    parts = refs[25:29]
    scratch = refs[29:]
    sums, temps = scratch[:4], scratch[4:6]
    staging, grad_res, branch, kv_out, kv_in, gains = scratch[6:12]
    sems, pulled, pushed, kv_sent, kv_came, gain_sent, gain_came = scratch[12:16], *scratch[16:22]
    at = Place()
    at.greet()
    scatter = Scatter(at, grad_ref, parts, sums, temps, sems, sum_ref)
    dma = pltpu.SemaphoreType.DMA
    vmem = pltpu.VMEM
    tokens, width = grad_res.shape
    lanes = hidden_ref.shape[2]
    size = lanes // 2
    tiles = size // 256

    def pull(src, dst, k):
        return pltpu.make_async_copy(src, dst, pulled.at[k])

    def pull_cut(pack, cut, dst, k):
        return [
            pull(
                full_refs[pack].at[half].reshape(width, lanes).at[:, pl.ds(cut * size, size)],
                dst.at[:, pl.ds(half * size, size)],
                k + half,
            )
            for half in range(2)
        ]

    def push(i):
        slot = i % 2
        return [
            pltpu.make_async_copy(
                staging.at[slot, half], grad_ref.at[i, half].reshape(width, size), pushed.at[slot, half]
            )
            for half in range(2)
        ]

    def weight_grad(i, left, right):
        def body(k, carry):
            half, cols = k // tiles, pl.ds(pl.multiple_of((k % tiles) * 256, 256), 256)
            staging[i % 2, half, :, cols] = dot_nn(left[...], right[half, :, cols]).astype(bf16)
            return carry

        lax.fori_loop(0, 2 * tiles, body, 0)
        start(push(i))

    def feed_forward(weights, acts, hidden, grad_out, out_turned, in_turned, grad_acts):
        def pulls(cut):
            cols = pl.ds(cut * size, size)
            return {
                "hidden": [pull(hidden_ref.at[:, :, cols], hidden, 0)],
                "down": pull_cut(3, cut, weights.at[0], 1),
                "acts": [pull(acts_ref.at[:, :, :, cols], acts, 3)],
                "gate": pull_cut(1, cut, weights.at[1], 4) + pull_cut(2, cut, weights.at[2], 6),
            }

        copies = pulls(0)
        given = [pull(grad_out_ref, grad_out, 8), pull(mlp_in_ref, branch, 9)]
        start(given + copies["hidden"] + copies["down"] + copies["acts"] + copies["gate"])
        wait(given)
        flip_rows(grad_out, out_turned)
        flip_rows(branch, in_turned)
        later = pulls(1)
        for cut in range(2):
            i = 3 * cut
            wait(copies["hidden"])
            if cut == 1:
                wait(push(i - 2))
                scatter.begin(i - 2)
            weight_grad(i, out_turned, hidden)
            if cut == 0:
                start(later["hidden"])
            else:
                scatter.first(i - 2)
            wait(copies["down"] + copies["acts"])

            def act_grads(k, carry):
                half, tile = k // tiles, k % tiles
                cols = pl.ds(pl.multiple_of(tile * 256, 256), 256)
                grad = dot_nn(grad_out[...], weights[0, :, pl.ds(pl.multiple_of(k * 256, 256), 256)])
                gate, up = acts[half, 0, :, cols], acts[half, 1, :, cols]
                sigmoid = jax.nn.sigmoid(gate)
                grad_acts[0, half, :, cols] = (
                    grad * up * sigmoid * (1.0 + gate * (1.0 - sigmoid))
                ).astype(bf16)
                grad_acts[1, half, :, cols] = (grad * gate * sigmoid).astype(bf16)
                return carry

            lax.fori_loop(0, 2 * tiles, act_grads, 0)
            if cut == 0:
                start(later["down"] + later["acts"])
            else:
                wait(push(i - 1))
                scatter.begin(i - 1)
            weight_grad(i + 1, in_turned, grad_acts.at[0])
            wait(push(i))
            scatter.begin(i)
            if cut == 1:
                scatter.first(i - 1)
            weight_grad(i + 2, in_turned, grad_acts.at[1])
            scatter.first(i)
            wait(copies["gate"])

            def rows_of(k, carry, cut=cut):
                rows = pl.ds(pl.multiple_of(k * 256, 256), 256)
                total = None if cut == 0 else grad_res[rows, :]
                for half in range(2):
                    for part in range(2):
                        term = dot_nt(
                            grad_acts[part, half, rows, :], weights[1 + part, :, pl.ds(half * size, size)]
                        )
                        total = term if total is None else total + term
                grad_res[rows, :] = total
                return carry

            lax.fori_loop(0, tokens // 256, rows_of, 0)
            if cut == 0:
                start(later["gate"])
            copies = later

    pl.run_scoped(
        feed_forward,
        vmem((3, width, lanes), bf16),
        vmem((2, 2, tokens, size), f32),
        vmem((2, tokens, size), bf16),
        vmem((tokens, width), bf16),
        vmem((width, tokens), bf16),
        vmem((width, tokens), bf16),
        vmem((2, 2, tokens, size), bf16),
    )
    wait(push(4))
    scatter.begin(4)
    wait(push(5))
    scatter.begin(5)
    scatter.first(4)

    def second_norm(residual, grad_out):
        copies = [pull(residual_ref, residual, 0), pull(grad_out_ref, grad_out, 1)]
        start(copies)
        wait(copies)
        gain = gain_two_ref[...]

        def rows_of(k, carry):
            rows = pl.ds(pl.multiple_of(k * 128, 128), 128)
            value, grad = residual[rows, :], grad_res[rows, :]
            inverse = lax.rsqrt(jnp.mean(value * value, axis=1, keepdims=True) + eps)
            normed = value * inverse
            scaled = grad * gain
            inner = jnp.mean(scaled * normed, axis=1, keepdims=True)
            total = grad_out[rows, :].astype(f32) + inverse * (scaled - normed * inner)
            grad_res[rows, :] = total
            branch[rows, :] = total.astype(bf16)
            return carry + jnp.sum(grad * normed, axis=0, keepdims=True)

        gains[0, pl.ds(1, 1), :] = lax.fori_loop(0, tokens // 128, rows_of, jnp.zeros((1, width), f32))

    gains[0] = jnp.zeros(gains.shape[1:], f32)
    pl.run_scoped(second_norm, vmem((tokens, width), f32), vmem((tokens, width), bf16))
    scatter.first(5)

    def attention(weights, y, kv, dup, flip, acc, mix, grad_mix, grad_y, turned, logs, grad_kv, held):
        copies = [
            pull(full_refs[0].at[half].reshape(width, lanes), weights.at[half], half) for half in range(2)
        ] + [
            pull(y_ref, y, 2),
            pull(kv_ref, kv, 3),
            pull(mix_ref, mix, 4),
            pull(logs_ref, logs, 5),
            pull(attn_in_ref, held, 6),
        ]
        start(copies)
        scatter.second(0)
        wait(copies[:2])

        def mix_of(k, carry):
            half, rows = k // 2, pl.ds(pl.multiple_of((k % 2) * 256, 256), 256)
            grad_mix[half, rows, :] = dot_nn(
                branch[rows, :], weights[half, :, pl.ds(7 * LANES, 5 * LANES)]
            ).astype(bf16)
            return carry

        lax.fori_loop(0, 4, mix_of, 0)
        scatter.second(1)
        wait(copies[2:])
        mine = pl.ds(pl.multiple_of(at.x * tokens, tokens), tokens)
        other = pl.ds(pl.multiple_of((1 - at.x) * tokens, tokens), tokens)
        block = 256
        steps = tokens // block

        def send_kv(half):
            return remote(kv_out.at[half], kv_in.at[half], kv_sent.at[half], kv_came.at[half], at.cross)

        def rows_of(i, carry):
            half = i // steps

            @pl.when(i % steps == 0)
            def _():
                load_groups(kv, half, dup, flip)
                acc[...] = jnp.zeros_like(acc)

            attend_back_rows(
                half, i % steps, block, y, dup, flip, first_ref, last_ref, logs, grad_mix, cos_ref, sin_ref, grad_y, acc
            )

            @pl.when(i % steps == steps - 1)
            def _():
                join_groups(acc, grad_kv, half)
                kv_out[half] = grad_kv[half, other, :].astype(bf16)

            for k, work in enumerate(
                [
                    lambda: (scatter.third(0), scatter.second(2)),
                    lambda: (send_kv(0).start(), scatter.third(1), scatter.second(3)),
                    lambda: (scatter.third(2), scatter.fourth(0), scatter.second(4)),
                    lambda: (send_kv(1).start(), scatter.third(3), scatter.fourth(1), scatter.second(5)),
                ]
            ):

                @pl.when(i == k)
                def _(work=work):
                    work()

            return carry

        lax.fori_loop(0, 2 * steps, rows_of, 0)
        flip_rows(held, turned.at[0])
        flip_rows(branch, turned.at[1])
        scatter.third(4)
        scatter.fourth(2)
        lane = lane_of((tokens, LANES))
        lower = lane % HEAD < HEAD // 2
        for half in range(2):
            send_kv(half).wait()
            for tile in range(3):
                cols = pl.ds(tile * LANES, LANES)
                total = grad_kv[half, mine, cols] + kv_in[half, :, cols].astype(f32)
                if tile < 2:
                    back = turn_back(total, cos_ref[...], sin_ref[...], lower)
                    total = back if tile == 0 else jnp.where(lane < HEAD, back, total)
                grad_y[half, :, cols] = total.astype(bf16)

        def first_part(k, carry):
            half, cols = k // tiles, pl.ds(pl.multiple_of((k % tiles) * 256, 256), 256)
            staging[0, half, :, cols] = dot_nn(turned[0], grad_y[half, :, cols]).astype(bf16)
            return carry

        lax.fori_loop(0, 2 * tiles, first_part, 0)
        start(push(6))
        for half in range(2):
            tail = dot_nn(turned[0], grad_y[half, :, pl.ds(6 * LANES, 2 * LANES)])
            head = dot_nn(turned[1], mix[half, :, pl.ds(0, LANES)])
            staging[1, half, :, pl.ds(0, LANES)] = tail[:, :LANES].astype(bf16)
            staging[1, half, :, pl.ds(LANES, LANES)] = (tail[:, LANES:] + head).astype(bf16)
            for k in range(2):
                staging[1, half, :, pl.ds((2 + 2 * k) * LANES, 2 * LANES)] = dot_nn(
                    turned[1], mix[half, :, pl.ds((1 + 2 * k) * LANES, 2 * LANES)]
                ).astype(bf16)
        start(push(7))
        wait(push(6))
        scatter.begin(6)
        scatter.third(5)
        scatter.fourth(3)
        wait(push(7))
        scatter.begin(7)
        scatter.first(6)
        scatter.first(7)
        load_x = pull(x_ref, held, 6)
        load_x.start()
        gain = gain_one_ref[...]
        load_x.wait()

        def input_rows(k, carry):
            rows = pl.ds(pl.multiple_of(k * 128, 128), 128)
            grad = dot_nt(grad_y[0, rows, :], weights[0, :, pl.ds(0, 8 * LANES)]) + dot_nt(
                grad_y[1, rows, :], weights[1, :, pl.ds(0, 8 * LANES)]
            )
            value = held[rows, :].astype(f32)
            inverse = lax.rsqrt(jnp.mean(value * value, axis=1, keepdims=True) + eps)
            normed = value * inverse
            scaled = grad * gain
            inner = jnp.mean(scaled * normed, axis=1, keepdims=True)
            branch[rows, :] = (grad_res[rows, :] + inverse * (scaled - normed * inner)).astype(bf16)
            return carry + jnp.sum(grad * normed, axis=0, keepdims=True)

        gains[0, pl.ds(0, 1), :] = lax.fori_loop(0, tokens // 128, input_rows, jnp.zeros((1, width), f32))

    keys = kv_ref.shape[1]
    pl.run_scoped(
        attention,
        vmem((2, width, lanes), bf16),
        vmem(y_ref.shape, bf16),
        vmem(kv_ref.shape, bf16),
        vmem((6, keys, LANES), bf16),
        vmem((6, LANES, keys), bf16),
        vmem((6, keys, LANES), f32),
        vmem(mix_ref.shape, bf16),
        vmem(mix_ref.shape, bf16),
        vmem(y_ref.shape, bf16),
        vmem((2, width, tokens), bf16),
        vmem(logs_ref.shape, f32),
        vmem((2, keys, 3 * LANES), f32),
        vmem((tokens, width), bf16),
    )
    out = pull(branch, grad_in_ref, 0)
    out.start()
    exchanges = [
        remote(gains.at[2 * k], gains.at[2 * k + 1], gain_sent.at[k], gain_came.at[k], peer)
        for k, peer in enumerate([at.twin, at.near, at.far])
    ]
    everyone = [
        remote(gains.at[6 + at.z], gains.at[6 + at.z], gain_sent.at[3 + k], gain_came.at[3 + k], at.line[k])
        for k in range(3)
    ]

    def fold(k):
        exchanges[k].wait()
        gains[6 + at.z if k == 2 else 2 * (k + 1)] = gains[2 * k] + gains[2 * k + 1]

    exchanges[0].start()
    scatter.fourth(4)
    scatter.second(6)
    fold(0)
    exchanges[1].start()
    scatter.second(7)
    scatter.fourth(5)
    fold(1)
    exchanges[2].start()
    scatter.third(6)
    fold(2)
    start(everyone)
    scatter.third(7)
    scatter.fourth(6)
    wait(everyone)
    gain_sum_ref[...] = gains[6] + gains[7] + gains[8] + gains[9]
    scatter.fourth(7)
    out.wait()
    scatter.finish()


def backward_special(grad_output, layer_input, gains, cosine, sine, first, last, packs, kept):
    tokens, width = layer_input.shape
    _, depth, lanes = packs[0].shape
    rows, size = depth // 16, lanes // 2
    count = len(SCATTER_PLAN)
    dma, vmem = pltpu.SemaphoreType.DMA, pltpu.VMEM
    anywhere = pl.BlockSpec(memory_space=pl.ANY)
    near = pl.BlockSpec(memory_space=pltpu.VMEM)
    shape = jax.ShapeDtypeStruct
    outs = pl.pallas_call(
        backward_kernel,
        out_shape=[
            shape((PACKS, rows, lanes), f32),
            shape((tokens, width), bf16),
            shape((8, width), f32),
            shape((count, 2, 4, 2, 2 * rows, size), bf16),
            shape((count, 4, 4, rows, size), bf16),
            shape((count, 2, 4, rows, size), bf16),
            shape((count, 4, rows, size), bf16),
            shape((count, 3, rows, size), bf16),
        ],
        in_specs=[anywhere] * 2 + [near] * 6 + [anywhere] * (PACKS + len(kept)),
        out_specs=[anywhere, anywhere, near] + [anywhere] * 5,
        scratch_shapes=[
            vmem((RING, 2, 4, rows, size), bf16),
            vmem((RING, 4, rows, size), bf16),
            vmem((RING, 3, rows, size), bf16),
            vmem((RING, rows, size), f32),
            vmem((4, 4, rows, size), bf16),
            vmem((3, rows, size), bf16),
            vmem((2, 2, width, size), bf16),
            vmem((tokens, width), f32),
            vmem((tokens, width), bf16),
            vmem((2, tokens, 3 * LANES), bf16),
            vmem((2, tokens, 3 * LANES), bf16),
            vmem((10, 8, width), f32),
            dma((count, 10)),
            dma((count, 10)),
            dma((14,)),
            dma((count,)),
            dma((10,)),
            dma((2, 2)),
            dma((2,)),
            dma((2,)),
            dma((6,)),
            dma((6,)),
        ],
        compiler_params=pltpu.CompilerParams(
            collective_id=2, has_side_effects=True, vmem_limit_bytes=VMEM_BYTES
        ),
        name="backward",
    )(
        grad_output,
        layer_input,
        gains[0],
        gains[1],
        cosine,
        sine,
        first,
        last,
        *[pack.reshape(2, 4, 2, 2 * rows, lanes) for pack in packs],
        *kept,
    )
    sums, grad_input, gain_sums = outs[:3]
    kv = lanes // 8
    mixed = sums[0]
    return (
        grad_input,
        gain_sums[:2],
        (
            mixed[:, 2 * kv : 5 * kv],
            mixed[:, :kv],
            mixed[:, kv : 2 * kv],
            mixed[:, 5 * kv :].T,
            sums[1],
            sums[2],
            sums[3].T,
        ),
    )


def special():
    return (lax.axis_size("row"), lax.axis_size("col")) == (16, 2)


def lane_of(shape):
    return lax.broadcasted_iota(jnp.int32, shape, len(shape) - 1)


def turn(values, cosine, sine, lower):
    ahead = pltpu.roll(values, LANES - HEAD // 2, 1)
    behind = pltpu.roll(values, HEAD // 2, 1)
    return values * cosine + jnp.where(lower, -ahead, behind) * sine


def turn_back(values, cosine, sine, lower):
    scaled = values * sine
    ahead = pltpu.roll(scaled, LANES - HEAD // 2, 1)
    behind = pltpu.roll(scaled, HEAD // 2, 1)
    return values * cosine - jnp.where(lower, -ahead, behind)


def project_half(half, attn_in_ref, weight_ref, cos_ref, sin_ref, y_ref):
    cosine, sine = cos_ref[...], sin_ref[...]
    lane = lane_of(cosine.shape)
    lower = lane % HEAD < HEAD // 2
    for pair in range(4):
        two = dot_nn(attn_in_ref[...], weight_ref[half, :, pl.ds(pair * 2 * LANES, 2 * LANES)]).astype(bf16)
        for side in range(2):
            tile = 2 * pair + side
            raw = two[:, side * LANES : (side + 1) * LANES].astype(f32)
            if tile == 2:
                out = raw
            else:
                out = turn(raw, cosine, sine, lower)
                if tile == 1:
                    out = jnp.where(lane < HEAD, out, raw)
                elif tile > 2:
                    out = out * HEAD ** (-0.5)
            y_ref[half, :, pl.ds(tile * LANES, LANES)] = out.astype(bf16)


def project_kernel(x_ref, gain_ref, weight_ref, cos_ref, sin_ref, attn_in_ref, y_ref):
    values = x_ref[...].astype(f32)
    inverse = lax.rsqrt(jnp.mean(values * values, axis=1, keepdims=True) + eps)
    attn_in_ref[...] = (values * inverse * gain_ref[...]).astype(bf16)
    for half in range(2):
        project_half(half, attn_in_ref, weight_ref, cos_ref, sin_ref, y_ref)


def head_rows(values, side, lane):
    return jnp.where((lane < HEAD) if side == 0 else (lane >= HEAD), values, jnp.zeros_like(values))


def twice(tile, side, lane):
    values = tile.astype(f32)
    other = pltpu.roll(values, HEAD, 1)
    keep = (lane < HEAD) if side == 0 else (lane >= HEAD)
    return jnp.where(keep, values, other)


def load_groups(kv_ref, half, dup_ref, flip_ref):
    for slot in range(6):
        tile = kv_ref[half, :, pl.ds((slot // 2) * LANES, LANES)]
        both = twice(tile, slot % 2, lane_of(tile.shape))
        dup_ref[slot] = both.astype(bf16)
        flip_ref[slot] = both.T.astype(bf16)


def seen(first_ref, last_ref, rows, keys):
    index = lax.broadcasted_iota(jnp.int32, (keys, rows.size), 0)
    return (index >= first_ref[:, rows]) & (index <= last_ref[:, rows])


def attend_rows(half, step, block, y_ref, dup_ref, flip_ref, first_ref, last_ref, mix_ref, log_ref):
    keys = dup_ref.shape[1]
    lane = lane_of((block, LANES))
    rows = pl.ds(pl.multiple_of(step * block, block), block)
    allowed = seen(first_ref, last_ref, rows, keys)
    previous = jnp.zeros((block, LANES), f32)
    for head in range(9):
        group = head // 3
        query = head_rows(y_ref[half, rows, pl.ds((3 + head // 2) * LANES, LANES)], head % 2, lane)
        scores = jnp.where(allowed, dot_nt(dup_ref[group], query), neg_fill)
        top = jnp.max(scores, axis=0, keepdims=True)
        powers = jnp.exp(scores - top)
        total = jnp.sum(powers, axis=0, keepdims=True)
        probs = (powers * (1.0 / total)).astype(bf16)
        mixed = dot_nn(flip_ref[3 + group], probs).T
        log_ref[half, pl.ds(head, 1), rows] = top + jnp.log(total)
        if head % 2 == 0:
            tile = jnp.where(lane < HEAD, previous, mixed)
            mix_ref[half, rows, pl.ds((head // 2) * LANES, LANES)] = tile.astype(bf16)
        previous = mixed


def attend_kernel(block, y_ref, kv_ref, first_ref, last_ref, mix_ref, log_ref, dup_ref, flip_ref):
    load_groups(kv_ref, 0, dup_ref, flip_ref)

    def rows_of(step, carry):
        attend_rows(0, step, block, y_ref, dup_ref, flip_ref, first_ref, last_ref, mix_ref, log_ref)
        return carry

    lax.fori_loop(0, y_ref.shape[1] // block, rows_of, 0)


def attend_back_rows(
    half, step, block, y_ref, dup_ref, flip_ref, first_ref, last_ref, log_ref, grad_ref, cos_ref, sin_ref, out_ref, acc_ref
):
    keys = dup_ref.shape[1]
    lane = lane_of((block, LANES))
    lower = lane % HEAD < HEAD // 2
    rows = pl.ds(pl.multiple_of(step * block, block), block)
    allowed = seen(first_ref, last_ref, rows, keys)
    previous = None
    for head in range(9):
        group = head // 3
        query = head_rows(y_ref[half, rows, pl.ds((3 + head // 2) * LANES, LANES)], head % 2, lane)
        upstream = head_rows(
            grad_ref[half, rows, pl.ds(((head + 1) // 2) * LANES, LANES)], (head + 1) % 2, lane
        )
        scores = jnp.where(allowed, dot_nt(dup_ref[group], query), neg_fill)
        probs = jnp.exp(scores - log_ref[half, pl.ds(head, 1), rows])
        grad_probs = dot_nt(dup_ref[3 + group], upstream)
        inner = jnp.sum(probs * grad_probs, axis=0, keepdims=True)
        grad_scores = (probs * (grad_probs - inner)).astype(bf16)
        acc_ref[3 + group] += dot_nn(probs.astype(bf16), upstream)
        acc_ref[group] += dot_nn(grad_scores, query)
        grad_query = dot_nn(flip_ref[group], grad_scores).T
        if head % 2 == 1 or head == 8:
            if head == 8:
                tile = jnp.where(lane < HEAD, grad_query, 0.0)
            else:
                tile = jnp.where(lane < HEAD, previous, grad_query)
            tile = turn_back(tile * HEAD ** (-0.5), cos_ref[rows, :], sin_ref[rows, :], lower)
            out_ref[half, rows, pl.ds((3 + head // 2) * LANES, LANES)] = tile.astype(bf16)
        previous = grad_query


def join_groups(acc_ref, out_ref, half):
    lane = lane_of((acc_ref.shape[1], LANES))
    for tile in range(3):
        low, high = acc_ref[2 * tile], acc_ref[2 * tile + 1]
        low = low + pltpu.roll(low, HEAD, 1)
        high = high + pltpu.roll(high, HEAD, 1)
        out_ref[half, :, pl.ds(tile * LANES, LANES)] = jnp.where(lane < HEAD, low, high)


def attend_back_kernel(
    block, y_ref, kv_ref, first_ref, last_ref, log_ref, grad_ref, cos_ref, sin_ref, dq_ref, dkv_ref, dup_ref, flip_ref, acc_ref
):
    load_groups(kv_ref, 0, dup_ref, flip_ref)
    acc_ref[...] = jnp.zeros_like(acc_ref)

    def rows_of(step, carry):
        attend_back_rows(
            0, step, block, y_ref, dup_ref, flip_ref, first_ref, last_ref, log_ref, grad_ref, cos_ref, sin_ref, dq_ref, acc_ref
        )
        return carry

    lax.fori_loop(0, y_ref.shape[1] // block, rows_of, 0)
    join_groups(acc_ref, dkv_ref, 0)


def full_spec(shape):
    return pl.BlockSpec(shape, lambda i: (0,) * len(shape))


def half_spec(shape):
    return pl.BlockSpec((1,) + shape[1:], lambda i: (i,) + (0,) * (len(shape) - 1))


def params():
    return pltpu.CompilerParams(vmem_limit_bytes=VMEM_BYTES)


def project(layer_input, gain, first_pack, cosine, sine):
    tokens, width = layer_input.shape
    vm = pl.BlockSpec(memory_space=pltpu.VMEM)
    return pl.pallas_call(
        project_kernel,
        grid=(1,),
        out_shape=(
            jax.ShapeDtypeStruct((tokens, width), bf16),
            jax.ShapeDtypeStruct((2, tokens, 8 * LANES), bf16),
        ),
        in_specs=[
            full_spec((tokens, width)),
            full_spec((1, width)),
            full_spec((2, width, 8 * LANES)),
            full_spec((tokens, LANES)),
            full_spec((tokens, LANES)),
        ],
        out_specs=(full_spec((tokens, width)), full_spec((2, tokens, 8 * LANES))),
        compiler_params=params(),
        name="project",
    )(layer_input, gain, first_pack, cosine, sine)


def attend(y, kv, first, last):
    tokens, keys = y.shape[1], kv.shape[1]
    block = min(256, tokens)
    return pl.pallas_call(
        lambda *refs: attend_kernel(block, *refs),
        grid=(2,),
        out_shape=(
            jax.ShapeDtypeStruct((2, tokens, 5 * LANES), bf16),
            jax.ShapeDtypeStruct((2, 16, tokens), f32),
        ),
        in_specs=[half_spec(y.shape), half_spec(kv.shape), full_spec((1, tokens)), full_spec((1, tokens))],
        out_specs=(half_spec((2, tokens, 5 * LANES)), half_spec((2, 16, tokens))),
        scratch_shapes=[pltpu.VMEM((6, keys, LANES), bf16), pltpu.VMEM((6, LANES, keys), bf16)],
        compiler_params=params(),
        name="attend",
    )(y, kv, first, last)


def attend_back(y, kv, first, last, logs, grad, cosine, sine):
    tokens, keys = y.shape[1], kv.shape[1]
    block = min(256, tokens)
    return pl.pallas_call(
        lambda *refs: attend_back_kernel(block, *refs),
        grid=(2,),
        out_shape=(
            jax.ShapeDtypeStruct((2, tokens, 8 * LANES), bf16),
            jax.ShapeDtypeStruct((2, keys, 3 * LANES), f32),
        ),
        in_specs=[
            half_spec(y.shape),
            half_spec(kv.shape),
            full_spec((1, tokens)),
            full_spec((1, tokens)),
            half_spec(logs.shape),
            half_spec(grad.shape),
            full_spec((tokens, LANES)),
            full_spec((tokens, LANES)),
        ],
        out_specs=(half_spec((2, tokens, 8 * LANES)), half_spec((2, keys, 3 * LANES))),
        scratch_shapes=[
            pltpu.VMEM((6, keys, LANES), bf16),
            pltpu.VMEM((6, LANES, keys), bf16),
            pltpu.VMEM((6, keys, LANES), f32),
        ],
        compiler_params=params(),
        name="attend_back",
    )(y, kv, first, last, logs, grad, cosine, sine)


def rope_tables(position):
    lane_index = (jnp.arange(LANES, dtype=jnp.int32) % (HEAD // 2)).astype(f32)
    frequency = jnp.exp(lane_index * (-2.0 * math.log(rope_base) / HEAD))
    angles = position[:, None] * frequency[None, :]
    return jnp.cos(angles), jnp.sin(angles)


def shards(
    layer_input,
    attn_gain,
    mlp_gain,
    query_weight,
    key_weight,
    value_weight,
    out_weight,
    gate_weight,
    up_weight,
    down_weight,
    seq_ids,
    block_ends,
    grad_output,
):
    tokens, width = layer_input.shape
    span = seq_ids.shape[0]
    start = lax.axis_index("col") * tokens
    index = jnp.arange(span, dtype=jnp.int32)
    in_first = seq_ids == seq_ids[0]
    seq_first = jnp.where(in_first, 0, jnp.sum(in_first.astype(jnp.int32)))
    block_last = block_ends - lax.axis_index("row") * span
    own_first = lax.dynamic_slice_in_dim(seq_first, start, tokens)
    own_last = lax.dynamic_slice_in_dim(block_last, start, tokens)
    position = lax.dynamic_slice_in_dim(index - seq_first, start, tokens).astype(f32)
    cosine, sine = rope_tables(position)
    own_first, own_last = own_first[None, :], own_last[None, :]
    gain_one = attn_gain.astype(f32)[None, :]
    gain_two = mlp_gain.astype(f32)[None, :]

    weights = (query_weight, key_weight, value_weight, out_weight, gate_weight, up_weight, down_weight)
    own = layer_input.astype(f32)
    if special():
        mine = jnp.concatenate([key_weight, value_weight, query_weight, out_weight.T], axis=1)
        packs, kept = forward_special(
            layer_input,
            (gain_one, gain_two),
            cosine,
            sine,
            own_first,
            own_last,
            (mine, gate_weight, up_weight, down_weight.T),
        )
        grad_input, gain_sums, weight_sums = backward_special(
            grad_output, layer_input, (gain_one, gain_two), cosine, sine, own_first, own_last, packs, kept[:9]
        )
        return (kept[9], grad_input, gain_sums[0], gain_sums[1]) + tuple(weight_sums)
    pack_first, pack_gate, pack_up, pack_down = gather_any(weights)
    attn_in, y = project(layer_input, gain_one, pack_first, cosine, sine)
    kv = lax.all_gather(y[:, :, : 3 * LANES], "col", axis=1, tiled=True)
    mix, logs = attend(y, kv, own_first, own_last)
    pack_out = pack_first[:, :, 7 * LANES :]
    branch = jnp.einsum("htq,hdq->td", mix, pack_out, preferred_element_type=f32)
    residual = own + branch
    inv_two = lax.rsqrt(jnp.mean(residual * residual, axis=1, keepdims=True) + eps)
    normed_two = residual * inv_two
    mlp_in = (normed_two * gain_two).astype(bf16)
    gate_act = jnp.einsum("td,hdf->htf", mlp_in, pack_gate, preferred_element_type=f32)
    up_act = jnp.einsum("td,hdf->htf", mlp_in, pack_up, preferred_element_type=f32)
    hidden = (jax.nn.silu(gate_act) * up_act).astype(bf16)
    layer_output = (
        residual + jnp.einsum("htf,hdf->td", hidden, pack_down, preferred_element_type=f32)
    ).astype(bf16)
    grad_down = jnp.einsum("td,htf->hdf", grad_output, hidden, preferred_element_type=f32).astype(bf16)
    grad_hidden = jnp.einsum("td,hdf->htf", grad_output, pack_down, preferred_element_type=f32)
    sigmoid = jax.nn.sigmoid(gate_act)
    grad_gate_act = (grad_hidden * up_act * sigmoid * (1.0 + gate_act * (1.0 - sigmoid))).astype(bf16)
    grad_up_act = (grad_hidden * gate_act * sigmoid).astype(bf16)
    grad_gate = jnp.einsum("td,htf->hdf", mlp_in, grad_gate_act, preferred_element_type=f32).astype(bf16)
    grad_up = jnp.einsum("td,htf->hdf", mlp_in, grad_up_act, preferred_element_type=f32).astype(bf16)
    grad_mlp_in = jnp.einsum(
        "htf,hdf->td", grad_gate_act, pack_gate, preferred_element_type=f32
    ) + jnp.einsum("htf,hdf->td", grad_up_act, pack_up, preferred_element_type=f32)
    scaled_two = grad_mlp_in * gain_two
    inner_two = jnp.mean(scaled_two * normed_two, axis=1, keepdims=True)
    grad_residual = grad_output.astype(f32) + inv_two * (scaled_two - normed_two * inner_two)
    grad_mlp_gain = jnp.sum(grad_mlp_in * normed_two, axis=0)
    grad_branch = grad_residual.astype(bf16)
    grad_mixture = jnp.einsum("td,hdq->htq", grad_branch, pack_out, preferred_element_type=f32).astype(bf16)
    grad_q, grad_kv = attend_back(y, kv, own_first, own_last, logs, grad_mixture, cosine, sine)
    grad_kv = lax.psum_scatter(grad_kv, "col", scatter_dimension=1, tiled=True)
    key_cos, key_sin = jnp.tile(cosine, (1, 3)), jnp.tile(sine, (1, 3))
    lane = jnp.arange(3 * LANES, dtype=jnp.int32)
    is_key = lane < 3 * HEAD
    scaled = grad_kv * key_sin
    turned = jnp.where(
        lane % HEAD < HEAD // 2, -jnp.roll(scaled, -(HEAD // 2), axis=2), jnp.roll(scaled, HEAD // 2, axis=2)
    )
    grad_kv = jnp.where(is_key, grad_kv * key_cos - turned, grad_kv).astype(bf16)
    grad_y = jnp.concatenate([grad_kv, grad_q[:, :, 3 * LANES :]], axis=2)
    grad_proj = jnp.einsum("td,htf->hdf", attn_in, grad_y, preferred_element_type=f32)
    grad_out = jnp.einsum("td,htq->hdq", grad_branch, mix, preferred_element_type=f32)
    grad_first = jnp.concatenate(
        [
            grad_proj[:, :, : 7 * LANES],
            grad_proj[:, :, 7 * LANES :] + grad_out[:, :, :LANES],
            grad_out[:, :, LANES:],
        ],
        axis=2,
    ).astype(bf16)
    grad_attn_in = jnp.einsum(
        "htf,hdf->td", grad_y, pack_first[:, :, : 8 * LANES], preferred_element_type=f32
    )
    inv_one = lax.rsqrt(jnp.mean(own * own, axis=1, keepdims=True) + eps)
    normed_one = own * inv_one
    scaled_one = grad_attn_in * gain_one
    inner_one = jnp.mean(scaled_one * normed_one, axis=1, keepdims=True)
    grad_input = (grad_residual + inv_one * (scaled_one - normed_one * inner_one)).astype(bf16)
    grad_attn_gain = jnp.sum(grad_attn_in * normed_one, axis=0)
    gain_sums, weight_sums = scatter_any(
        (grad_first, grad_gate, grad_up, grad_down), jnp.stack([grad_attn_gain, grad_mlp_gain])
    )
    return (layer_output, grad_input, gain_sums[0], gain_sums[1]) + tuple(weight_sums)


def solution(mesh):
    tokens_spec = P(("row", "col"), None)
    in_specs = (
        tokens_spec,
        P(),
        P(),
        P("row", "col"),
        P("row", "col"),
        P("row", "col"),
        P("col", "row"),
        P("row", "col"),
        P("row", "col"),
        P("col", "row"),
        P("row"),
        P("row"),
        tokens_spec,
    )
    out_specs = (
        tokens_spec,
        tokens_spec,
        P(),
        P(),
        P("row", "col"),
        P("row", "col"),
        P("row", "col"),
        P("col", "row"),
        P("row", "col"),
        P("row", "col"),
        P("col", "row"),
    )
    return jax.shard_map(shards, mesh=mesh, in_specs=in_specs, out_specs=out_specs, check_vma=False)
```

time: 601 us -> 386 us (0.64)
  the two profiles are of different devices: /device:TPU:0 before, /device:TPU:1 now
where the time goes in v2:
time: 386 us; the launch traced here: 380 us
  Pallas kernels  360 us (93%)
  local copies, waits for them, and re-layouts  14.5 us (4%)
  other arithmetic  5.18 us (1%)
    pallas_call x1, Pallas kernels, backward_special(): pl.pallas_call(backward_kernel, out_shape=[shape((PACKS, rows, lanes), f3...  194 us
    pallas_call x1, Pallas kernels, forward_special(): pl.pallas_call(lambda *refs: forward_kernel(plan, *refs), out_shape=[jax....  166 us

profile of v2, /device:TPU:1, one launch (start us, length us, event | category | flops | bytes accessed | tf_op | source)
XLA Modules:
  0.0 380.4 jit_solution(14287736515273033392)
XLA Ops:
  0.6 1.2 slice.36
  1.9 2.0 convert_reduce_fusion
  3.8 0.7 broadcast_subtract_fusion
  4.5 0.7 dynamic_slice.11
  5.2 1.3 reshape.35.refs_1_.refs_2_
  6.5 1.3 reshape.36.refs_2_.refs_3_
  7.7 0.6 broadcast_select_fusion
  8.4 0.7 dynamic_slice.10
  9.0 0.1 dynamic-slice_convert_fusion
  9.1 1.8 concatenate.3.refs_7_
  10.9 1.8 multiply_sine_fusion
  12.7 166.0 %forward.1 = (bf16[2,4,2,144,1536]{4,3,2,1,0:T(8,128)(2,1)}, bf16[2,4,2,144,1536]{4,3,2,1,0:T(8,128)(2,1)}, bf16[2,4,2,144,1536]{4,3,2,1,0:T(8,128)(2,1)}, bf16[...) custom-call(bf16[512,1152]{1,0:T(8,128)(2,1)} %refs_1_.1, ...), custom_call_target="tpu_custom_call" | custom-call | tf_op jit(solution)/shard_map/forward/pallas_call | solution.py:394
  178.7 193.9 %backward.1 = (f32[4,72,1536]{2,1,0:T(8,128)}, bf16[512,1152]{1,0:T(8,128)(2,1)}, f32[8,1152]{1,0:T(8,128)}, bf16[8,2,4,2,144,768]{5,4,3,2,1,0:T(8,128)(2,1)}, b...) custom-call(bf16[512,1152]{1,0:T(8,128)(2,1)} %refs_0_.3, ...), custom_call_target="tpu_custom_call" | custom-call | tf_op jit(solution)/shard_map/backward/pallas_call | solution.py:934
  372.6 1.5 slice_reduce_fusion
  374.1 0.0 copy-start
  374.1 2.6 slice_bitcast_fusion
  376.7 0.0 copy-start.1
  376.7 0.7 fusion.3
  377.4 0.8 slice_bitcast_fusion.4
  378.2 0.0 copy-done
  378.2 1.0 copy.26
  379.2 0.0 copy-done.1
  379.2 1.0 copy.27
  (1 shorter events, 0.0 us)
Async XLA Ops:
  374.1 4.1 %copy-start = (bf16[512,1152]{1,0:T(8,128)(2,1)S(1)}, bf16[512,1152]{1,0:T(8,128)(2,1)}, u32[]{:S(2)}) copy-start(bf16[512,1152]{1,0:T(8,128)(2,1)} %get-tuple-element.72) | copy-start | bytes 3538948
  376.7 2.5 copy-start.1

commit v3 on v2

--- a/solution.py
+++ b/solution.py
@@ -81,6 +81,29 @@
 
 PACKS = 4
 MESH = pl.DeviceIdType.MESH
+
+
+class Sides:
+    def __init__(self, at, core0, core1):
+        if core0 == core1:
+            along_x = twin_x = int(core0 == "x")
+        else:
+            along_x = at.c if core0 == "y" else 1 - at.c
+            twin_x = 1 - along_x
+        self.near_x, self.near_y, self.far_x, self.far_y = self.spots(at, along_x)
+        self.near = at.device(self.near_x, at.z, self.near_y, at.c)
+        self.far = at.device(self.far_x, at.z, self.far_y, at.c)
+        twin = self.spots(at, twin_x)
+        rest = (1 - at.x, 1 - at.y)
+        self.order = [(self.far_x, self.far_y), rest, (self.near_x, self.near_y), (at.x, at.y)]
+        self.twin_order = [twin[2:], rest, twin[:2], (at.x, at.y)]
+
+    @staticmethod
+    def spots(at, along_x):
+        x, y = at.x, at.y
+        near = (x + along_x * (1 - 2 * x), y + (1 - along_x) * (1 - 2 * y))
+        far = (x + (1 - along_x) * (1 - 2 * x), y + along_x * (1 - 2 * y))
+        return near + far
 
 
 class Place:
@@ -115,27 +138,53 @@
 
 
 GATHER_PLAN = [
-    (0, 0, 512, 0),
-    (0, 512, 512, 0),
-    (0, 1024, 512, 0),
-    (1, 0, 768, 1),
-    (2, 0, 768, 0),
-    (1, 768, 768, 0),
-    (2, 768, 768, 0),
-    (3, 0, 768, 1),
-    (3, 768, 768, 0),
+    (0, 0, 512, 0, "y", "y"),
+    (0, 512, 512, 0, "y", "x"),
+    (0, 1024, 512, 0, "x", "x"),
+    (1, 0, 768, 0, "y", "x"),
+    (2, 0, 768, 1, "x", "x"),
+    (1, 768, 768, 1, "y", "x"),
+    (2, 768, 768, 0, "x", "x"),
+    (3, 0, 768, 0, "x", "y"),
+    (3, 768, 768, 1, "y", "y"),
 ]
-SCATTER_PLAN = [(3, 0), (1, 0), (2, 0), (3, 1), (1, 1), (2, 1), (0, 0), (0, 1)]
+FORWARD_ORDER = [
+    ("B", 0), ("B", 1), ("B", 2), ("F", 0), ("B", 6), ("F", 1), ("S", 1), ("F", 2), ("S", 0), "norm",
+    ("F", 6), ("B", 4), ("B", 3), ("T", 0), ("B", 7), ("S", 2), ("T", 1), "kv", ("S", 6), "q", ("B", 5),
+    ("F", 4), ("F", 3), "a0", ("B", 8), ("F", 7), "a1", "a2", ("T", 2), ("S", 3), ("S", 4), ("F", 5),
+    ("F", 8), "a3", ("T", 6), "br", ("T", 3), ("S", 5), ("T", 4), ("S", 8), "h0", ("T", 5), ("S", 7), "h1",
+    ("T", 7), ("T", 8), "o0", "o1",
+]
+SCATTER_PLAN = [
+    (3, 0, 1, "y", "x"),
+    (1, 0, 1, "y", "x"),
+    (2, 0, 1, "x", "x"),
+    (3, 1, 0, "y", "x"),
+    (1, 1, 0, "x", "y"),
+    (2, 1, 0, "y", "y"),
+    (0, 1, 0, "y", "x"),
+    (0, 0, 0, "x", "y"),
+]
+BACKWARD_ORDER = [
+    "ld", "w0", "d0", ("B", 0), "w1", "w2", ("1", 0), "m0", ("B", 1), "w3", "d1", ("1", 1), ("B", 3),
+    ("2", 0), "w4", "w5", ("B", 5), ("1", 3), "m1", ("2", 1), ("B", 2), ("3", 0), ("B", 4), ("1", 5), "norm",
+    "mx", ("2", 3), ("1", 2), "a0", "a1", ("2", 2), "a2", ("2", 5), ("4", 0), ("1", 4), ("3", 1), ("3", 3),
+    "a3", "g1", ("B", 6), ("3", 5), ("1", 6), "kvw", ("3", 2), "g0", ("2", 4), ("B", 7), ("4", 1), "in",
+    ("2", 6), ("1", 7), ("4", 3), ("3", 4), ("2", 7), ("3", 6), ("3", 7), ("4", 4), ("4", 6), ("4", 5),
+    ("4", 2), ("4", 7),
+]
 RING = 6
 
 
 class Gather:
     def __init__(self, at, plan, own_refs, out_refs, copied, sent, came):
         x, y, z = at.x, at.y, at.z
+        self.plan, self.arrived = plan, set()
         size = own_refs[0].shape[0]
         rows = pl.ds(pl.multiple_of(at.c * size, 8), size)
         self.steps = []
-        for i, (pack, lane, lanes, kind) in enumerate(plan):
+        for i, (pack, lane, lanes, kind, *axes) in enumerate(plan):
+            sides = Sides(at, *axes)
             cols = pl.ds(lane, lanes)
             own = own_refs[pack].at[:, cols]
 
@@ -149,17 +198,25 @@
             step = {"kind": kind, "keep": pltpu.make_async_copy(own, one(x, y), copied.at[i])}
             step["line"] = [remote(own, one(x, y), sent.at[i, k], came.at[i, k], at.line[k]) for k in range(3)]
             if kind == 0:
-                step["near"] = line(x, y, 3, at.near)
+                step["near"] = line(x, y, 3, sides.near)
             else:
-                step["near"] = remote(own, one(x, y), sent.at[i, 3], came.at[i, 3], at.near)
+                step["near"] = remote(own, one(x, y), sent.at[i, 3], came.at[i, 3], sides.near)
                 step["more"] = [
-                    remote(one(at.xa, at.ya), one(at.xa, at.ya), sent.at[i, 4 + k], came.at[i, 4 + k], at.line[k])
+                    remote(
+                        one(sides.near_x, sides.near_y),
+                        one(sides.near_x, sides.near_y),
+                        sent.at[i, 4 + k],
+                        came.at[i, 4 + k],
+                        at.line[k],
+                    )
                     for k in range(3)
                 ]
-            step["far"] = [line(x, y, 7, at.far), line(at.xa, at.ya, 8, at.far)]
+            step["far"] = [line(x, y, 7, sides.far), line(sides.near_x, sides.near_y, 8, sides.far)]
             step["twin"] = [
                 line(xx, yy, 9 + j, at.twin)
-                for j, (xx, yy) in enumerate([(x, y), (at.xa, at.ya), (at.xb, at.yb), (1 - x, 1 - y)])
+                for j, (xx, yy) in enumerate(
+                    [(x, y), (sides.near_x, sides.near_y), (sides.far_x, sides.far_y), (1 - x, 1 - y)]
+                )
             ]
             self.steps.append(step)
 
@@ -201,15 +258,21 @@
                 step["far"][j].wait_recv()
                 step["twin"][2 + j].start()
 
-    def arrive(self, i):
-        for copy in self.steps[i]["twin"]:
-            copy.wait_recv()
-
-    def move(self, t):
-        self.first(t)
-        self.begin(t + 2)
-        self.second(t - 1)
-        self.third(t - 2)
+    def arrive(self, *chunks):
+        for i in chunks:
+            if i not in self.arrived:
+                self.arrived.add(i)
+                for copy in self.steps[i]["twin"]:
+                    copy.wait_recv()
+
+    def arrive_lanes(self, pack, low, high):
+        for i, (held, lane, lanes, *_) in enumerate(self.plan):
+            if held == pack and lane < high and lane + lanes > low:
+                self.arrive(i)
+
+    def run(self, moves):
+        for name, i in moves:
+            {"B": self.begin, "F": self.first, "S": self.second, "T": self.third}[name](i)
 
     def finish(self):
         for step in self.steps:
@@ -218,11 +281,13 @@
 
 
 def forward_kernel(plan, *refs):
-    x_ref, gain_one_ref, gain_two_ref, cos_ref, sin_ref, first_ref, last_ref = refs[:7]
-    own_refs, full_refs = refs[7:11], refs[11:15]
-    saved = refs[15:25]
-    weights, attn_in, y, kv, dup, flip, mix, logs, residual, mlp_in, acts, hidden, output = refs[25:38]
-    copied, sent, came, loaded, stored, kv_sent, kv_came = refs[38:]
+    x_ref, gain_ref, frequency_ref, ids_ref, ends_ref = refs[:5]
+    own_refs, full_refs = refs[5:9], refs[9:13]
+    saved = refs[13:27]
+    weights, attn_in, y, kv, dup, flip, mix, logs, residual, mlp_in, acts, hidden, output = refs[27:40]
+    cos_ref, sin_ref, first_ref, last_ref = refs[40:44]
+    copied, sent, came, loaded, stored, kv_sent, kv_came = refs[44:]
+    gain_one_ref, gain_two_ref = gain_ref.at[pl.ds(0, 1)], gain_ref.at[pl.ds(1, 1)]
     at = Place()
     at.greet()
     gather = Gather(at, plan, own_refs, full_refs, copied, sent, came)
@@ -256,81 +321,101 @@
         copy.start()
         return copy
 
-    gather.begin(0)
-    gather.begin(1)
-    values = x_ref[...].astype(f32)
-    inverse = lax.rsqrt(jnp.mean(values * values, axis=1, keepdims=True) + eps)
-    attn_in[...] = (values * inverse * gain_one_ref[...]).astype(bf16)
-    saves = [save(0, attn_in)]
-    for t in range(4):
-        gather.move(t)
-    gather.arrive(0)
-    gather.arrive(1)
-    start(project_loads)
     mine = pl.ds(pl.multiple_of(at.x * tokens, tokens), tokens)
-    for half in range(2):
-        project_loads[half].wait()
-        project_half(half, attn_in, weights, cos_ref, sin_ref, y)
-        kv[half, mine, :] = y[half, :, : 3 * LANES]
-        exchange = remote(kv.at[half, mine, :], kv.at[half, mine, :], kv_sent.at[half], kv_came.at[half], at.cross)
-        exchange.start()
-    saves.append(save(1, y))
-    gather.move(4)
-    for half in range(2):
-        remote(kv.at[half, mine, :], kv.at[half, mine, :], kv_sent.at[half], kv_came.at[half], at.cross).wait()
-    saves.append(save(2, kv))
+    exchanges = [
+        remote(kv.at[half, mine, :], kv.at[half, mine, :], kv_sent.at[half], kv_came.at[half], at.cross)
+        for half in range(2)
+    ]
     block = 256
     steps = tokens // block
-
-    def rows_of(i, carry):
-        half = i // steps
-
-        @pl.when(i % steps == 0)
-        def _():
-            load_groups(kv, half, dup, flip)
-
-        attend_rows(half, i % steps, block, y, dup, flip, first_ref, last_ref, mix, logs)
-        for k in range(4):
-
-            @pl.when(i == k * steps // 2)
-            def _(k=k):
-                gather.move(5 + k)
-
-        return carry
-
-    lax.fori_loop(0, 2 * steps, rows_of, 0)
-    saves.append(save(3, mix))
-    saves.append(save(4, logs))
-    gather.arrive(2)
-    start(out_loads)
-    wait(out_loads)
     span = pl.ds(7 * LANES, 5 * LANES)
-
-    def branch_of(i, carry):
-        rows = pl.ds(pl.multiple_of(i * 256, 256), 256)
-        total = x_ref[rows, :].astype(f32)
+    size = lanes // 2
+    saves = {}
+
+    def norm():
+        length = jnp.sum(1 - (ids_ref[...] & 1), axis=1, keepdims=True)
+        index = at.x * tokens + lax.broadcasted_iota(jnp.int32, (1, tokens), 1)
+        first_ref[...] = jnp.where(index < length, 0, length)
+        row_start = lax.axis_index("row") * ids_ref.shape[1]
+        last_ref[...] = ends_ref[:, pl.ds(pl.multiple_of(at.x * tokens, LANES), tokens)] - row_start
+        index = at.x * tokens + lax.broadcasted_iota(jnp.int32, (tokens, LANES), 0)
+        position = (index - jnp.where(index < length, 0, length)).astype(f32)
+        angles = position * frequency_ref[...]
+        cos_ref[...] = jnp.cos(angles)
+        sin_ref[...] = jnp.sin(angles)
+        for k, ref in enumerate((cos_ref, sin_ref, first_ref, last_ref)):
+            saves[10 + k] = save(10 + k, ref)
+        values = x_ref[...].astype(f32)
+        inverse = lax.rsqrt(jnp.mean(values * values, axis=1, keepdims=True) + eps)
+        attn_in[...] = (values * inverse * gain_one_ref[...]).astype(bf16)
+        saves[0] = save(0, attn_in)
+
+    def keys():
+        gather.arrive_lanes(0, 0, 8 * LANES)
+        start(project_loads)
         for half in range(2):
-            total = total + dot_nt(mix[half, rows, :], weights[half, :, span])
-        residual[rows, :] = total
-        inverse = lax.rsqrt(jnp.mean(total * total, axis=1, keepdims=True) + eps)
-        mlp_in[rows, :] = (total * inverse * gain_two_ref[...]).astype(bf16)
-        return carry
-
-    lax.fori_loop(0, tokens // 256, branch_of, 0)
-    saves.append(save(5, residual))
-    saves.append(save(6, mlp_in))
-    gather.move(9)
-    gather.move(10)
-    for cut in range(2):
-        for i in (3, 4) if cut == 0 else (5, 6):
-            gather.arrive(i)
+            project_loads[half].wait()
+            project_tiles(half, range(2), attn_in, weights, cos_ref, sin_ref, y)
+            kv[half, mine, :] = y[half, :, : 3 * LANES]
+            exchanges[half].start()
+
+    def queries():
+        for half in range(2):
+            project_tiles(half, range(2, 4), attn_in, weights, cos_ref, sin_ref, y)
+        saves[1] = save(1, y)
+
+    def attend_all(moves):
+        def rows_of(i, carry):
+            half = i // steps
+            for k in range(2):
+
+                @pl.when(i == k * steps)
+                def _(k=k):
+                    exchanges[k].wait()
+
+            @pl.when(i % steps == 0)
+            def _():
+                load_groups(kv, half, dup, flip)
+
+            attend_rows(half, i % steps, block, y, dup, flip, first_ref, last_ref, mix, logs)
+            for k, part in enumerate(moves):
+                if part:
+
+                    @pl.when(i == k * steps // 2)
+                    def _(part=part):
+                        gather.run(part)
+
+            return carry
+
+        lax.fori_loop(0, 2 * steps, rows_of, 0)
+        saves[2], saves[3], saves[4] = save(2, kv), save(3, mix), save(4, logs)
+
+    def branch():
+        gather.arrive_lanes(0, 8 * LANES, lanes)
+        start(out_loads)
+        wait(out_loads)
+
+        def rows_of(i, carry):
+            rows = pl.ds(pl.multiple_of(i * 256, 256), 256)
+            total = x_ref[rows, :].astype(f32)
+            for half in range(2):
+                total = total + dot_nt(mix[half, rows, :], weights[half, :, span])
+            residual[rows, :] = total
+            inverse = lax.rsqrt(jnp.mean(total * total, axis=1, keepdims=True) + eps)
+            mlp_in[rows, :] = (total * inverse * gain_two_ref[...]).astype(bf16)
+            return carry
+
+        lax.fori_loop(0, tokens // 256, rows_of, 0)
+        saves[5], saves[6] = save(5, residual), save(6, mlp_in)
+
+    def hide(cut):
+        gather.arrive_lanes(1, cut * size, (cut + 1) * size)
+        gather.arrive_lanes(2, cut * size, (cut + 1) * size)
         start(gate_loads[cut])
-    size = lanes // 2
-    for cut in range(2):
         wait(gate_loads[cut])
         slot = 2 - 2 * cut
 
-        def hidden_of(i, carry):
+        def tile_of(i, carry):
             half, tile = i // (size // 256), i % (size // 256)
             cols = pl.ds(pl.multiple_of(i * 256, 256), 256)
             into = pl.ds(pl.multiple_of(cut * size + tile * 256, 256), 256)
@@ -341,35 +426,58 @@
             hidden[half, :, into] = (gate * jax.nn.sigmoid(gate) * up).astype(bf16)
             return carry
 
-        lax.fori_loop(0, lanes // 256, hidden_of, 0)
+        lax.fori_loop(0, lanes // 256, tile_of, 0)
+        if cut == 1:
+            saves[7], saves[8] = save(7, acts), save(8, hidden)
+
+    def finish_rows(cut):
+        gather.arrive_lanes(3, cut * size, (cut + 1) * size)
+        start(down_loads[cut])
+        wait(down_loads[cut])
         if cut == 0:
-            gather.arrive(7)
-            start(down_loads[0])
-    gather.arrive(8)
-    start(down_loads[1])
-    saves.append(save(7, acts))
-    saves.append(save(8, hidden))
-    wait(down_loads[0] + down_loads[1])
-
-    def output_of(i, carry):
-        rows = pl.ds(pl.multiple_of(i * 256, 256), 256)
-        total = residual[rows, :]
-        for half in range(2):
-            for cut in range(2):
+            saves.pop(5).wait()
+
+        def rows_of(i, carry):
+            rows = pl.ds(pl.multiple_of(i * 256, 256), 256)
+            total = residual[rows, :]
+            for half in range(2):
                 total = total + dot_nt(
                     hidden[half, rows, pl.ds(cut * size, size)], weights[2 + cut, :, pl.ds(half * size, size)]
                 )
-        output[rows, :] = total.astype(bf16)
-        return carry
-
-    lax.fori_loop(0, tokens // 256, output_of, 0)
-    saves.append(save(9, output))
+            if cut == 0:
+                residual[rows, :] = total
+            else:
+                output[rows, :] = total.astype(bf16)
+            return carry
+
+        lax.fori_loop(0, tokens // 256, rows_of, 0)
+        if cut == 1:
+            saves[9] = save(9, output)
+
+    work = {
+        "norm": norm,
+        "kv": keys,
+        "q": queries,
+        "br": branch,
+        "h0": lambda: hide(0),
+        "h1": lambda: hide(1),
+        "o0": lambda: finish_rows(0),
+        "o1": lambda: finish_rows(1),
+    }
+    plain, looped = split_schedule(FORWARD_ORDER)
+    for entry in plain:
+        if isinstance(entry, tuple):
+            gather.run([entry])
+        elif entry == "a":
+            attend_all(looped)
+        else:
+            work[entry]()
     gather.finish()
-    for copy in saves:
+    for copy in saves.values():
         copy.wait()
 
 
-def forward_special(layer_input, gains, cosine, sine, first, last, packs):
+def forward_special(layer_input, gains, frequency, ids, ends, packs):
     plan = GATHER_PLAN
     tokens, width = layer_input.shape
     rows, lanes = packs[0].shape
@@ -388,13 +496,17 @@
         ((2, 2, tokens, lanes), f32),
         ((2, tokens, lanes), bf16),
         ((tokens, width), bf16),
+        ((tokens, LANES), f32),
+        ((tokens, LANES), f32),
+        ((1, tokens), jnp.int32),
+        ((1, tokens), jnp.int32),
     ]
     full = [((2, 4, 2, 2 * rows, lanes), bf16)] * PACKS
     count = len(plan)
     outs = pl.pallas_call(
         lambda *refs: forward_kernel(plan, *refs),
         out_shape=[jax.ShapeDtypeStruct(*shape) for shape in full + saved],
-        in_specs=[near] * 7 + [anywhere] * PACKS,
+        in_specs=[near] * 5 + [anywhere] * PACKS,
         out_specs=[anywhere] * (PACKS + len(saved)),
         scratch_shapes=[
             vmem((4, width, lanes), bf16),
@@ -410,6 +522,10 @@
             vmem(*saved[7]),
             vmem(*saved[8]),
             vmem(*saved[9]),
+            vmem(*saved[10]),
+            vmem(*saved[11]),
+            vmem(*saved[12]),
+            vmem(*saved[13]),
             dma((count,)),
             dma((count, 13)),
             dma((count, 13)),
@@ -422,8 +538,23 @@
             collective_id=1, has_side_effects=True, vmem_limit_bytes=VMEM_BYTES
         ),
         name="forward",
-    )(layer_input, gains[0], gains[1], cosine, sine, first, last, *packs)
+    )(layer_input, gains, frequency, ids, ends, *packs)
     return [part.reshape(2, 16 * rows, lanes) for part in outs[:PACKS]], outs[PACKS:]
+
+
+def split_schedule(order):
+    plain, looped, part = [], [[] for _ in range(4)], None
+    for entry in order:
+        if isinstance(entry, str) and entry[0] == "a":
+            part = int(entry[1])
+            if part == 0:
+                plain.append("a")
+        elif isinstance(entry, tuple) and part is not None and part < 4:
+            looped[part].append(entry)
+        else:
+            part = None
+            plain.append(entry)
+    return plain, looped
 
 
 def start(copies):
@@ -437,17 +568,16 @@
 
 
 class Scatter:
-    def __init__(self, at, grad_ref, parts, sums, temps, sems, out_ref):
+    def __init__(self, at, grad_ref, parts, sums, temps, sems, out_ref, pushes):
+        self.pushes, self.ready = pushes, set()
         self.at, self.grad, self.sums, self.temps = at, grad_ref, sums, temps
         self.from_twin, self.from_far, self.from_near, self.from_line = parts
         self.sent, self.came, self.loaded, self.stored = sems
         self.out_ref = out_ref
-        x, y = at.x, at.y
-        self.mine = [(at.xb, at.yb), (1 - x, 1 - y), (at.xa, at.ya), (x, y)]
-        self.theirs = [(at.xa, at.ya), (1 - x, 1 - y), (at.xb, at.yb), (x, y)]
         to_far, to_near, to_line, result = sums
         self.steps = []
-        for i, (pack, cut) in enumerate(SCATTER_PLAN):
+        for i, (pack, cut, kind, *axes) in enumerate(SCATTER_PLAN):
+            sides = Sides(at, *axes)
             lanes = result.shape[2]
 
             def send(src, dst, slot, device, i=i):
@@ -456,13 +586,23 @@
             self.steps.append(
                 {
                     "twin": [
-                        send(self.line(i, self.theirs[j], 1 - at.c), self.from_twin.at[i, j], j, at.twin)
+                        send(self.line(i, sides.twin_order[j], 1 - at.c), self.from_twin.at[i, j], j, at.twin)
                         for j in range(4)
                     ],
                     "far": [
-                        send(to_far.at[i % RING, j], self.from_far.at[i, j], 4 + j, at.far) for j in range(2)
+                        send(to_far.at[i % RING, j], self.from_far.at[i, j], 4 + j, sides.far) for j in range(2)
                     ],
-                    "near": send(to_near.at[i % RING], self.from_near.at[i], 6, at.near),
+                    "kind": kind,
+                    "near": (
+                        send(to_near.at[i % RING], self.from_near.at[i], 6, sides.near)
+                        if kind == 0
+                        else send(to_near.at[i % RING, at.z], self.from_near.at[i, 3], 6, sides.near)
+                    ),
+                    "more": [
+                        send(to_near.at[i % RING, at.others[k]], self.from_near.at[i, k], 10 + k, at.line[k])
+                        for k in range(3 * kind)
+                    ],
+                    "own": [self.line(i, sides.order[j], at.c) for j in range(4)],
                     "line": [
                         send(to_line.at[i % RING, k], self.from_line.at[i, k], 7 + k, at.line[k])
                         for k in range(3)
@@ -482,7 +622,13 @@
         copy.start()
         return copy
 
+    def pushed(self, i):
+        if i not in self.ready:
+            self.ready.add(i)
+            wait(self.pushes(i))
+
     def begin(self, i):
+        self.pushed(i)
         for j in (1, 0, 2, 3):
             self.steps[i]["twin"][j].start()
 
@@ -491,9 +637,10 @@
         self.free(i, lambda old: old["far"])
         copies = []
         for j in (1, 0):
-            own = self.load(self.line(i, self.mine[j], self.at.c), to_far.at[slot, j], 2 * j)
+            own = self.load(step["own"][j], to_far.at[slot, j], 2 * j)
             step["twin"][j].wait_recv()
             copies.append((j, [own, self.load(self.from_twin.at[i, j], temp.at[j], 2 * j + 1)]))
+        yield
         for j, pair in copies:
             wait(pair)
 
@@ -505,13 +652,14 @@
             step["far"][j].start()
 
     def second(self, i):
-        step, to_near, temp, slot = self.steps[i], self.sums[1], self.temps[0], i % RING
-        self.free(i, lambda old: [old["near"]])
-        copies = [self.load(self.line(i, self.mine[2], self.at.c), to_near.at[slot], 4)]
+        step, to_near, temp, slot = self.steps[i], self.sums[1], self.temps[1], i % RING
+        self.free(i, lambda old: [old["near"]] + old["more"])
+        copies = [self.load(step["own"][2], to_near.at[slot], 4)]
         step["twin"][2].wait_recv()
         copies.append(self.load(self.from_twin.at[i, 2], temp.at[0], 5))
         step["far"][1].wait_recv()
         copies.append(self.load(self.from_far.at[i, 1], temp.at[1], 6))
+        yield
         wait(copies)
 
         def body(q, carry):
@@ -520,27 +668,41 @@
             return carry
 
         lax.fori_loop(0, 4, body, 0)
-        step["near"].start()
+        if step["kind"] == 0:
+            step["near"].start()
+        start(step["more"])
 
     def third(self, i):
-        step, temp, slot = self.steps[i], self.temps[0], i % RING
-        to_line, result = self.sums[2:]
+        step, temp, slot = self.steps[i], self.temps[2], i % RING
+        to_near, to_line, result = self.sums[1:]
+        early = step["kind"] == 1
         self.free(i, lambda old: old["line"])
         if i >= RING:
             self.steps[slot]["store"].wait()
-        copies = [self.load(self.line(i, self.mine[3], self.at.c), temp.at[0], 7)]
+        copies = [self.load(step["own"][3], temp.at[0], 7)]
         step["twin"][3].wait_recv()
         copies.append(self.load(self.from_twin.at[i, 3], temp.at[1], 8))
         step["far"][0].wait_recv()
         copies.append(self.load(self.from_far.at[i, 0], temp.at[2], 9))
-        step["near"].wait_recv()
-        copies.append(self.load(self.from_near.at[i], temp.at[3], 10))
+        if early:
+            for copy in step["more"]:
+                copy.wait_recv()
+            copies.append(self.load(self.from_near.at[i, pl.ds(0, 3)], temp.at[3, pl.ds(0, 3)], 10))
+        else:
+            step["near"].wait_recv()
+            copies.append(self.load(self.from_near.at[i], temp.at[3], 10))
+        yield
         wait(copies)
+        if early:
+            value = to_near[slot, self.at.z].astype(f32)
+            for k in range(3):
+                value = value + temp[3, k].astype(f32)
+            to_near[slot, self.at.z] = value.astype(bf16)
+            step["near"].start()
 
         def total(q):
-            return (temp[0, q].astype(f32) + temp[1, q].astype(f32)) + (
-                temp[2, q].astype(f32) + temp[3, q].astype(f32)
-            )
+            value = (temp[0, q].astype(f32) + temp[1, q].astype(f32)) + temp[2, q].astype(f32)
+            return value if early else value + temp[3, q].astype(f32)
 
         for k in range(3):
             to_line[slot, k] = total(self.at.others[k]).astype(bf16)
@@ -548,14 +710,42 @@
         result[slot] = total(self.at.z)
 
     def fourth(self, i):
-        step, temp, result, slot = self.steps[i], self.temps[1], self.sums[3], i % RING
+        step, temp, result, slot = self.steps[i], self.temps[3], self.sums[3], i % RING
         copies = []
         for k in range(3):
             step["line"][k].wait_recv()
             copies.append(self.load(self.from_line.at[i, k], temp.at[k], 11 + k))
+        if step["kind"] == 1:
+            step["near"].wait_recv()
+            copies.append(self.load(self.from_near.at[i, 3], temp.at[3], 14))
+        yield
         wait(copies)
-        result[slot] = result[slot] + temp[0].astype(f32) + temp[1].astype(f32) + temp[2].astype(f32)
+        value = result[slot]
+        for k in range(len(copies)):
+            value = value + temp[k].astype(f32)
+        result[slot] = value
         step["store"].start()
+
+    def run(self, stages):
+        names = {"1": self.first, "2": self.second, "3": self.third, "4": self.fourth}
+        turn = []
+
+        def flush():
+            works = [names[name](i) for name, i in turn]
+            for work in works:
+                next(work)
+            for work in works:
+                next(work, None)
+            turn.clear()
+
+        for name, i in stages:
+            if name == "B":
+                self.begin(i)
+            else:
+                if any(name == held or (name > held and i == j) or i == j + RING for held, j in turn):
+                    flush()
+                turn.append((name, i))
+        flush()
 
     def free(self, i, sends):
         if i >= RING:
@@ -567,7 +757,7 @@
             for copy in step["twin"]:
                 copy.wait_send()
             if i + RING >= len(self.steps):
-                for copy in step["far"] + [step["near"]] + step["line"]:
+                for copy in step["far"] + [step["near"]] + step["more"] + step["line"]:
                     copy.wait_send()
                 step["store"].wait()
 
@@ -579,18 +769,18 @@
 
 
 def backward_kernel(*refs):
-    grad_out_ref, x_ref, gain_one_ref, gain_two_ref, cos_ref, sin_ref, first_ref, last_ref = refs[:8]
-    full_refs, kept = refs[8:12], refs[12:21]
+    grad_out_ref, x_ref, gain_ref, cos_ref, sin_ref, first_ref, last_ref = refs[:7]
+    full_refs, kept = refs[7:11], refs[11:20]
+    gain_one_ref, gain_two_ref = gain_ref.at[pl.ds(0, 1)], gain_ref.at[pl.ds(1, 1)]
     attn_in_ref, y_ref, kv_ref, mix_ref, logs_ref, residual_ref, mlp_in_ref, acts_ref, hidden_ref = kept
-    sum_ref, grad_in_ref, gain_sum_ref, grad_ref = refs[21:25]
-    parts = refs[25:29]
-    scratch = refs[29:]
-    sums, temps = scratch[:4], scratch[4:6]
-    staging, grad_res, branch, kv_out, kv_in, gains = scratch[6:12]
-    sems, pulled, pushed, kv_sent, kv_came, gain_sent, gain_came = scratch[12:16], *scratch[16:22]
+    sum_ref, grad_in_ref, gain_sum_ref, grad_ref = refs[20:24]
+    parts = refs[24:28]
+    scratch = refs[28:]
+    sums, temps = scratch[:4], scratch[4:8]
+    staging, grad_res, branch, kv_out, kv_in, gains = scratch[8:14]
+    sems, pulled, pushed, kv_sent, kv_came, gain_sent, gain_came = scratch[14:18], *scratch[18:24]
     at = Place()
     at.greet()
-    scatter = Scatter(at, grad_ref, parts, sums, temps, sems, sum_ref)
     dma = pltpu.SemaphoreType.DMA
     vmem = pltpu.VMEM
     tokens, width = grad_res.shape
@@ -620,12 +810,29 @@
             for half in range(2)
         ]
 
+    scatter = Scatter(at, grad_ref, parts, sums, temps, sems, sum_ref, push)
+    plain, looped = split_schedule(BACKWARD_ORDER)
+    first_end, second_end, third_end = (plain.index(name) for name in ("norm", "mx", "in"))
+
+    def follow(entries, work):
+        moves = []
+        for entry in entries:
+            if isinstance(entry, tuple):
+                moves.append(entry)
+            else:
+                scatter.run(moves)
+                moves = []
+                work[entry]()
+        scatter.run(moves)
+
     def weight_grad(i, left, right):
         def body(k, carry):
             half, cols = k // tiles, pl.ds(pl.multiple_of((k % tiles) * 256, 256), 256)
             staging[i % 2, half, :, cols] = dot_nn(left[...], right[half, :, cols]).astype(bf16)
             return carry
 
+        if i >= 2:
+            scatter.pushed(i - 2)
         lax.fori_loop(0, 2 * tiles, body, 0)
         start(push(i))
 
@@ -639,27 +846,26 @@
                 "gate": pull_cut(1, cut, weights.at[1], 4) + pull_cut(2, cut, weights.at[2], 6),
             }
 
-        copies = pulls(0)
+        cuts = [pulls(0), pulls(1)]
         given = [pull(grad_out_ref, grad_out, 8), pull(mlp_in_ref, branch, 9)]
-        start(given + copies["hidden"] + copies["down"] + copies["acts"] + copies["gate"])
-        wait(given)
-        flip_rows(grad_out, out_turned)
-        flip_rows(branch, in_turned)
-        later = pulls(1)
-        for cut in range(2):
-            i = 3 * cut
-            wait(copies["hidden"])
-            if cut == 1:
-                wait(push(i - 2))
-                scatter.begin(i - 2)
-            weight_grad(i, out_turned, hidden)
+
+        def load():
+            copies = cuts[0]
+            start(given + copies["hidden"] + copies["down"] + copies["acts"] + copies["gate"])
+            wait(given)
+            flip_rows(grad_out, out_turned)
+            flip_rows(branch, in_turned)
+
+        def down_grad(cut):
+            wait(cuts[cut]["hidden"])
+            weight_grad(3 * cut, out_turned, hidden)
             if cut == 0:
-                start(later["hidden"])
-            else:
-                scatter.first(i - 2)
-            wait(copies["down"] + copies["acts"])
-
-            def act_grads(k, carry):
+                start(cuts[1]["hidden"])
+
+        def act_grad(cut):
+            wait(cuts[cut]["down"] + cuts[cut]["acts"])
+
+            def tile_of(k, carry):
                 half, tile = k // tiles, k % tiles
                 cols = pl.ds(pl.multiple_of(tile * 256, 256), 256)
                 grad = dot_nn(grad_out[...], weights[0, :, pl.ds(pl.multiple_of(k * 256, 256), 256)])
@@ -671,22 +877,14 @@
                 grad_acts[1, half, :, cols] = (grad * gate * sigmoid).astype(bf16)
                 return carry
 
-            lax.fori_loop(0, 2 * tiles, act_grads, 0)
+            lax.fori_loop(0, 2 * tiles, tile_of, 0)
             if cut == 0:
-                start(later["down"] + later["acts"])
-            else:
-                wait(push(i - 1))
-                scatter.begin(i - 1)
-            weight_grad(i + 1, in_turned, grad_acts.at[0])
-            wait(push(i))
-            scatter.begin(i)
-            if cut == 1:
-                scatter.first(i - 1)
-            weight_grad(i + 2, in_turned, grad_acts.at[1])
-            scatter.first(i)
-            wait(copies["gate"])
-
-            def rows_of(k, carry, cut=cut):
+                start(cuts[1]["down"] + cuts[1]["acts"])
+
+        def input_grad(cut):
+            wait(cuts[cut]["gate"])
+
+            def rows_of(k, carry):
                 rows = pl.ds(pl.multiple_of(k * 256, 256), 256)
                 total = None if cut == 0 else grad_res[rows, :]
                 for half in range(2):
@@ -700,8 +898,16 @@
 
             lax.fori_loop(0, tokens // 256, rows_of, 0)
             if cut == 0:
-                start(later["gate"])
-            copies = later
+                start(cuts[1]["gate"])
+
+        work = {"ld": load}
+        for cut in range(2):
+            work["w" + str(3 * cut)] = lambda cut=cut: down_grad(cut)
+            work["d" + str(cut)] = lambda cut=cut: act_grad(cut)
+            work["w" + str(3 * cut + 1)] = lambda cut=cut: weight_grad(3 * cut + 1, in_turned, grad_acts.at[0])
+            work["w" + str(3 * cut + 2)] = lambda cut=cut: weight_grad(3 * cut + 2, in_turned, grad_acts.at[1])
+            work["m" + str(cut)] = lambda cut=cut: input_grad(cut)
+        follow(plain[:first_end], work)
 
     pl.run_scoped(
         feed_forward,
@@ -713,12 +919,6 @@
         vmem((width, tokens), bf16),
         vmem((2, 2, tokens, size), bf16),
     )
-    wait(push(4))
-    scatter.begin(4)
-    wait(push(5))
-    scatter.begin(5)
-    scatter.first(4)
-
     def second_norm(residual, grad_out):
         copies = [pull(residual_ref, residual, 0), pull(grad_out_ref, grad_out, 1)]
         start(copies)
@@ -741,7 +941,7 @@
 
     gains[0] = jnp.zeros(gains.shape[1:], f32)
     pl.run_scoped(second_norm, vmem((tokens, width), f32), vmem((tokens, width), bf16))
-    scatter.first(5)
+    follow(plain[first_end + 1 : second_end], {})
 
     def attention(weights, y, kv, dup, flip, acc, mix, grad_mix, grad_y, turned, logs, grad_kv, held):
         copies = [
@@ -753,20 +953,20 @@
             pull(logs_ref, logs, 5),
             pull(attn_in_ref, held, 6),
         ]
-        start(copies)
-        scatter.second(0)
-        wait(copies[:2])
-
-        def mix_of(k, carry):
-            half, rows = k // 2, pl.ds(pl.multiple_of((k % 2) * 256, 256), 256)
-            grad_mix[half, rows, :] = dot_nn(
-                branch[rows, :], weights[half, :, pl.ds(7 * LANES, 5 * LANES)]
-            ).astype(bf16)
-            return carry
-
-        lax.fori_loop(0, 4, mix_of, 0)
-        scatter.second(1)
-        wait(copies[2:])
+        def mix_grad():
+            start(copies)
+            wait(copies[:2])
+
+            def rows_of(k, carry):
+                half, rows = k // 2, pl.ds(pl.multiple_of((k % 2) * 256, 256), 256)
+                grad_mix[half, rows, :] = dot_nn(
+                    branch[rows, :], weights[half, :, pl.ds(7 * LANES, 5 * LANES)]
+                ).astype(bf16)
+                return carry
+
+            lax.fori_loop(0, 4, rows_of, 0)
+            wait(copies[2:])
+
         mine = pl.ds(pl.multiple_of(at.x * tokens, tokens), tokens)
         other = pl.ds(pl.multiple_of((1 - at.x) * tokens, tokens), tokens)
         block = 256
@@ -775,99 +975,101 @@
         def send_kv(half):
             return remote(kv_out.at[half], kv_in.at[half], kv_sent.at[half], kv_came.at[half], at.cross)
 
-        def rows_of(i, carry):
-            half = i // steps
-
-            @pl.when(i % steps == 0)
-            def _():
-                load_groups(kv, half, dup, flip)
-                acc[...] = jnp.zeros_like(acc)
-
-            attend_back_rows(
-                half, i % steps, block, y, dup, flip, first_ref, last_ref, logs, grad_mix, cos_ref, sin_ref, grad_y, acc
-            )
-
-            @pl.when(i % steps == steps - 1)
-            def _():
-                join_groups(acc, grad_kv, half)
-                kv_out[half] = grad_kv[half, other, :].astype(bf16)
-
-            for k, work in enumerate(
-                [
-                    lambda: (scatter.third(0), scatter.second(2)),
-                    lambda: (send_kv(0).start(), scatter.third(1), scatter.second(3)),
-                    lambda: (scatter.third(2), scatter.fourth(0), scatter.second(4)),
-                    lambda: (send_kv(1).start(), scatter.third(3), scatter.fourth(1), scatter.second(5)),
-                ]
-            ):
-
-                @pl.when(i == k)
-                def _(work=work):
-                    work()
-
-            return carry
-
-        lax.fori_loop(0, 2 * steps, rows_of, 0)
-        flip_rows(held, turned.at[0])
-        flip_rows(branch, turned.at[1])
-        scatter.third(4)
-        scatter.fourth(2)
-        lane = lane_of((tokens, LANES))
-        lower = lane % HEAD < HEAD // 2
-        for half in range(2):
-            send_kv(half).wait()
-            for tile in range(3):
-                cols = pl.ds(tile * LANES, LANES)
-                total = grad_kv[half, mine, cols] + kv_in[half, :, cols].astype(f32)
-                if tile < 2:
-                    back = turn_back(total, cos_ref[...], sin_ref[...], lower)
-                    total = back if tile == 0 else jnp.where(lane < HEAD, back, total)
-                grad_y[half, :, cols] = total.astype(bf16)
-
-        def first_part(k, carry):
-            half, cols = k // tiles, pl.ds(pl.multiple_of((k % tiles) * 256, 256), 256)
-            staging[0, half, :, cols] = dot_nn(turned[0], grad_y[half, :, cols]).astype(bf16)
-            return carry
-
-        lax.fori_loop(0, 2 * tiles, first_part, 0)
-        start(push(6))
-        for half in range(2):
-            tail = dot_nn(turned[0], grad_y[half, :, pl.ds(6 * LANES, 2 * LANES)])
-            head = dot_nn(turned[1], mix[half, :, pl.ds(0, LANES)])
-            staging[1, half, :, pl.ds(0, LANES)] = tail[:, :LANES].astype(bf16)
-            staging[1, half, :, pl.ds(LANES, LANES)] = (tail[:, LANES:] + head).astype(bf16)
-            for k in range(2):
-                staging[1, half, :, pl.ds((2 + 2 * k) * LANES, 2 * LANES)] = dot_nn(
-                    turned[1], mix[half, :, pl.ds((1 + 2 * k) * LANES, 2 * LANES)]
-                ).astype(bf16)
-        start(push(7))
-        wait(push(6))
-        scatter.begin(6)
-        scatter.third(5)
-        scatter.fourth(3)
-        wait(push(7))
-        scatter.begin(7)
-        scatter.first(6)
-        scatter.first(7)
+        def attend_back_all():
+            def rows_of(i, carry):
+                half = i // steps
+
+                @pl.when(i % steps == 0)
+                def _():
+                    load_groups(kv, half, dup, flip)
+                    acc[...] = jnp.zeros_like(acc)
+
+                attend_back_rows(
+                    half, i % steps, block, y, dup, flip, first_ref, last_ref, logs, grad_mix, cos_ref, sin_ref, grad_y, acc
+                )
+
+                @pl.when(i % steps == steps - 1)
+                def _():
+                    join_groups(acc, grad_kv, half)
+                    kv_out[half] = grad_kv[half, other, :].astype(bf16)
+
+                for k in range(2):
+
+                    @pl.when(i == (k + 1) * steps - 1)
+                    def _(k=k):
+                        send_kv(k).start()
+
+                for k, part in enumerate(looped):
+                    if part:
+
+                        @pl.when(i == k * steps // 2)
+                        def _(part=part):
+                            scatter.run(part)
+
+                return carry
+
+            lax.fori_loop(0, 2 * steps, rows_of, 0)
+
+        def late_part():
+            scatter.pushed(4)
+            flip_rows(held, turned.at[0])
+            flip_rows(branch, turned.at[1])
+            for half in range(2):
+                tail = dot_nn(turned[0], grad_y[half, :, pl.ds(6 * LANES, 2 * LANES)])
+                head = dot_nn(turned[1], mix[half, :, pl.ds(0, LANES)])
+                staging[0, half, :, pl.ds(0, LANES)] = tail[:, :LANES].astype(bf16)
+                staging[0, half, :, pl.ds(LANES, LANES)] = (tail[:, LANES:] + head).astype(bf16)
+                for k in range(2):
+                    staging[0, half, :, pl.ds((2 + 2 * k) * LANES, 2 * LANES)] = dot_nn(
+                        turned[1], mix[half, :, pl.ds((1 + 2 * k) * LANES, 2 * LANES)]
+                    ).astype(bf16)
+            start(push(6))
+            load_x.start()
+
+        def join_keys():
+            lane = lane_of((tokens, LANES))
+            lower = lane % HEAD < HEAD // 2
+            for half in range(2):
+                send_kv(half).wait()
+                for tile in range(3):
+                    cols = pl.ds(tile * LANES, LANES)
+                    total = grad_kv[half, mine, cols] + kv_in[half, :, cols].astype(f32)
+                    if tile < 2:
+                        back = turn_back(total, cos_ref[...], sin_ref[...], lower)
+                        total = back if tile == 0 else jnp.where(lane < HEAD, back, total)
+                    grad_y[half, :, cols] = total.astype(bf16)
+
+        def input_rows():
+            load_x.wait()
+            gain = gain_one_ref[...]
+
+            def rows_of(k, carry):
+                rows = pl.ds(pl.multiple_of(k * 128, 128), 128)
+                grad = dot_nt(grad_y[0, rows, :], weights[0, :, pl.ds(0, 8 * LANES)]) + dot_nt(
+                    grad_y[1, rows, :], weights[1, :, pl.ds(0, 8 * LANES)]
+                )
+                value = held[rows, :].astype(f32)
+                inverse = lax.rsqrt(jnp.mean(value * value, axis=1, keepdims=True) + eps)
+                normed = value * inverse
+                scaled = grad * gain
+                inner = jnp.mean(scaled * normed, axis=1, keepdims=True)
+                branch[rows, :] = (grad_res[rows, :] + inverse * (scaled - normed * inner)).astype(bf16)
+                return carry + jnp.sum(grad * normed, axis=0, keepdims=True)
+
+            gains[0, pl.ds(0, 1), :] = lax.fori_loop(0, tokens // 128, rows_of, jnp.zeros((1, width), f32))
+
         load_x = pull(x_ref, held, 6)
-        load_x.start()
-        gain = gain_one_ref[...]
-        load_x.wait()
-
-        def input_rows(k, carry):
-            rows = pl.ds(pl.multiple_of(k * 128, 128), 128)
-            grad = dot_nt(grad_y[0, rows, :], weights[0, :, pl.ds(0, 8 * LANES)]) + dot_nt(
-                grad_y[1, rows, :], weights[1, :, pl.ds(0, 8 * LANES)]
-            )
-            value = held[rows, :].astype(f32)
-            inverse = lax.rsqrt(jnp.mean(value * value, axis=1, keepdims=True) + eps)
-            normed = value * inverse
-            scaled = grad * gain
-            inner = jnp.mean(scaled * normed, axis=1, keepdims=True)
-            branch[rows, :] = (grad_res[rows, :] + inverse * (scaled - normed * inner)).astype(bf16)
-            return carry + jnp.sum(grad * normed, axis=0, keepdims=True)
-
-        gains[0, pl.ds(0, 1), :] = lax.fori_loop(0, tokens // 128, input_rows, jnp.zeros((1, width), f32))
+        follow(
+            plain[second_end : third_end + 1],
+            {
+                "mx": mix_grad,
+                "a": attend_back_all,
+                "g1": late_part,
+                "kvw": join_keys,
+                "g0": lambda: weight_grad(7, turned.at[0], grad_y),
+                "in": input_rows,
+            },
+        )
 
     keys = kv_ref.shape[1]
     pl.run_scoped(
@@ -901,23 +1103,18 @@
         exchanges[k].wait()
         gains[6 + at.z if k == 2 else 2 * (k + 1)] = gains[2 * k] + gains[2 * k + 1]
 
-    exchanges[0].start()
-    scatter.fourth(4)
-    scatter.second(6)
-    fold(0)
-    exchanges[1].start()
-    scatter.second(7)
-    scatter.fourth(5)
-    fold(1)
-    exchanges[2].start()
-    scatter.third(6)
-    fold(2)
-    start(everyone)
-    scatter.third(7)
-    scatter.fourth(6)
+    rest = plain[third_end + 1 :]
+    share = -(-len(rest) // 4)
+    for k in range(4):
+        if k < 3:
+            exchanges[k].start()
+        else:
+            start(everyone)
+        follow(rest[k * share : (k + 1) * share], {})
+        if k < 3:
+            fold(k)
     wait(everyone)
     gain_sum_ref[...] = gains[6] + gains[7] + gains[8] + gains[9]
-    scatter.fourth(7)
     out.wait()
     scatter.finish()
 
@@ -943,24 +1140,26 @@
             shape((count, 4, rows, size), bf16),
             shape((count, 3, rows, size), bf16),
         ],
-        in_specs=[anywhere] * 2 + [near] * 6 + [anywhere] * (PACKS + len(kept)),
+        in_specs=[anywhere] * 2 + [near] * 5 + [anywhere] * (PACKS + len(kept)),
         out_specs=[anywhere, anywhere, near] + [anywhere] * 5,
         scratch_shapes=[
             vmem((RING, 2, 4, rows, size), bf16),
             vmem((RING, 4, rows, size), bf16),
             vmem((RING, 3, rows, size), bf16),
             vmem((RING, rows, size), f32),
+            vmem((2, 4, rows, size), bf16),
+            vmem((2, 4, rows, size), bf16),
             vmem((4, 4, rows, size), bf16),
-            vmem((3, rows, size), bf16),
+            vmem((4, rows, size), bf16),
             vmem((2, 2, width, size), bf16),
             vmem((tokens, width), f32),
             vmem((tokens, width), bf16),
             vmem((2, tokens, 3 * LANES), bf16),
             vmem((2, tokens, 3 * LANES), bf16),
             vmem((10, 8, width), f32),
-            dma((count, 10)),
-            dma((count, 10)),
-            dma((14,)),
+            dma((count, 13)),
+            dma((count, 13)),
+            dma((15,)),
             dma((count,)),
             dma((10,)),
             dma((2, 2)),
@@ -976,8 +1175,7 @@
     )(
         grad_output,
         layer_input,
-        gains[0],
-        gains[1],
+        gains,
         cosine,
         sine,
         first,
@@ -1024,11 +1222,11 @@
     return values * cosine - jnp.where(lower, -ahead, behind)
 
 
-def project_half(half, attn_in_ref, weight_ref, cos_ref, sin_ref, y_ref):
+def project_tiles(half, pairs, attn_in_ref, weight_ref, cos_ref, sin_ref, y_ref):
     cosine, sine = cos_ref[...], sin_ref[...]
     lane = lane_of(cosine.shape)
     lower = lane % HEAD < HEAD // 2
-    for pair in range(4):
+    for pair in pairs:
         two = dot_nn(attn_in_ref[...], weight_ref[half, :, pl.ds(pair * 2 * LANES, 2 * LANES)]).astype(bf16)
         for side in range(2):
             tile = 2 * pair + side
@@ -1049,7 +1247,7 @@
     inverse = lax.rsqrt(jnp.mean(values * values, axis=1, keepdims=True) + eps)
     attn_in_ref[...] = (values * inverse * gain_ref[...]).astype(bf16)
     for half in range(2):
-        project_half(half, attn_in_ref, weight_ref, cos_ref, sin_ref, y_ref)
+        project_tiles(half, range(4), attn_in_ref, weight_ref, cos_ref, sin_ref, y_ref)
 
 
 def head_rows(values, side, lane):
@@ -1250,11 +1448,9 @@
     )(y, kv, first, last, logs, grad, cosine, sine)
 
 
-def rope_tables(position):
+def rope_frequency():
     lane_index = (jnp.arange(LANES, dtype=jnp.int32) % (HEAD // 2)).astype(f32)
-    frequency = jnp.exp(lane_index * (-2.0 * math.log(rope_base) / HEAD))
-    angles = position[:, None] * frequency[None, :]
-    return jnp.cos(angles), jnp.sin(angles)
+    return jnp.exp(lane_index * (-2.0 * math.log(rope_base) / HEAD))
 
 
 def shards(
@@ -1275,35 +1471,31 @@
     tokens, width = layer_input.shape
     span = seq_ids.shape[0]
     start = lax.axis_index("col") * tokens
-    index = jnp.arange(span, dtype=jnp.int32)
-    in_first = seq_ids == seq_ids[0]
-    seq_first = jnp.where(in_first, 0, jnp.sum(in_first.astype(jnp.int32)))
-    block_last = block_ends - lax.axis_index("row") * span
-    own_first = lax.dynamic_slice_in_dim(seq_first, start, tokens)
-    own_last = lax.dynamic_slice_in_dim(block_last, start, tokens)
-    position = lax.dynamic_slice_in_dim(index - seq_first, start, tokens).astype(f32)
-    cosine, sine = rope_tables(position)
-    own_first, own_last = own_first[None, :], own_last[None, :]
-    gain_one = attn_gain.astype(f32)[None, :]
-    gain_two = mlp_gain.astype(f32)[None, :]
-
+    gains = jnp.stack([attn_gain, mlp_gain]).astype(f32)
     weights = (query_weight, key_weight, value_weight, out_weight, gate_weight, up_weight, down_weight)
-    own = layer_input.astype(f32)
     if special():
         mine = jnp.concatenate([key_weight, value_weight, query_weight, out_weight.T], axis=1)
         packs, kept = forward_special(
             layer_input,
-            (gain_one, gain_two),
-            cosine,
-            sine,
-            own_first,
-            own_last,
+            gains,
+            rope_frequency()[None, :],
+            seq_ids[None, :],
+            block_ends[None, :],
             (mine, gate_weight, up_weight, down_weight.T),
         )
         grad_input, gain_sums, weight_sums = backward_special(
-            grad_output, layer_input, (gain_one, gain_two), cosine, sine, own_first, own_last, packs, kept[:9]
+            grad_output, layer_input, gains, *kept[10:], packs, kept[:9]
         )
         return (kept[9], grad_input, gain_sums[0], gain_sums[1]) + tuple(weight_sums)
+    own = layer_input.astype(f32)
+    gain_one, gain_two = gains[:1], gains[1:]
+    index = start + jnp.arange(tokens, dtype=jnp.int32)
+    length = jnp.sum(1 - (seq_ids & 1))
+    own_first = jnp.where(index < length, 0, length)
+    own_last = lax.dynamic_slice_in_dim(block_ends, start, tokens) - lax.axis_index("row") * span
+    angles = (index - own_first).astype(f32)[:, None] * rope_frequency()[None, :]
+    cosine, sine = jnp.cos(angles), jnp.sin(angles)
+    own_first, own_last = own_first[None, :], own_last[None, :]
     pack_first, pack_gate, pack_up, pack_down = gather_any(weights)
     attn_in, y = project(layer_input, gain_one, pack_first, cosine, sine)
     kv = lax.all_gather(y[:, :, : 3 * LANES], "col", axis=1, tiled=True)

time: 386 us -> 355 us (0.920)
  the two profiles are of different devices: /device:TPU:1 before, /device:TPU:0 now
where the time goes in v3:
time: 355 us; the launch traced here: 349 us
  Pallas kernels  337 us (95%)
  local copies, waits for them, and re-layouts  10.8 us (3%)
    pallas_call x1, Pallas kernels, backward_special(): pl.pallas_call(backward_kernel, out_shape=[shape((PACKS, rows, lanes), f3...  181 us
    pallas_call x1, Pallas kernels, forward_special(): pl.pallas_call(lambda *refs: forward_kernel(plan, *refs), out_shape=[jax....  156 us

profile of v3, /device:TPU:0, one launch (start us, length us, event | category | flops | bytes accessed | tf_op | source)
XLA Modules:
  0.0 349.3 jit_solution(11640470914176637347)
XLA Ops:
  0.6 0.5 fusion.2.refs_2_
  1.2 0.7 stack.9
  1.9 0.7 stack.10
  2.5 0.6 maximum_convert_fusion.refs_1_.refs_2_
  3.2 1.8 concatenate.3.refs_5_
  5.0 155.8 %forward.1 = (bf16[2,4,2,144,1536]{4,3,2,1,0:T(8,128)(2,1)}, bf16[2,4,2,144,1536]{4,3,2,1,0:T(8,128)(2,1)}, bf16[2,4,2,144,1536]{4,3,2,1,0:T(8,128)(2,1)}, bf16[...) custom-call(bf16[512,1152]{1,0:T(8,128)(2,1)} %refs_1_.1, ...), custom_call_target="tpu_custom_call" | custom-call | tf_op jit(solution)/shard_map/forward/pallas_call | solution.py:506
  160.8 180.7 %backward.1 = (f32[4,72,1536]{2,1,0:T(8,128)}, bf16[512,1152]{1,0:T(8,128)(2,1)}, f32[8,1152]{1,0:T(8,128)}, bf16[8,2,4,2,144,768]{5,4,3,2,1,0:T(8,128)(2,1)}, b...) custom-call(bf16[512,1152]{1,0:T(8,128)(2,1)} %refs_0_.3, ...), custom_call_target="tpu_custom_call" | custom-call | tf_op jit(solution)/shard_map/backward/pallas_call | solution.py:1131
  341.5 1.5 slice_reduce_fusion
  343.0 0.0 copy-start
  343.0 2.6 slice_bitcast_fusion
  345.6 0.0 copy-start.1
  345.6 0.7 fusion.3
  346.3 0.8 slice_bitcast_fusion.4
  347.1 0.0 copy-done
  347.1 1.0 copy.26
  348.1 0.0 copy-done.1
  348.1 1.0 copy.27
Async XLA Ops:
  343.0 4.1 %copy-start = (bf16[512,1152]{1,0:T(8,128)(2,1)S(1)}, bf16[512,1152]{1,0:T(8,128)(2,1)}, u32[]{:S(2)}) copy-start(bf16[512,1152]{1,0:T(8,128)(2,1)} %get-tuple-element.74) | copy-start | bytes 3538948
  345.6 2.5 copy-start.1

commit v4 on v3

--- a/solution.py
+++ b/solution.py
@@ -119,6 +119,7 @@
         self.far = self.device(self.xb, z, self.yb, c)
         self.twin = self.device(x, z, y, 1 - c)
         self.cross = self.device(1 - x, z, y, c)
+        self.corner = self.device(1 - x, z, 1 - y, c)
 
     @staticmethod
     def device(x, z, y, c):
@@ -126,9 +127,10 @@
 
     def greet(self):
         barrier = pltpu.get_barrier_semaphore()
-        for peer in self.line + [self.near, self.far, self.twin]:
+        peers = self.line + [self.near, self.far, self.corner, self.twin]
+        for peer in peers:
             pl.semaphore_signal(barrier, inc=1, device_id=peer, device_id_type=MESH)
-        pl.semaphore_wait(barrier, 6)
+        pl.semaphore_wait(barrier, len(peers))
 
 
 def remote(src, dst, send, recv, device):
@@ -138,40 +140,40 @@
 
 
 GATHER_PLAN = [
-    (0, 0, 512, 0, "y", "y"),
+    (0, 0, 512, 0, "x", "y"),
     (0, 512, 512, 0, "y", "x"),
     (0, 1024, 512, 0, "x", "x"),
-    (1, 0, 768, 0, "y", "x"),
+    (1, 0, 768, 0, "y", "y"),
     (2, 0, 768, 1, "x", "x"),
-    (1, 768, 768, 1, "y", "x"),
-    (2, 768, 768, 0, "x", "x"),
-    (3, 0, 768, 0, "x", "y"),
-    (3, 768, 768, 1, "y", "y"),
+    (1, 768, 768, 0, "y", "x"),
+    (2, 768, 768, 0, "x", "y"),
+    (3, 0, 768, 1, "x", "y"),
+    (3, 768, 768, 1, "x", "y"),
 ]
 FORWARD_ORDER = [
-    ("B", 0), ("B", 1), ("B", 2), ("F", 0), ("B", 6), ("F", 1), ("S", 1), ("F", 2), ("S", 0), "norm",
-    ("F", 6), ("B", 4), ("B", 3), ("T", 0), ("B", 7), ("S", 2), ("T", 1), "kv", ("S", 6), "q", ("B", 5),
-    ("F", 4), ("F", 3), "a0", ("B", 8), ("F", 7), "a1", "a2", ("T", 2), ("S", 3), ("S", 4), ("F", 5),
-    ("F", 8), "a3", ("T", 6), "br", ("T", 3), ("S", 5), ("T", 4), ("S", 8), "h0", ("T", 5), ("S", 7), "h1",
-    ("T", 7), ("T", 8), "o0", "o1",
+    ("B", 0), ("B", 1), "norm", ("F", 0), ("B", 2), ("F", 1), ("B", 3), ("S", 0), ("F", 2), ("B", 4),
+    ("S", 1), ("T", 0), ("F", 3), ("B", 5), ("S", 2), ("T", 1), "kv", ("F", 4), ("B", 6), "q", ("T", 2),
+    ("S", 3), ("F", 5), ("B", 7), "a0", ("S", 4), "a1", ("F", 6), ("B", 8), "a2", ("F", 7), ("S", 5),
+    ("T", 3), ("T", 4), "a3", "br", ("S", 7), ("S", 6), ("F", 8), "h0", ("T", 5), ("S", 8), ("T", 6),
+    ("T", 7), "h1", ("T", 8), "o0", "o1",
 ]
 SCATTER_PLAN = [
     (3, 0, 1, "y", "x"),
-    (1, 0, 1, "y", "x"),
-    (2, 0, 1, "x", "x"),
-    (3, 1, 0, "y", "x"),
-    (1, 1, 0, "x", "y"),
+    (1, 0, 0, "x", "y"),
+    (2, 0, 0, "y", "x"),
+    (3, 1, 1, "y", "x"),
+    (1, 1, 0, "x", "x"),
     (2, 1, 0, "y", "y"),
     (0, 1, 0, "y", "x"),
     (0, 0, 0, "x", "y"),
 ]
 BACKWARD_ORDER = [
-    "ld", "w0", "d0", ("B", 0), "w1", "w2", ("1", 0), "m0", ("B", 1), "w3", "d1", ("1", 1), ("B", 3),
-    ("2", 0), "w4", "w5", ("B", 5), ("1", 3), "m1", ("2", 1), ("B", 2), ("3", 0), ("B", 4), ("1", 5), "norm",
-    "mx", ("2", 3), ("1", 2), "a0", "a1", ("2", 2), "a2", ("2", 5), ("4", 0), ("1", 4), ("3", 1), ("3", 3),
-    "a3", "g1", ("B", 6), ("3", 5), ("1", 6), "kvw", ("3", 2), "g0", ("2", 4), ("B", 7), ("4", 1), "in",
-    ("2", 6), ("1", 7), ("4", 3), ("3", 4), ("2", 7), ("3", 6), ("3", 7), ("4", 4), ("4", 6), ("4", 5),
-    ("4", 2), ("4", 7),
+    "ld", "w0", ("B", 0), "d0", "w1", ("B", 1), ("1", 0), "w2", "m0", ("1", 1), ("B", 2), "w3", ("B", 3),
+    ("1", 2), "d1", "w4", "w5", ("B", 5), "m1", ("2", 1), ("1", 3), ("B", 4), "norm", ("1", 5), ("2", 0),
+    "mx", "a0", ("1", 4), ("2", 3), ("3", 0), "a1", "a2", ("2", 2), ("3", 1), ("2", 5), "a3", ("3", 3), "g1",
+    ("B", 6), ("4", 1), ("3", 2), ("3", 5), ("2", 4), ("1", 6), "kvw", "g0", "in", ("4", 0), ("B", 7),
+    ("3", 4), ("2", 6), ("4", 3), ("1", 7), ("4", 2), ("3", 6), ("4", 4), ("2", 7), ("4", 5), ("3", 7),
+    ("4", 6), ("4", 7),
 ]
 RING = 6
 
@@ -1090,31 +1092,29 @@
     )
     out = pull(branch, grad_in_ref, 0)
     out.start()
-    exchanges = [
-        remote(gains.at[2 * k], gains.at[2 * k + 1], gain_sent.at[k], gain_came.at[k], peer)
-        for k, peer in enumerate([at.twin, at.near, at.far])
+    swap = remote(gains.at[0], gains.at[1], gain_sent.at[0], gain_came.at[0], at.twin)
+    spot = 2 + 2 * at.x + at.y
+    plane = [
+        remote(gains.at[spot], gains.at[spot], gain_sent.at[1 + k], gain_came.at[1 + k], peer)
+        for k, peer in enumerate([at.near, at.far, at.corner])
     ]
     everyone = [
-        remote(gains.at[6 + at.z], gains.at[6 + at.z], gain_sent.at[3 + k], gain_came.at[3 + k], at.line[k])
+        remote(gains.at[6 + at.z], gains.at[6 + at.z], gain_sent.at[4 + k], gain_came.at[4 + k], at.line[k])
         for k in range(3)
     ]
-
-    def fold(k):
-        exchanges[k].wait()
-        gains[6 + at.z if k == 2 else 2 * (k + 1)] = gains[2 * k] + gains[2 * k + 1]
-
     rest = plain[third_end + 1 :]
-    share = -(-len(rest) // 4)
-    for k in range(4):
-        if k < 3:
-            exchanges[k].start()
-        else:
-            start(everyone)
-        follow(rest[k * share : (k + 1) * share], {})
-        if k < 3:
-            fold(k)
+    swap.start()
+    follow(rest[:2], {})
+    swap.wait()
+    gains[spot] = gains[0] + gains[1]
+    start(plane)
+    follow(rest[2:7], {})
+    wait(plane)
+    gains[6 + at.z] = (gains[2] + gains[3]) + (gains[4] + gains[5])
+    start(everyone)
+    follow(rest[7:], {})
     wait(everyone)
-    gain_sum_ref[...] = gains[6] + gains[7] + gains[8] + gains[9]
+    gain_sum_ref[...] = (gains[6] + gains[7]) + (gains[8] + gains[9])
     out.wait()
     scatter.finish()
 
@@ -1165,8 +1165,8 @@
             dma((2, 2)),
             dma((2,)),
             dma((2,)),
-            dma((6,)),
-            dma((6,)),
+            dma((7,)),
+            dma((7,)),
         ],
         compiler_params=pltpu.CompilerParams(
             collective_id=2, has_side_effects=True, vmem_limit_bytes=VMEM_BYTES

time: 355 us -> 339 us (0.955)
  Pallas kernels: 337 us -> 322 us
    pallas_call x1, Pallas kernels: 156 us -> 146 us  [forward_special(): pl.pallas_call(lambda *refs: forward_kernel(plan, *refs), out_shape=[jax....]
    pallas_call x1, Pallas kernels: 181 us -> 176 us  [backward_special(): pl.pallas_call(backward_kernel, out_shape=[shape((PACKS, rows, lanes), f3...]
where the time goes in v4:
time: 339 us; the launch traced here: 334 us
  Pallas kernels  322 us (95%)
  local copies, waits for them, and re-layouts  10.8 us (3%)
    pallas_call x1, Pallas kernels, backward_special(): pl.pallas_call(backward_kernel, out_shape=[shape((PACKS, rows, lanes), f3...  176 us
    pallas_call x1, Pallas kernels, forward_special(): pl.pallas_call(lambda *refs: forward_kernel(plan, *refs), out_shape=[jax....  146 us

profile of v4, /device:TPU:0, one launch (start us, length us, event | category | flops | bytes accessed | tf_op | source)
XLA Modules:
  0.0 334.3 jit_solution(604818498978359447)
XLA Ops:
  0.6 0.5 fusion.2.refs_2_
  1.2 0.7 stack.9
  1.9 0.7 stack.10
  2.5 0.6 maximum_convert_fusion.refs_1_.refs_2_
  3.2 1.8 concatenate.3.refs_5_
  5.0 145.6 %forward.1 = (bf16[2,4,2,144,1536]{4,3,2,1,0:T(8,128)(2,1)}, bf16[2,4,2,144,1536]{4,3,2,1,0:T(8,128)(2,1)}, bf16[2,4,2,144,1536]{4,3,2,1,0:T(8,128)(2,1)}, bf16[...) custom-call(bf16[512,1152]{1,0:T(8,128)(2,1)} %refs_1_.1, ...), custom_call_target="tpu_custom_call" | custom-call | tf_op jit(solution)/shard_map/forward/pallas_call | solution.py:508
  150.6 175.9 %backward.1 = (f32[4,72,1536]{2,1,0:T(8,128)}, bf16[512,1152]{1,0:T(8,128)(2,1)}, f32[8,1152]{1,0:T(8,128)}, bf16[8,2,4,2,144,768]{5,4,3,2,1,0:T(8,128)(2,1)}, b...) custom-call(bf16[512,1152]{1,0:T(8,128)(2,1)} %refs_0_.3, ...), custom_call_target="tpu_custom_call" | custom-call | tf_op jit(solution)/shard_map/backward/pallas_call | solution.py:1131
  326.5 1.5 slice_reduce_fusion
  328.0 0.0 copy-start
  328.0 2.6 slice_bitcast_fusion
  330.6 0.0 copy-start.1
  330.6 0.7 fusion.3
  331.3 0.8 slice_bitcast_fusion.4
  332.1 0.0 copy-done
  332.1 1.0 copy.26
  333.1 0.0 copy-done.1
  333.1 1.0 copy.27
Async XLA Ops:
  328.0 4.1 %copy-start = (bf16[512,1152]{1,0:T(8,128)(2,1)S(1)}, bf16[512,1152]{1,0:T(8,128)(2,1)}, u32[]{:S(2)}) copy-start(bf16[512,1152]{1,0:T(8,128)(2,1)} %get-tuple-element.74) | copy-start | bytes 3538948
  330.6 2.5 copy-start.1

commit v5 on v4

--- a/solution.py
+++ b/solution.py
@@ -1108,11 +1108,11 @@
     swap.wait()
     gains[spot] = gains[0] + gains[1]
     start(plane)
-    follow(rest[2:7], {})
+    follow(rest[2:10], {})
     wait(plane)
     gains[6 + at.z] = (gains[2] + gains[3]) + (gains[4] + gains[5])
     start(everyone)
-    follow(rest[7:], {})
+    follow(rest[10:], {})
     wait(everyone)
     gain_sum_ref[...] = (gains[6] + gains[7]) + (gains[8] + gains[9])
     out.wait()

time: 339 us -> 339 us (level)
  no operation moved by 1% of the time
where the time goes in v5:
time: 339 us; the launch traced here: 334 us
  Pallas kernels  322 us (95%)
  local copies, waits for them, and re-layouts  10.8 us (3%)
    pallas_call x1, Pallas kernels, backward_special(): pl.pallas_call(backward_kernel, out_shape=[shape((PACKS, rows, lanes), f3...  176 us
    pallas_call x1, Pallas kernels, forward_special(): pl.pallas_call(lambda *refs: forward_kernel(plan, *refs), out_shape=[jax....  146 us

profile of v5, /device:TPU:0, one launch (start us, length us, event | category | flops | bytes accessed | tf_op | source)
XLA Modules:
  0.0 334.4 jit_solution(8077370599434295196)
XLA Ops:
  0.6 0.5 fusion.2.refs_2_
  1.2 0.7 stack.9
  1.9 0.7 stack.10
  2.5 0.6 maximum_convert_fusion.refs_1_.refs_2_
  3.2 1.8 concatenate.3.refs_5_
  5.0 145.6 %forward.1 = (bf16[2,4,2,144,1536]{4,3,2,1,0:T(8,128)(2,1)}, bf16[2,4,2,144,1536]{4,3,2,1,0:T(8,128)(2,1)}, bf16[2,4,2,144,1536]{4,3,2,1,0:T(8,128)(2,1)}, bf16[...) custom-call(bf16[512,1152]{1,0:T(8,128)(2,1)} %refs_1_.1, ...), custom_call_target="tpu_custom_call" | custom-call | tf_op jit(solution)/shard_map/forward/pallas_call | solution.py:508
  150.6 176.0 %backward.1 = (f32[4,72,1536]{2,1,0:T(8,128)}, bf16[512,1152]{1,0:T(8,128)(2,1)}, f32[8,1152]{1,0:T(8,128)}, bf16[8,2,4,2,144,768]{5,4,3,2,1,0:T(8,128)(2,1)}, b...) custom-call(bf16[512,1152]{1,0:T(8,128)(2,1)} %refs_0_.3, ...), custom_call_target="tpu_custom_call" | custom-call | tf_op jit(solution)/shard_map/backward/pallas_call | solution.py:1131
  326.6 1.5 slice_reduce_fusion
  328.1 0.0 copy-start
  328.1 2.6 slice_bitcast_fusion
  330.7 0.0 copy-start.1
  330.7 0.7 fusion.3
  331.4 0.8 slice_bitcast_fusion.4
  332.2 0.0 copy-done
  332.2 1.0 copy.26
  333.2 0.0 copy-done.1
  333.2 1.0 copy.27
Async XLA Ops:
  328.1 4.1 %copy-start = (bf16[512,1152]{1,0:T(8,128)(2,1)S(1)}, bf16[512,1152]{1,0:T(8,128)(2,1)}, u32[]{:S(2)}) copy-start(bf16[512,1152]{1,0:T(8,128)(2,1)} %get-tuple-element.74) | copy-start | bytes 3538948
  330.7 2.5 copy-start.1
